TPU v7x, 32 devices: a whole 2x2x4 slice. The times are simulated.
32 devices in a mesh: blk: 16 (over z, y, x), lay: 2 (over core).
Axes of the slice: x: 2, y: 2, z: 4, core: 2. Of those that a mesh axis runs over, the one named last changes fastest.
Arguments:
- matrix_source: float32 [32, 256, 256], P('lay', 'blk'), may hold values from -6 to 6
- accum: float32 [32, 256, 256], P('lay', 'blk'), may hold values from 0.02 to 0.5
- faces: float32 [6, 32, 256, 256], P(None, 'lay', 'blk'), may hold values from 0.03 to 30, as said below
- basis: float32 [4, 32, 256, 256], P(None, 'lay', 'blk'), may hold values from 0.05 to 0.5
- coarse_diag: float32 [8, 64], P('lay', 'blk'), may hold values from 32 to 128
- coarse_ratio: float32 [4, 8, 64], P(None, 'lay', 'blk'), may hold values from 0.1 to 0.24
- frac_source: float32 [16384], P(('blk', 'lay')), may hold values from -6 to 6
- frac_accum: float32 [16384], P(('blk', 'lay')), may hold values from 0.05 to 0.5
- frac_link: float32 [16384], P(('blk', 'lay')), may hold values from 0.5 to 5
- frac_trans: float32 [2, 16384], P(None, ('blk', 'lay')), may hold values from 0.5 to 5
- frac_cell: int32 [16384], P(('blk', 'lay')), may hold values from 0 to 65535
- frac_peer: int32 [2, 16384], P(None, ('blk', 'lay')), may hold values from 0 to 16383, as said below
- frac_count: int32 [32], P(('blk', 'lay')), may hold values from 1 to 512, as said below
Outputs:
- pressure: float32 [32, 256, 256], P('lay', 'blk')
- fracture: float32 [16384], P(('blk', 'lay'))
Inputs may be any that keep to these rules, and one draw needn't show every extreme that they name: `faces`: the x+ face of a cell equals the x- face of the next cell along the first dimension, likewise y and z. `frac_count`: some owner has exactly 512 live slots in every draw. `frac_peer`: each entry is a live slot (slot index below its owner's count) of the same owner or of the owner just before or after it in the order blk index * 2 + lay index.
All inputs are finite; a program needn't handle non-finite values.
Results may differ from a plain program's by a relative error of at most 0.0001.
Values sent between devices are 32-bit elements; how exact they have to be, the bound alone decides.
No kernel may reach another device: no remote copies, remote signals or barrier semaphores. Data moves between devices by JAX's collectives and lax.ppermute only.
A program may use at most 64 MiB of HBM per device.

v0:
```python
import jax
import jax.numpy as jnp
from jax import lax
from jax.sharding import PartitionSpec as P

BLOCK = 4
ITERS = 2


OMEGA = 0.8


def padded_2(block, sides, width):
    for axis, dim in sides:
        count = lax.axis_size(axis)
        forward = [(i, i + 1) for i in range(count - 1)]
        backward = [(target, source) for source, target in forward]
        low = lax.ppermute(
            lax.slice_in_dim(block, block.shape[dim] - width, None, axis=dim), axis, forward
        )
        high = lax.ppermute(lax.slice_in_dim(block, 0, width, axis=dim), axis, backward)
        block = jnp.concatenate([low, block, high], axis=dim)
    return block


def place(block_sums, row_start, col_start):
    return jnp.pad(block_sums, ((row_start, 2 - row_start), (col_start, 2 - col_start)))


def spread(node_terms):
    low_mask = (jnp.arange(BLOCK) < BLOCK // 2).astype(jnp.float32)
    high_mask = 1.0 - low_mask
    x_low = low_mask[None, :, None, None]
    x_high = high_mask[None, :, None, None]
    y_low = low_mask[None, None, None, :]
    y_high = high_mask[None, None, None, :]

    def masked_sum(values, weight):
        return jnp.sum(values * weight, axis=(1, 3))

    spread_sum = place(jnp.sum(node_terms[0], axis=(1, 3)), 1, 1)
    spread_sum = (
        spread_sum
        + place(masked_sum(node_terms[1], x_low), 0, 1)
        + place(masked_sum(node_terms[1], x_high), 2, 1)
    )
    spread_sum = (
        spread_sum
        + place(masked_sum(node_terms[2], y_low), 1, 0)
        + place(masked_sum(node_terms[2], y_high), 1, 2)
    )
    spread_sum = (
        spread_sum
        + place(masked_sum(node_terms[3], x_low * y_low), 0, 0)
        + place(masked_sum(node_terms[3], x_low * y_high), 0, 2)
    )
    spread_sum = (
        spread_sum
        + place(masked_sum(node_terms[3], x_high * y_low), 2, 0)
        + place(masked_sum(node_terms[3], x_high * y_high), 2, 2)
    )
    return spread_sum


def node_values(extended):
    node_rows = extended.shape[0] - 2
    node_cols = extended.shape[1] - 2
    low_mask = jnp.arange(BLOCK) < BLOCK // 2
    x_low = low_mask[None, :, None, None]
    y_low = low_mask[None, None, None, :]

    def node_grid(row_start, col_start):
        return extended[row_start : row_start + node_rows, col_start : col_start + node_cols][
            :, None, :, None
        ]

    full_shape = (node_rows, BLOCK, node_cols, BLOCK)
    centre = jnp.broadcast_to(node_grid(1, 1), full_shape)
    side_x = jnp.broadcast_to(jnp.where(x_low, node_grid(0, 1), node_grid(2, 1)), full_shape)
    side_y = jnp.broadcast_to(jnp.where(y_low, node_grid(1, 0), node_grid(1, 2)), full_shape)
    corner = jnp.where(
        x_low,
        jnp.where(y_low, node_grid(0, 0), node_grid(0, 2)),
        jnp.where(y_low, node_grid(2, 0), node_grid(2, 2)),
    )
    stacked = jnp.stack([centre, side_x, side_y, corner])
    return stacked.reshape(4, node_rows * BLOCK, node_cols * BLOCK)


def prolong(basis, extended):
    fields = node_values(extended)
    return jnp.sum(basis * fields[..., None], axis=0)


def restrict_terms(basis, residual):
    node_sums = jnp.sum(basis * residual[None], axis=3)
    node_rows = node_sums.shape[1] // BLOCK
    node_cols = node_sums.shape[2] // BLOCK
    return spread(node_sums.reshape(4, node_rows, BLOCK, node_cols, BLOCK))


def coarse_second(first_sweep, first_padded, coarse_ratio):
    neighbours = [
        first_padded[:-2, 1:-1],
        first_padded[2:, 1:-1],
        first_padded[1:-1, :-2],
        first_padded[1:-1, 2:],
    ]
    second = first_sweep
    for direction in range(4):
        second = second + coarse_ratio[direction] * neighbours[direction]
    return second


def flow_rows(padded, faces, accum):
    centre = padded[1:-1, 1:-1, 1:-1]
    beside = [
        padded[2:, 1:-1, 1:-1],
        padded[:-2, 1:-1, 1:-1],
        padded[1:-1, 2:, 1:-1],
        padded[1:-1, :-2, 1:-1],
        padded[1:-1, 1:-1, 2:],
        padded[1:-1, 1:-1, :-2],
    ]
    result = accum * centre
    for direction in range(6):
        result = result + faces[direction] * (centre - beside[direction])
    return result


def fetch_rim(pressure):
    return padded_2(pressure, (("blk", 1), ("lay", 0)), 1)


def matrix_rows(pressure_wide, pressure, fracture, faces, accum, cell_index, couple):
    padded = jnp.pad(pressure_wide, ((0, 0), (0, 0), (1, 1)))
    result = flow_rows(padded, faces, accum)
    pressure_at = pressure.reshape(-1)[cell_index]
    link_flux = couple * (pressure_at - fracture)
    linked = jax.ops.segment_sum(link_flux, cell_index, num_segments=pressure.size).reshape(
        pressure.shape
    )
    return (result + linked, pressure_at)


def local(
    matrix_source,
    accum,
    faces,
    basis,
    coarse_diag,
    coarse_ratio,
    frac_source,
    frac_accum,
    frac_link,
    frac_trans,
    frac_cell,
    frac_peer,
    frac_count,
):
    slot_count = frac_source.shape[0]
    cell_rows, cell_cols, depth_cells = matrix_source.shape
    margin = BLOCK // 2
    live_mask = (jnp.arange(slot_count) < frac_count[0]).astype(jnp.float32)
    couple = live_mask * frac_link
    matrix_diag = (
        accum
        + jnp.sum(faces, axis=0)
        + jax.ops.segment_sum(couple, frac_cell, num_segments=accum.size).reshape(accum.shape)
    )
    frac_diag = frac_accum + couple + jnp.sum(frac_trans, axis=0)
    position = lax.axis_index(("blk", "lay"))
    local_peer = frac_peer - (position - 1) * slot_count
    basis_wide = padded_2(basis, (("blk", 2), ("lay", 1)), margin)
    basis_wide = jnp.pad(basis_wide, ((0, 0), (margin, margin), (margin, margin), (0, 0)))
    pressure = jnp.zeros(matrix_source.shape, jnp.float32)
    pressure_wide = jnp.zeros((cell_rows + 2, cell_cols + 2, depth_cells), jnp.float32)
    fracture = jnp.zeros(frac_source.shape, jnp.float32)
    for iteration in range(ITERS):
        if iteration == 0:
            residual = matrix_source
        else:
            pressure_wide = fetch_rim(pressure)
            rows_now, pressure_at = matrix_rows(
                pressure_wide, pressure, fracture, faces, accum, frac_cell, couple
            )
            residual = matrix_source - rows_now
        wide_rows = padded_2(residual, (("blk", 1), ("lay", 0)), margin)
        wide_rows = jnp.pad(wide_rows, ((margin, margin), (margin, margin), (0, 0)))
        extended = restrict_terms(basis_wide, wide_rows)
        first_sweep = extended[2:-2, 2:-2] / coarse_diag
        first_wide = padded_2(first_sweep, (("blk", 1), ("lay", 0)), 1)
        second = coarse_second(first_sweep, first_wide, coarse_ratio)
        node_grid_wide = padded_2(second, (("blk", 1), ("lay", 0)), 1)
        pressure = pressure + prolong(basis, node_grid_wide)
        pressure_wide = fetch_rim(pressure)
        rows_now, pressure_at = matrix_rows(
            pressure_wide, pressure, fracture, faces, accum, frac_cell, couple
        )
        fracture_wide = padded_2(fracture, ((("blk", "lay"), 0),), slot_count)
        peer_values = fracture_wide[local_peer]
        frac_now = (
            frac_accum * fracture
            + couple * (fracture - pressure_at)
            + jnp.sum(frac_trans * (fracture[None] - peer_values), axis=0)
        )
        pressure = pressure + OMEGA * (matrix_source - rows_now) / matrix_diag
        fracture = fracture + OMEGA * live_mask * (frac_source - frac_now) / frac_diag
    return (pressure, fracture)


def solution(mesh):
    return jax.shard_map(
        local,
        mesh=mesh,
        in_specs=(
            P("lay", "blk", None),
            P("lay", "blk", None),
            P(None, "lay", "blk", None),
            P(None, "lay", "blk", None),
            P("lay", "blk"),
            P(None, "lay", "blk"),
            P(("blk", "lay")),
            P(("blk", "lay")),
            P(("blk", "lay")),
            P(None, ("blk", "lay")),
            P(("blk", "lay")),
            P(None, ("blk", "lay")),
            P(("blk", "lay")),
        ),
        out_specs=(P("lay", "blk", None), P(("blk", "lay"))),
        check_vma=False,
    )
```

profile of v0, /device:TPU:8, one launch (start us, length us, event | category | flops | bytes accessed | tf_op | source)
XLA Modules:
  0.0 210.1 jit_solution(6532132172409786741)
XLA Ops:
  0.7 2.1 collective-permute-start.24
  3.7 3.4 %collective-permute-start.4 = (f32[16,2,256]{2,1,0:T(2,128)S(1)}, f32[16,2,256]{2,1,0:T(2,128)S(1)}, u32[]{:S(2)}, u32[]{:S(2)}) collective-permute-start(f32[16,2,256]{2,1,0:T(2,128)S(1)} %get-tuple-element.50), channel_id=1, source_target_pairs={{0,2},{2,4},{4,6},{6,8},{8,10},{10,12},{12,14},{14,16},{16,18},{18... | collective-permute-start | bytes 98312 | tf_op jit(solution)/shard_map/ppermute | solution.py:18
  7.1 4.2 %collective-permute-start.5 = (f32[16,2,256]{2,1,0:T(2,128)S(1)}, f32[16,2,256]{2,1,0:T(2,128)S(1)}, u32[]{:S(2)}, u32[]{:S(2)}) collective-permute-start(f32[16,2,256]{2,1,0:T(2,128)S(1)} %get-tuple-element.51), channel_id=1, source_target_pairs={{2,0},{4,2},{6,4},{8,6},{10,8},{12,10},{14,12},{16,14},{18,16},{20... | collective-permute-start | bytes 98312 | tf_op jit(solution)/shard_map/ppermute | solution.py:21
  11.4 1.3 fusion.93
  12.7 1.9 collective-permute-start
  14.6 5.7 %collective-permute-start.1 = (f32[4,16,2,256]{3,2,1,0:T(2,128)S(1)}, f32[4,16,2,256]{3,2,1,0:T(2,128)S(1)}, u32[]{:S(2)}, u32[]{:S(2)}) collective-permute-start(f32[4,16,2,256]{3,2,1,0:T(2,128)S(1)} %get-tuple-element.31), channel_id=1, source_target_pairs={{2,0},{4,2},{6,4},{8,6},{10,8},{12,10},{14,12},{16,14},{18,16},{20... | collective-permute-start | bytes 393224 | tf_op jit(solution)/shard_map/ppermute | solution.py:21
  22.7 2.3 %reduce_sum.245 = f32[16,16,256]{2,1,0:T(8,128)} reduce(f32[6,16,16,256]{3,2,1,0:T(8,128)} %param.15, f32[]{:T(128)} %constant.11.clone.1), dimensions={0}, to_apply=%region_12.13 | reduce | flops 327680 | bytes 1835012 | tf_op jit(solution)/shard_map/reduce_sum | solution.py:168
  24.9 2.3 %collective-permute-start.25 = (f32[512]{0:T(512)S(1)}, f32[512]{0:T(512)S(1)}, u32[]{:S(2)}, u32[]{:S(2)}) collective-permute-start(f32[512]{0:T(512)S(1)} %broadcast.532), channel_id=1, source_target_pairs={{1,0},{2,1},{3,2},{4,3},{5,4},{6,5},{7,6},{8,7},{9,8},{10,9},{11,1... | collective-permute-start | bytes 6152 | tf_op jit(solution)/shard_map/ppermute | solution.py:21
  27.3 2.0 collective-permute-start.6
  29.3 1.3 collective-permute-start.7
  30.7 3.0 %collective-permute-start.2 = (f32[4,2,20,256]{3,2,1,0:T(8,128)S(1)}, f32[4,2,20,256]{3,2,1,0:T(8,128)S(1)}, u32[]{:S(2)}, u32[]{:S(2)}) collective-permute-start(f32[4,2,20,256]{3,2,1,0:T(8,128)S(1)} %get-tuple-element.28), channel_id=1, source_target_pairs={{0,1},{2,3},{4,5},{6,7},{8,9},{10,11},{12,13},{14,15},{16,17},{18,... | collective-permute-start | bytes 491528 | tf_op jit(solution)/shard_map/ppermute | solution.py:18
  33.8 1.3 collective-permute-start.3
  35.1 6.2 %gather_fusion.2 = f32[1024]{0:T(1024)S(1)} fusion(f32[1536]{0:T(1024)S(1)} %pad_maximum_fusion.42, s32[1024]{0:T(1024)S(1)} %broadcast_clamp_fusion), kind=kCustom, calls=%fused_computation.2 | custom fusion | bytes 12288 | tf_op jit(solution)/shard_map/gather | solution.py:201
  43.4 2.9 %collective-permute-start.8 = (f32[4,1]{1,0:T(4,128)S(1)}, f32[4,1]{1,0:T(4,128)S(1)}, u32[]{:S(2)}, u32[]{:S(2)}) collective-permute-start(f32[4,1]{1,0:T(4,128)S(1)} %get-tuple-element.104), channel_id=1, source_target_pairs={{0,2},{2,4},{4,6},{6,8},{8,10},{10,12},{12,14},{14,16},{16,18},{18... | collective-permute-start | bytes 56 | tf_op jit(solution)/shard_map/ppermute | solution.py:18
  46.3 4.8 %collective-permute-start.9 = (f32[4,1]{1,0:T(4,128)S(1)}, f32[4,1]{1,0:T(4,128)S(1)}, u32[]{:S(2)}, u32[]{:S(2)}) collective-permute-start(f32[4,1]{1,0:T(4,128)S(1)} %get-tuple-element.105), channel_id=1, source_target_pairs={{2,0},{4,2},{6,4},{8,6},{10,8},{12,10},{14,12},{16,14},{18,16},{20... | collective-permute-start | bytes 56 | tf_op jit(solution)/shard_map/ppermute | solution.py:21
  51.1 1.3 collective-permute-done.9
  52.4 1.9 collective-permute-start.10
  54.3 1.3 collective-permute-start.11
  55.7 1.7 collective-permute-done.11
  57.6 2.2 %collective-permute-start.12 = (f32[4,1]{1,0:T(4,128)S(1)}, f32[4,1]{1,0:T(4,128)S(1)}, u32[]{:S(2)}, u32[]{:S(2)}) collective-permute-start(f32[4,1]{1,0:T(4,128)S(1)} %get-tuple-element.98), channel_id=1, source_target_pairs={{0,2},{2,4},{4,6},{6,8},{8,10},{10,12},{12,14},{14,16},{16,18},{18... | collective-permute-start | bytes 56 | tf_op jit(solution)/shard_map/ppermute | solution.py:18
  59.9 5.4 %collective-permute-start.13 = (f32[4,1]{1,0:T(4,128)S(1)}, f32[4,1]{1,0:T(4,128)S(1)}, u32[]{:S(2)}, u32[]{:S(2)}) collective-permute-start(f32[4,1]{1,0:T(4,128)S(1)} %get-tuple-element.99), channel_id=1, source_target_pairs={{2,0},{4,2},{6,4},{8,6},{10,8},{12,10},{14,12},{16,14},{18,16},{20... | collective-permute-start | bytes 56 | tf_op jit(solution)/shard_map/ppermute | solution.py:21
  66.8 1.3 collective-permute-start.15
  68.1 3.0 %collective-permute-start.14 = (f32[1,6]{1,0:T(1,128)S(1)}, f32[1,6]{1,0:T(1,128)S(1)}, u32[]{:S(2)}, u32[]{:S(2)}) collective-permute-start(f32[1,6]{1,0:T(1,128)S(1)} %get-tuple-element.97), channel_id=1, source_target_pairs={{0,1},{2,3},{4,5},{6,7},{8,9},{10,11},{12,13},{14,15},{16,17},{18,... | collective-permute-start | bytes 80 | tf_op jit(solution)/shard_map/ppermute | solution.py:18
  73.0 4.3 %collective-permute-start.16 = (f32[16,1,256]{2,1,0:T(1,128)S(1)}, f32[16,1,256]{2,1,0:T(1,128)S(1)}, u32[]{:S(2)}, u32[]{:S(2)}) collective-permute-start(f32[16,1,256]{2,1,0:T(1,128)S(1)} %get-tuple-element.48), channel_id=1, source_target_pairs={{0,2},{2,4},{4,6},{6,8},{8,10},{10,12},{12,14},{14,16},{16,18},{18... | collective-permute-start | bytes 49160 | tf_op jit(solution)/shard_map/ppermute | solution.py:18
  77.3 3.6 %collective-permute-start.17 = (f32[16,1,256]{2,1,0:T(1,128)S(1)}, f32[16,1,256]{2,1,0:T(1,128)S(1)}, u32[]{:S(2)}, u32[]{:S(2)}) collective-permute-start(f32[16,1,256]{2,1,0:T(1,128)S(1)} %get-tuple-element.49), channel_id=1, source_target_pairs={{2,0},{4,2},{6,4},{8,6},{10,8},{12,10},{14,12},{16,14},{18,16},{20... | collective-permute-start | bytes 49160 | tf_op jit(solution)/shard_map/ppermute | solution.py:21
  81.7 3.1 %gather_fusion = f32[512]{0:T(512)S(1)} fusion(f32[65536]{0:T(1024)S(1)} %bitcast.84, s32[1024]{0:T(1024)S(1)} %pad_clamp_fusion), kind=kCustom, calls=%fused_computation | custom fusion | bytes 6144 | tf_op jit(solution)/shard_map/gather | solution.py:138
  85.5 2.6 %collective-permute-start.19 = (f32[1,18,256]{2,1,0:T(8,128)}, f32[1,18,256]{2,1,0:T(8,128)}, u32[]{:S(2)}, u32[]{:S(2)}) collective-permute-start(f32[1,18,256]{2,1,0:T(8,128)} %get-tuple-element.40), channel_id=1, source_target_pairs={{0,1},{2,3},{4,5},{6,7},{8,9},{10,11},{12,13},{14,15},{16,17},{18,... | collective-permute-start | bytes 55304 | tf_op jit(solution)/shard_map/ppermute | solution.py:18
  88.1 1.3 collective-permute-start.18
  90.0 3.5 %scatter_custom_fusion = f32[65536]{0:T(1024)S(1)} fusion(s32[512]{0:T(512)} %param.23, f32[512]{0:T(512)} %get-tuple-element.26, f32[]{:T(128)} %constant.11.clone.1), kind=kCustom, calls=%fused_computation.154 | custom fusion | flops 512 | bytes 262656 | tf_op jit(solution)/shard_map/scatter-add | solution.py:140
  94.3 3.5 %scatter_custom_fusion.1 = f32[65536]{0:T(1024)S(1)} fusion(s32[512]{0:T(512)} %param.23, f32[512]{0:T(512)} %get-tuple-element.27, f32[]{:T(128)} %constant.11.clone.1), kind=kCustom, calls=%fused_computation.152 | custom fusion | flops 512 | bytes 262656 | tf_op jit(solution)/shard_map/scatter-add | solution.py:169
  99.7 1.7 fusion.52
  102.1 2.2 %collective-permute-start.20 = (f32[16,1,256]{2,1,0:T(1,128)}, f32[16,1,256]{2,1,0:T(1,128)S(1)}, u32[]{:S(2)}, u32[]{:S(2)}) collective-permute-start(f32[16,1,256]{2,1,0:T(1,128)} %get-tuple-element.46), channel_id=1, source_target_pairs={{0,2},{2,4},{4,6},{6,8},{8,10},{10,12},{12,14},{14,16},{16,18},{18... | collective-permute-start | bytes 49160 | tf_op jit(solution)/shard_map/ppermute | solution.py:18
  104.3 5.4 %collective-permute-start.21 = (f32[16,1,256]{2,1,0:T(1,128)}, f32[16,1,256]{2,1,0:T(1,128)}, u32[]{:S(2)}, u32[]{:S(2)}) collective-permute-start(f32[16,1,256]{2,1,0:T(1,128)} %get-tuple-element.47), channel_id=1, source_target_pairs={{2,0},{4,2},{6,4},{8,6},{10,8},{12,10},{14,12},{16,14},{18,16},{20... | collective-permute-start | bytes 49160 | tf_op jit(solution)/shard_map/ppermute | solution.py:21
  110.5 4.4 %gather_fusion.1 = f32[512]{0:T(512)} fusion(f32[65536]{0:T(1024)S(1)} %bitcast.85, s32[1024]{0:T(1024)} %copy-done.17), kind=kCustom, calls=%fused_computation.1 | custom fusion | bytes 6144 | tf_op jit(solution)/shard_map/gather | solution.py:138
  114.9 1.3 pad_maximum_fusion.36
  116.2 3.7 %collective-permute-start.23 = (f32[1,18,256]{2,1,0:T(8,128)}, f32[1,18,256]{2,1,0:T(8,128)}, u32[]{:S(2)}, u32[]{:S(2)}) collective-permute-start(f32[1,18,256]{2,1,0:T(8,128)} %get-tuple-element.38), channel_id=1, source_target_pairs={{0,1},{2,3},{4,5},{6,7},{8,9},{10,11},{12,13},{14,15},{16,17},{18,... | collective-permute-start | bytes 55304 | tf_op jit(solution)/shard_map/ppermute | solution.py:18
  119.9 1.3 collective-permute-start.22
  121.1 1.3 subtract_multiply_fusion.1
  122.5 3.5 %scatter_custom_fusion.2 = f32[65536]{0:T(1024)S(1)} fusion(s32[512]{0:T(512)} %param.23, f32[512]{0:T(512)} %get-tuple-element.24, f32[]{:T(128)} %constant.11.clone.1), kind=kCustom, calls=%fused_computation.150 | custom fusion | flops 512 | bytes 262656 | tf_op jit(solution)/shard_map/scatter-add | solution.py:140
  127.9 1.5 fusion.31
  129.4 1.9 collective-permute-start.26
  131.3 5.7 %collective-permute-start.27 = (f32[16,2,256]{2,1,0:T(2,128)S(1)}, f32[16,2,256]{2,1,0:T(2,128)S(1)}, u32[]{:S(2)}, u32[]{:S(2)}) collective-permute-start(f32[16,2,256]{2,1,0:T(2,128)S(1)} %get-tuple-element.45), channel_id=1, source_target_pairs={{2,0},{4,2},{6,4},{8,6},{10,8},{12,10},{14,12},{16,14},{18,16},{20... | collective-permute-start | bytes 98312 | tf_op jit(solution)/shard_map/ppermute | solution.py:21
  137.1 3.1 %collective-permute-start.42 = (f32[512]{0:T(512)S(1)}, f32[512]{0:T(512)S(1)}, u32[]{:S(2)}, u32[]{:S(2)}) collective-permute-start(f32[512]{0:T(512)S(1)} %copy-done.13), channel_id=1, source_target_pairs={{0,1},{1,2},{2,3},{3,4},{4,5},{5,6},{6,7},{7,8},{8,9},{9,10},{10,1... | collective-permute-start | bytes 6152 | tf_op jit(solution)/shard_map/ppermute | solution.py:18
  140.2 4.3 %collective-permute-start.43 = (f32[512]{0:T(512)S(1)}, f32[512]{0:T(512)S(1)}, u32[]{:S(2)}, u32[]{:S(2)}) collective-permute-start(f32[512]{0:T(512)S(1)} %copy-done.13), channel_id=1, source_target_pairs={{1,0},{2,1},{3,2},{4,3},{5,4},{6,5},{7,6},{8,7},{9,8},{10,9},{11,1... | collective-permute-start | bytes 6152 | tf_op jit(solution)/shard_map/ppermute | solution.py:21
  145.1 1.9 collective-permute-start.28
  147.0 1.5 collective-permute-start.29
  148.6 6.3 %gather_fusion.4 = f32[1024]{0:T(1024)S(1)} fusion(f32[1536]{0:T(1024)S(1)} %pad_maximum_fusion.43, s32[1024]{0:T(1024)} %copy-done.12), kind=kCustom, calls=%fused_computation.4 | custom fusion | bytes 12288 | tf_op jit(solution)/shard_map/gather | solution.py:201
  156.0 1.9 multiply_reduce_fusion
  158.9 1.9 collective-permute-start.30
  160.9 5.7 %collective-permute-start.31 = (f32[4,1]{1,0:T(4,128)S(1)}, f32[4,1]{1,0:T(4,128)S(1)}, u32[]{:S(2)}, u32[]{:S(2)}) collective-permute-start(f32[4,1]{1,0:T(4,128)S(1)} %get-tuple-element.93), channel_id=1, source_target_pairs={{2,0},{4,2},{6,4},{8,6},{10,8},{12,10},{14,12},{16,14},{18,16},{20... | collective-permute-start | bytes 56 | tf_op jit(solution)/shard_map/ppermute | solution.py:21
  166.6 1.3 collective-permute-done.31
  168.0 2.3 %collective-permute-start.32 = (f32[1,6]{1,0:T(1,128)S(1)}, f32[1,6]{1,0:T(1,128)S(1)}, u32[]{:S(2)}, u32[]{:S(2)}) collective-permute-start(f32[1,6]{1,0:T(1,128)S(1)} %get-tuple-element.88), channel_id=1, source_target_pairs={{0,1},{2,3},{4,5},{6,7},{8,9},{10,11},{12,13},{14,15},{16,17},{18,... | collective-permute-start | bytes 80 | tf_op jit(solution)/shard_map/ppermute | solution.py:18
  170.3 1.3 collective-permute-start.33
  171.6 1.7 collective-permute-done.33
  173.6 1.9 collective-permute-start.34
  175.5 5.7 %collective-permute-start.35 = (f32[4,1]{1,0:T(4,128)S(1)}, f32[4,1]{1,0:T(4,128)S(1)}, u32[]{:S(2)}, u32[]{:S(2)}) collective-permute-start(f32[4,1]{1,0:T(4,128)S(1)} %get-tuple-element.87), channel_id=1, source_target_pairs={{2,0},{4,2},{6,4},{8,6},{10,8},{12,10},{14,12},{16,14},{18,16},{20... | collective-permute-start | bytes 56 | tf_op jit(solution)/shard_map/ppermute | solution.py:21
  182.7 1.3 collective-permute-start.37
  184.0 3.0 %collective-permute-start.36 = (f32[1,6]{1,0:T(1,128)S(1)}, f32[1,6]{1,0:T(1,128)S(1)}, u32[]{:S(2)}, u32[]{:S(2)}) collective-permute-start(f32[1,6]{1,0:T(1,128)S(1)} %get-tuple-element.85), channel_id=1, source_target_pairs={{0,1},{2,3},{4,5},{6,7},{8,9},{10,11},{12,13},{14,15},{16,17},{18,... | collective-permute-start | bytes 80 | tf_op jit(solution)/shard_map/ppermute | solution.py:18
  189.0 4.3 %collective-permute-start.38 = (f32[16,1,256]{2,1,0:T(1,128)S(1)}, f32[16,1,256]{2,1,0:T(1,128)S(1)}, u32[]{:S(2)}, u32[]{:S(2)}) collective-permute-start(f32[16,1,256]{2,1,0:T(1,128)S(1)} %get-tuple-element.42), channel_id=1, source_target_pairs={{0,2},{2,4},{4,6},{6,8},{8,10},{10,12},{12,14},{14,16},{16,18},{18... | collective-permute-start | bytes 49160 | tf_op jit(solution)/shard_map/ppermute | solution.py:18
  193.3 3.6 %collective-permute-start.39 = (f32[16,1,256]{2,1,0:T(1,128)S(1)}, f32[16,1,256]{2,1,0:T(1,128)S(1)}, u32[]{:S(2)}, u32[]{:S(2)}) collective-permute-start(f32[16,1,256]{2,1,0:T(1,128)S(1)} %get-tuple-element.43), channel_id=1, source_target_pairs={{2,0},{4,2},{6,4},{8,6},{10,8},{12,10},{14,12},{16,14},{18,16},{20... | collective-permute-start | bytes 49160 | tf_op jit(solution)/shard_map/ppermute | solution.py:21
  197.2 3.1 %gather_fusion.3 = f32[512]{0:T(512)S(1)} fusion(f32[65536]{0:T(1024)S(1)} %bitcast.83, s32[1024]{0:T(1024)S(1)} %copy-done.18), kind=kCustom, calls=%fused_computation.3 | custom fusion | bytes 6144 | tf_op jit(solution)/shard_map/gather | solution.py:138
  201.0 2.0 collective-permute-start.41
  203.0 1.3 collective-permute-start.40
  204.9 3.5 %scatter_custom_fusion.3 = f32[65536]{0:T(1024)S(1)} fusion(s32[512]{0:T(512)} %param.23, f32[512]{0:T(512)S(1)} %get-tuple-element.61, f32[]{:T(128)} %constant.11.clone.1), kind=kCustom, calls=%fused_computation.148 | custom fusion | flops 512 | bytes 262656 | tf_op jit(solution)/shard_map/scatter-add | solution.py:140
  (253 shorter events, 25.9 us)
Async XLA Ops:
  0.6 26.6 %copy-start.2 = (f32[16,16,256]{2,1,0:T(8,128)S(1)}, f32[16,16,256]{2,1,0:T(8,128)}, u32[]{:S(2)}) copy-start(f32[16,16,256]{2,1,0:T(8,128)} %param.13) | copy-start | bytes 786436
  0.6 30.0 %copy-start = (f32[4,16,16,256]{3,2,1,0:T(8,128)S(1)}, f32[4,16,16,256]{3,2,1,0:T(8,128)}, u32[]{:S(2)}) copy-start(f32[4,16,16,256]{3,2,1,0:T(8,128)} %param.16) | copy-start | bytes 3145732
  0.7 33.1 %collective-permute-start.24 = (f32[512]{0:T(512)S(1)}, f32[512]{0:T(512)S(1)}, u32[]{:S(2)}, u32[]{:S(2)}) collective-permute-start(f32[512]{0:T(512)S(1)} %broadcast.532), channel_id=1, source_target_pairs={{0,1},{1,2},{2,3},{3,4},{4,5},{5,6},{6,7},{7,8},{8,9},{9,10},{10,1... | collective-permute-start | bytes 6152 | tf_op jit(solution)/shard_map/ppermute | solution.py:18
  3.7 21.2 %collective-permute-start.4 = (f32[16,2,256]{2,1,0:T(2,128)S(1)}, f32[16,2,256]{2,1,0:T(2,128)S(1)}, u32[]{:S(2)}, u32[]{:S(2)}) collective-permute-start(f32[16,2,256]{2,1,0:T(2,128)S(1)} %get-tuple-element.50), channel_id=1, source_target_pairs={{0,2},{2,4},{4,6},{6,8},{8,10},{10,12},{12,14},{14,16},{16,18},{18... | collective-permute-start | bytes 98312 | tf_op jit(solution)/shard_map/ppermute | solution.py:18
  7.1 20.1 %collective-permute-start.5 = (f32[16,2,256]{2,1,0:T(2,128)S(1)}, f32[16,2,256]{2,1,0:T(2,128)S(1)}, u32[]{:S(2)}, u32[]{:S(2)}) collective-permute-start(f32[16,2,256]{2,1,0:T(2,128)S(1)} %get-tuple-element.51), channel_id=1, source_target_pairs={{2,0},{4,2},{6,4},{8,6},{10,8},{12,10},{14,12},{16,14},{18,16},{20... | collective-permute-start | bytes 98312 | tf_op jit(solution)/shard_map/ppermute | solution.py:21
  12.7 16.6 %collective-permute-start = (f32[4,16,2,256]{3,2,1,0:T(2,128)S(1)}, f32[4,16,2,256]{3,2,1,0:T(2,128)S(1)}, u32[]{:S(2)}, u32[]{:S(2)}) collective-permute-start(f32[4,16,2,256]{3,2,1,0:T(2,128)S(1)} %get-tuple-element.30), channel_id=1, source_target_pairs={{0,2},{2,4},{4,6},{6,8},{8,10},{10,12},{12,14},{14,16},{16,18},{18... | collective-permute-start | bytes 393224 | tf_op jit(solution)/shard_map/ppermute | solution.py:18
  14.6 16.0 %collective-permute-start.1 = (f32[4,16,2,256]{3,2,1,0:T(2,128)S(1)}, f32[4,16,2,256]{3,2,1,0:T(2,128)S(1)}, u32[]{:S(2)}, u32[]{:S(2)}) collective-permute-start(f32[4,16,2,256]{3,2,1,0:T(2,128)S(1)} %get-tuple-element.31), channel_id=1, source_target_pairs={{2,0},{4,2},{6,4},{8,6},{10,8},{12,10},{14,12},{16,14},{18,16},{20... | collective-permute-start | bytes 393224 | tf_op jit(solution)/shard_map/ppermute | solution.py:21
  20.4 22.6 %copy-start.27 = (f32[4]{0:T(128)}, f32[4]{0:T(128)S(1)}, u32[]{:S(2)}) copy-start(f32[4]{0:T(128)S(1)} %fusion.88) | copy-start | bytes 52
  20.4 22.6 %copy-start.29 = (f32[4]{0:T(128)}, f32[4]{0:T(128)S(1)}, u32[]{:S(2)}) copy-start(f32[4]{0:T(128)S(1)} %broadcast_subtract_fusion.1) | copy-start | bytes 52
  21.1 60.6 %copy-start.17 = (s32[1024]{0:T(1024)}, s32[1024]{0:T(1024)S(1)}, u32[]{:S(2)}) copy-start(s32[1024]{0:T(1024)S(1)} %pad_clamp_fusion) | copy-start | bytes 12292
  21.9 21.1 %copy-start.19 = (f32[4,4]{1,0:T(4,128)}, f32[4,4]{1,0:T(4,128)S(1)}, u32[]{:S(2)}) copy-start(f32[4,4]{1,0:T(4,128)S(1)} %get-tuple-element.106) | copy-start | bytes 196
  21.9 21.1 %copy-start.21 = (f32[4,4]{1,0:T(4,128)}, f32[4,4]{1,0:T(4,128)S(1)}, u32[]{:S(2)}) copy-start(f32[4,4]{1,0:T(4,128)S(1)} %get-tuple-element.107) | copy-start | bytes 196
  21.9 21.1 %copy-start.23 = (f32[4,4]{1,0:T(4,128)}, f32[4,4]{1,0:T(4,128)S(1)}, u32[]{:S(2)}) copy-start(f32[4,4]{1,0:T(4,128)S(1)} %get-tuple-element.116) | copy-start | bytes 196
  21.9 21.1 %copy-start.25 = (f32[4,4]{1,0:T(4,128)}, f32[4,4]{1,0:T(4,128)S(1)}, u32[]{:S(2)}) copy-start(f32[4,4]{1,0:T(4,128)S(1)} %get-tuple-element.117) | copy-start | bytes 196
  21.9 50.3 %copy-start.41 = (pred[4]{0:T(512)(128)(4,1)}, pred[4]{0:T(512)(128)(4,1)S(1)}, u32[]{:S(2)}) copy-start(pred[4]{0:T(512)(128)(4,1)S(1)} %iota_compare_fusion.11) | copy-start | bytes 16
  22.7 50.0 %copy-start.44 = (pred[16]{0:T(512)(128)(4,1)}, pred[16]{0:T(512)(128)(4,1)S(1)}, u32[]{:S(2)}) copy-start(pred[16]{0:T(512)(128)(4,1)S(1)} %broadcast_in_dim.249) | copy-start | bytes 52
  24.9 10.1 %collective-permute-start.25 = (f32[512]{0:T(512)S(1)}, f32[512]{0:T(512)S(1)}, u32[]{:S(2)}, u32[]{:S(2)}) collective-permute-start(f32[512]{0:T(512)S(1)} %broadcast.532), channel_id=1, source_target_pairs={{1,0},{2,1},{3,2},{4,3},{5,4},{6,5},{7,6},{8,7},{9,8},{10,9},{11,1... | collective-permute-start | bytes 6152 | tf_op jit(solution)/shard_map/ppermute | solution.py:21
  27.3 14.0 %collective-permute-start.6 = (f32[2,20,256]{2,1,0:T(8,128)S(1)}, f32[2,20,256]{2,1,0:T(8,128)S(1)}, u32[]{:S(2)}, u32[]{:S(2)}) collective-permute-start(f32[2,20,256]{2,1,0:T(8,128)S(1)} %get-tuple-element.34), channel_id=1, source_target_pairs={{0,1},{2,3},{4,5},{6,7},{8,9},{10,11},{12,13},{14,15},{16,17},{18,... | collective-permute-start | bytes 122888 | tf_op jit(solution)/shard_map/ppermute | solution.py:18
  29.3 12.0 %collective-permute-start.7 = (f32[2,20,256]{2,1,0:T(8,128)S(1)}, f32[2,20,256]{2,1,0:T(8,128)S(1)}, u32[]{:S(2)}, u32[]{:S(2)}) collective-permute-start(f32[2,20,256]{2,1,0:T(8,128)S(1)} %get-tuple-element.35), channel_id=1, source_target_pairs={{1,0},{3,2},{5,4},{7,6},{9,8},{11,10},{13,12},{15,14},{17,16},{19,... | collective-permute-start | bytes 122888 | tf_op jit(solution)/shard_map/ppermute | solution.py:21
  30.7 10.7 %collective-permute-start.2 = (f32[4,2,20,256]{3,2,1,0:T(8,128)S(1)}, f32[4,2,20,256]{3,2,1,0:T(8,128)S(1)}, u32[]{:S(2)}, u32[]{:S(2)}) collective-permute-start(f32[4,2,20,256]{3,2,1,0:T(8,128)S(1)} %get-tuple-element.28), channel_id=1, source_target_pairs={{0,1},{2,3},{4,5},{6,7},{8,9},{10,11},{12,13},{14,15},{16,17},{18,... | collective-permute-start | bytes 491528 | tf_op jit(solution)/shard_map/ppermute | solution.py:18
  33.8 7.7 %collective-permute-start.3 = (f32[4,2,20,256]{3,2,1,0:T(8,128)S(1)}, f32[4,2,20,256]{3,2,1,0:T(8,128)S(1)}, u32[]{:S(2)}, u32[]{:S(2)}) collective-permute-start(f32[4,2,20,256]{3,2,1,0:T(8,128)S(1)} %get-tuple-element.29), channel_id=1, source_target_pairs={{1,0},{3,2},{5,4},{7,6},{9,8},{11,10},{13,12},{15,14},{17,16},{19,... | collective-permute-start | bytes 491528 | tf_op jit(solution)/shard_map/ppermute | solution.py:21
  41.5 16.0 %copy-start.15 = (f32[4,4,4]{2,1,0:T(4,128)S(1)}, f32[4,4,4]{2,1,0:T(4,128)}, u32[]{:S(2)}) copy-start(f32[4,4,4]{2,1,0:T(4,128)} %param.18) | copy-start | bytes 772
  43.4 7.7 %collective-permute-start.8 = (f32[4,1]{1,0:T(4,128)S(1)}, f32[4,1]{1,0:T(4,128)S(1)}, u32[]{:S(2)}, u32[]{:S(2)}) collective-permute-start(f32[4,1]{1,0:T(4,128)S(1)} %get-tuple-element.104), channel_id=1, source_target_pairs={{0,2},{2,4},{4,6},{6,8},{8,10},{10,12},{12,14},{14,16},{16,18},{18... | collective-permute-start | bytes 56 | tf_op jit(solution)/shard_map/ppermute | solution.py:18
  46.3 6.0 %collective-permute-start.9 = (f32[4,1]{1,0:T(4,128)S(1)}, f32[4,1]{1,0:T(4,128)S(1)}, u32[]{:S(2)}, u32[]{:S(2)}) collective-permute-start(f32[4,1]{1,0:T(4,128)S(1)} %get-tuple-element.105), channel_id=1, source_target_pairs={{2,0},{4,2},{6,4},{8,6},{10,8},{12,10},{14,12},{16,14},{18,16},{20... | collective-permute-start | bytes 56 | tf_op jit(solution)/shard_map/ppermute | solution.py:21
  52.4 3.3 %collective-permute-start.10 = (f32[1,6]{1,0:T(1,128)S(1)}, f32[1,6]{1,0:T(1,128)S(1)}, u32[]{:S(2)}, u32[]{:S(2)}) collective-permute-start(f32[1,6]{1,0:T(1,128)S(1)} %get-tuple-element.100), channel_id=1, source_target_pairs={{0,1},{2,3},{4,5},{6,7},{8,9},{10,11},{12,13},{14,15},{16,17},{18,... | collective-permute-start | bytes 80 | tf_op jit(solution)/shard_map/ppermute | solution.py:18
  54.3 3.1 %collective-permute-start.11 = (f32[1,6]{1,0:T(1,128)S(1)}, f32[1,6]{1,0:T(1,128)S(1)}, u32[]{:S(2)}, u32[]{:S(2)}) collective-permute-start(f32[1,6]{1,0:T(1,128)S(1)} %get-tuple-element.101), channel_id=1, source_target_pairs={{1,0},{3,2},{5,4},{7,6},{9,8},{11,10},{13,12},{15,14},{17,16},{19,... | collective-permute-start | bytes 80 | tf_op jit(solution)/shard_map/ppermute | solution.py:21
  57.6 7.8 %collective-permute-start.12 = (f32[4,1]{1,0:T(4,128)S(1)}, f32[4,1]{1,0:T(4,128)S(1)}, u32[]{:S(2)}, u32[]{:S(2)}) collective-permute-start(f32[4,1]{1,0:T(4,128)S(1)} %get-tuple-element.98), channel_id=1, source_target_pairs={{0,2},{2,4},{4,6},{6,8},{8,10},{10,12},{12,14},{14,16},{16,18},{18... | collective-permute-start | bytes 56 | tf_op jit(solution)/shard_map/ppermute | solution.py:18
  59.9 6.7 %collective-permute-start.13 = (f32[4,1]{1,0:T(4,128)S(1)}, f32[4,1]{1,0:T(4,128)S(1)}, u32[]{:S(2)}, u32[]{:S(2)}) collective-permute-start(f32[4,1]{1,0:T(4,128)S(1)} %get-tuple-element.99), channel_id=1, source_target_pairs={{2,0},{4,2},{6,4},{8,6},{10,8},{12,10},{14,12},{16,14},{18,16},{20... | collective-permute-start | bytes 56 | tf_op jit(solution)/shard_map/ppermute | solution.py:21
  66.8 4.3 %collective-permute-start.15 = (f32[1,6]{1,0:T(1,128)S(1)}, f32[1,6]{1,0:T(1,128)S(1)}, u32[]{:S(2)}, u32[]{:S(2)}) collective-permute-start(f32[1,6]{1,0:T(1,128)S(1)} %get-tuple-element.96), channel_id=1, source_target_pairs={{1,0},{3,2},{5,4},{7,6},{9,8},{11,10},{13,12},{15,14},{17,16},{19,... | collective-permute-start | bytes 80 | tf_op jit(solution)/shard_map/ppermute | solution.py:21
  68.1 3.8 %collective-permute-start.14 = (f32[1,6]{1,0:T(1,128)S(1)}, f32[1,6]{1,0:T(1,128)S(1)}, u32[]{:S(2)}, u32[]{:S(2)}) collective-permute-start(f32[1,6]{1,0:T(1,128)S(1)} %get-tuple-element.97), channel_id=1, source_target_pairs={{0,1},{2,3},{4,5},{6,7},{8,9},{10,11},{12,13},{14,15},{16,17},{18,... | collective-permute-start | bytes 80 | tf_op jit(solution)/shard_map/ppermute | solution.py:18
  73.0 16.4 %copy-start.43 = (f32[512]{0:T(512)S(1)}, f32[512]{0:T(512)}, u32[]{:S(2)}) copy-start(f32[512]{0:T(512)} %param.21) | copy-start | bytes 6148
  73.0 11.8 %collective-permute-start.16 = (f32[16,1,256]{2,1,0:T(1,128)S(1)}, f32[16,1,256]{2,1,0:T(1,128)S(1)}, u32[]{:S(2)}, u32[]{:S(2)}) collective-permute-start(f32[16,1,256]{2,1,0:T(1,128)S(1)} %get-tuple-element.48), channel_id=1, source_target_pairs={{0,2},{2,4},{4,6},{6,8},{8,10},{10,12},{12,14},{14,16},{16,18},{18... | collective-permute-start | bytes 49160 | tf_op jit(solution)/shard_map/ppermute | solution.py:18
  77.3 7.6 %collective-permute-start.17 = (f32[16,1,256]{2,1,0:T(1,128)S(1)}, f32[16,1,256]{2,1,0:T(1,128)S(1)}, u32[]{:S(2)}, u32[]{:S(2)}) collective-permute-start(f32[16,1,256]{2,1,0:T(1,128)S(1)} %get-tuple-element.49), channel_id=1, source_target_pairs={{2,0},{4,2},{6,4},{8,6},{10,8},{12,10},{14,12},{16,14},{18,16},{20... | collective-permute-start | bytes 49160 | tf_op jit(solution)/shard_map/ppermute | solution.py:21
  85.5 13.0 %collective-permute-start.19 = (f32[1,18,256]{2,1,0:T(8,128)}, f32[1,18,256]{2,1,0:T(8,128)}, u32[]{:S(2)}, u32[]{:S(2)}) collective-permute-start(f32[1,18,256]{2,1,0:T(8,128)} %get-tuple-element.40), channel_id=1, source_target_pairs={{0,1},{2,3},{4,5},{6,7},{8,9},{10,11},{12,13},{14,15},{16,17},{18,... | collective-permute-start | bytes 55304 | tf_op jit(solution)/shard_map/ppermute | solution.py:18
  88.1 10.4 %collective-permute-start.18 = (f32[1,18,256]{2,1,0:T(8,128)}, f32[1,18,256]{2,1,0:T(8,128)}, u32[]{:S(2)}, u32[]{:S(2)}) collective-permute-start(f32[1,18,256]{2,1,0:T(8,128)} %get-tuple-element.41), channel_id=1, source_target_pairs={{1,0},{3,2},{5,4},{7,6},{9,8},{11,10},{13,12},{15,14},{17,16},{19,... | collective-permute-start | bytes 55304 | tf_op jit(solution)/shard_map/ppermute | solution.py:21
  102.1 12.8 %collective-permute-start.20 = (f32[16,1,256]{2,1,0:T(1,128)}, f32[16,1,256]{2,1,0:T(1,128)S(1)}, u32[]{:S(2)}, u32[]{:S(2)}) collective-permute-start(f32[16,1,256]{2,1,0:T(1,128)} %get-tuple-element.46), channel_id=1, source_target_pairs={{0,2},{2,4},{4,6},{6,8},{8,10},{10,12},{12,14},{14,16},{16,18},{18... | collective-permute-start | bytes 49160 | tf_op jit(solution)/shard_map/ppermute | solution.py:18
  104.3 10.6 %collective-permute-start.21 = (f32[16,1,256]{2,1,0:T(1,128)}, f32[16,1,256]{2,1,0:T(1,128)}, u32[]{:S(2)}, u32[]{:S(2)}) collective-permute-start(f32[16,1,256]{2,1,0:T(1,128)} %get-tuple-element.47), channel_id=1, source_target_pairs={{2,0},{4,2},{6,4},{8,6},{10,8},{12,10},{14,12},{16,14},{18,16},{20... | collective-permute-start | bytes 49160 | tf_op jit(solution)/shard_map/ppermute | solution.py:21
  116.2 10.6 %collective-permute-start.23 = (f32[1,18,256]{2,1,0:T(8,128)}, f32[1,18,256]{2,1,0:T(8,128)}, u32[]{:S(2)}, u32[]{:S(2)}) collective-permute-start(f32[1,18,256]{2,1,0:T(8,128)} %get-tuple-element.38), channel_id=1, source_target_pairs={{0,1},{2,3},{4,5},{6,7},{8,9},{10,11},{12,13},{14,15},{16,17},{18,... | collective-permute-start | bytes 55304 | tf_op jit(solution)/shard_map/ppermute | solution.py:18
  119.9 6.9 %collective-permute-start.22 = (f32[1,18,256]{2,1,0:T(8,128)}, f32[1,18,256]{2,1,0:T(8,128)}, u32[]{:S(2)}, u32[]{:S(2)}) collective-permute-start(f32[1,18,256]{2,1,0:T(8,128)} %get-tuple-element.39), channel_id=1, source_target_pairs={{1,0},{3,2},{5,4},{7,6},{9,8},{11,10},{13,12},{15,14},{17,16},{19,... | collective-permute-start | bytes 55304 | tf_op jit(solution)/shard_map/ppermute | solution.py:21
  129.4 15.0 %collective-permute-start.26 = (f32[16,2,256]{2,1,0:T(2,128)S(1)}, f32[16,2,256]{2,1,0:T(2,128)S(1)}, u32[]{:S(2)}, u32[]{:S(2)}) collective-permute-start(f32[16,2,256]{2,1,0:T(2,128)S(1)} %get-tuple-element.44), channel_id=1, source_target_pairs={{0,2},{2,4},{4,6},{6,8},{8,10},{10,12},{12,14},{14,16},{16,18},{18... | collective-permute-start | bytes 98312 | tf_op jit(solution)/shard_map/ppermute | solution.py:18
  131.3 13.1 %collective-permute-start.27 = (f32[16,2,256]{2,1,0:T(2,128)S(1)}, f32[16,2,256]{2,1,0:T(2,128)S(1)}, u32[]{:S(2)}, u32[]{:S(2)}) collective-permute-start(f32[16,2,256]{2,1,0:T(2,128)S(1)} %get-tuple-element.45), channel_id=1, source_target_pairs={{2,0},{4,2},{6,4},{8,6},{10,8},{12,10},{14,12},{16,14},{18,16},{20... | collective-permute-start | bytes 98312 | tf_op jit(solution)/shard_map/ppermute | solution.py:21
  137.1 11.4 %collective-permute-start.42 = (f32[512]{0:T(512)S(1)}, f32[512]{0:T(512)S(1)}, u32[]{:S(2)}, u32[]{:S(2)}) collective-permute-start(f32[512]{0:T(512)S(1)} %copy-done.13), channel_id=1, source_target_pairs={{0,1},{1,2},{2,3},{3,4},{4,5},{5,6},{6,7},{7,8},{8,9},{9,10},{10,1... | collective-permute-start | bytes 6152 | tf_op jit(solution)/shard_map/ppermute | solution.py:18
  140.2 8.4 %collective-permute-start.43 = (f32[512]{0:T(512)S(1)}, f32[512]{0:T(512)S(1)}, u32[]{:S(2)}, u32[]{:S(2)}) collective-permute-start(f32[512]{0:T(512)S(1)} %copy-done.13), channel_id=1, source_target_pairs={{1,0},{2,1},{3,2},{4,3},{5,4},{6,5},{7,6},{8,7},{9,8},{10,9},{11,1... | collective-permute-start | bytes 6152 | tf_op jit(solution)/shard_map/ppermute | solution.py:21
  145.1 9.7 %collective-permute-start.28 = (f32[2,20,256]{2,1,0:T(8,128)}, f32[2,20,256]{2,1,0:T(8,128)}, u32[]{:S(2)}, u32[]{:S(2)}) collective-permute-start(f32[2,20,256]{2,1,0:T(8,128)} %get-tuple-element.32), channel_id=1, source_target_pairs={{0,1},{2,3},{4,5},{6,7},{8,9},{10,11},{12,13},{14,15},{16,17},{18,... | collective-permute-start | bytes 122888 | tf_op jit(solution)/shard_map/ppermute | solution.py:18
  147.0 7.8 %collective-permute-start.29 = (f32[2,20,256]{2,1,0:T(8,128)}, f32[2,20,256]{2,1,0:T(8,128)}, u32[]{:S(2)}, u32[]{:S(2)}) collective-permute-start(f32[2,20,256]{2,1,0:T(8,128)} %get-tuple-element.33), channel_id=1, source_target_pairs={{1,0},{3,2},{5,4},{7,6},{9,8},{11,10},{13,12},{15,14},{17,16},{19,... | collective-permute-start | bytes 122888 | tf_op jit(solution)/shard_map/ppermute | solution.py:21
  155.9 17.5 %copy-start.16 = (f32[4,4,4]{2,1,0:T(4,128)S(1)}, f32[4,4,4]{2,1,0:T(4,128)}, u32[]{:S(2)}) copy-start(f32[4,4,4]{2,1,0:T(4,128)} %param.18) | copy-start | bytes 772
  155.9 32.1 %copy-start.42 = (pred[4]{0:T(512)(128)(4,1)S(1)}, pred[4]{0:T(512)(128)(4,1)}, u32[]{:S(2)}) copy-start(pred[4]{0:T(512)(128)(4,1)} %copy-done.41) | copy-start | bytes 16
  155.9 32.7 %copy-start.45 = (pred[16]{0:T(512)(128)(4,1)S(1)}, pred[16]{0:T(512)(128)(4,1)}, u32[]{:S(2)}) copy-start(pred[16]{0:T(512)(128)(4,1)} %copy-done.44) | copy-start | bytes 52
  158.5 38.5 %copy-start.14 = (f32[512]{0:T(512)S(1)}, f32[512]{0:T(512)}, u32[]{:S(2)}) copy-start(f32[512]{0:T(512)} %get-tuple-element.25) | copy-start | bytes 6148
  158.5 38.5 %copy-start.35 = (f32[2,512]{1,0:T(2,128)S(1)}, f32[2,512]{1,0:T(2,128)}, u32[]{:S(2)}) copy-start(f32[2,512]{1,0:T(2,128)} %param.22) | copy-start | bytes 12292
  158.9 7.7 %collective-permute-start.30 = (f32[4,1]{1,0:T(4,128)S(1)}, f32[4,1]{1,0:T(4,128)S(1)}, u32[]{:S(2)}, u32[]{:S(2)}) collective-permute-start(f32[4,1]{1,0:T(4,128)S(1)} %get-tuple-element.92), channel_id=1, source_target_pairs={{0,2},{2,4},{4,6},{6,8},{8,10},{10,12},{12,14},{14,16},{16,18},{18... | collective-permute-start | bytes 56 | tf_op jit(solution)/shard_map/ppermute | solution.py:18
  160.9 7.0 %collective-permute-start.31 = (f32[4,1]{1,0:T(4,128)S(1)}, f32[4,1]{1,0:T(4,128)S(1)}, u32[]{:S(2)}, u32[]{:S(2)}) collective-permute-start(f32[4,1]{1,0:T(4,128)S(1)} %get-tuple-element.93), channel_id=1, source_target_pairs={{2,0},{4,2},{6,4},{8,6},{10,8},{12,10},{14,12},{16,14},{18,16},{20... | collective-permute-start | bytes 56 | tf_op jit(solution)/shard_map/ppermute | solution.py:21
  168.0 3.7 %collective-permute-start.32 = (f32[1,6]{1,0:T(1,128)S(1)}, f32[1,6]{1,0:T(1,128)S(1)}, u32[]{:S(2)}, u32[]{:S(2)}) collective-permute-start(f32[1,6]{1,0:T(1,128)S(1)} %get-tuple-element.88), channel_id=1, source_target_pairs={{0,1},{2,3},{4,5},{6,7},{8,9},{10,11},{12,13},{14,15},{16,17},{18,... | collective-permute-start | bytes 80 | tf_op jit(solution)/shard_map/ppermute | solution.py:18
  170.3 3.1 %collective-permute-start.33 = (f32[1,6]{1,0:T(1,128)S(1)}, f32[1,6]{1,0:T(1,128)S(1)}, u32[]{:S(2)}, u32[]{:S(2)}) collective-permute-start(f32[1,6]{1,0:T(1,128)S(1)} %get-tuple-element.89), channel_id=1, source_target_pairs={{1,0},{3,2},{5,4},{7,6},{9,8},{11,10},{13,12},{15,14},{17,16},{19,... | collective-permute-start | bytes 80 | tf_op jit(solution)/shard_map/ppermute | solution.py:21
  173.6 7.8 %collective-permute-start.34 = (f32[4,1]{1,0:T(4,128)S(1)}, f32[4,1]{1,0:T(4,128)S(1)}, u32[]{:S(2)}, u32[]{:S(2)}) collective-permute-start(f32[4,1]{1,0:T(4,128)S(1)} %get-tuple-element.86), channel_id=1, source_target_pairs={{0,2},{2,4},{4,6},{6,8},{8,10},{10,12},{12,14},{14,16},{16,18},{18... | collective-permute-start | bytes 56 | tf_op jit(solution)/shard_map/ppermute | solution.py:18
  175.5 7.0 %collective-permute-start.35 = (f32[4,1]{1,0:T(4,128)S(1)}, f32[4,1]{1,0:T(4,128)S(1)}, u32[]{:S(2)}, u32[]{:S(2)}) collective-permute-start(f32[4,1]{1,0:T(4,128)S(1)} %get-tuple-element.87), channel_id=1, source_target_pairs={{2,0},{4,2},{6,4},{8,6},{10,8},{12,10},{14,12},{16,14},{18,16},{20... | collective-permute-start | bytes 56 | tf_op jit(solution)/shard_map/ppermute | solution.py:21
  182.7 4.3 %collective-permute-start.37 = (f32[1,6]{1,0:T(1,128)S(1)}, f32[1,6]{1,0:T(1,128)S(1)}, u32[]{:S(2)}, u32[]{:S(2)}) collective-permute-start(f32[1,6]{1,0:T(1,128)S(1)} %get-tuple-element.84), channel_id=1, source_target_pairs={{1,0},{3,2},{5,4},{7,6},{9,8},{11,10},{13,12},{15,14},{17,16},{19,... | collective-permute-start | bytes 80 | tf_op jit(solution)/shard_map/ppermute | solution.py:21
  184.0 3.8 %collective-permute-start.36 = (f32[1,6]{1,0:T(1,128)S(1)}, f32[1,6]{1,0:T(1,128)S(1)}, u32[]{:S(2)}, u32[]{:S(2)}) collective-permute-start(f32[1,6]{1,0:T(1,128)S(1)} %get-tuple-element.85), channel_id=1, source_target_pairs={{0,1},{2,3},{4,5},{6,7},{8,9},{10,11},{12,13},{14,15},{16,17},{18,... | collective-permute-start | bytes 80 | tf_op jit(solution)/shard_map/ppermute | solution.py:18
  189.0 15.3 %copy-start.31 = (f32[512]{0:T(512)S(1)}, f32[512]{0:T(512)}, u32[]{:S(2)}) copy-start(f32[512]{0:T(512)} %get-tuple-element.27) | copy-start | bytes 6148
  189.0 15.3 %copy-start.32 = (f32[512]{0:T(512)S(1)}, f32[512]{0:T(512)}, u32[]{:S(2)}) copy-start(f32[512]{0:T(512)} %get-tuple-element.18) | copy-start | bytes 6148
  189.0 11.3 %collective-permute-start.38 = (f32[16,1,256]{2,1,0:T(1,128)S(1)}, f32[16,1,256]{2,1,0:T(1,128)S(1)}, u32[]{:S(2)}, u32[]{:S(2)}) collective-permute-start(f32[16,1,256]{2,1,0:T(1,128)S(1)} %get-tuple-element.42), channel_id=1, source_target_pairs={{0,2},{2,4},{4,6},{6,8},{8,10},{10,12},{12,14},{14,16},{16,18},{18... | collective-permute-start | bytes 49160 | tf_op jit(solution)/shard_map/ppermute | solution.py:18
  193.3 7.0 %collective-permute-start.39 = (f32[16,1,256]{2,1,0:T(1,128)S(1)}, f32[16,1,256]{2,1,0:T(1,128)S(1)}, u32[]{:S(2)}, u32[]{:S(2)}) collective-permute-start(f32[16,1,256]{2,1,0:T(1,128)S(1)} %get-tuple-element.43), channel_id=1, source_target_pairs={{2,0},{4,2},{6,4},{8,6},{10,8},{12,10},{14,12},{16,14},{18,16},{20... | collective-permute-start | bytes 49160 | tf_op jit(solution)/shard_map/ppermute | solution.py:21
  201.0 7.5 %collective-permute-start.41 = (f32[1,18,256]{2,1,0:T(8,128)}, f32[1,18,256]{2,1,0:T(8,128)S(1)}, u32[]{:S(2)}, u32[]{:S(2)}) collective-permute-start(f32[1,18,256]{2,1,0:T(8,128)} %get-tuple-element.36), channel_id=1, source_target_pairs={{0,1},{2,3},{4,5},{6,7},{8,9},{10,11},{12,13},{14,15},{16,17},{18,... | collective-permute-start | bytes 55304 | tf_op jit(solution)/shard_map/ppermute | solution.py:18
  203.0 5.5 %collective-permute-start.40 = (f32[1,18,256]{2,1,0:T(8,128)S(1)}, f32[1,18,256]{2,1,0:T(8,128)S(1)}, u32[]{:S(2)}, u32[]{:S(2)}) collective-permute-start(f32[1,18,256]{2,1,0:T(8,128)S(1)} %get-tuple-element.37), channel_id=1, source_target_pairs={{1,0},{3,2},{5,4},{7,6},{9,8},{11,10},{13,12},{15,14},{17,16},{19,... | collective-permute-start | bytes 55304 | tf_op jit(solution)/shard_map/ppermute | solution.py:21
  (26 other events, 174.2 us)
where the time goes:
time: 213 us; the launch traced here: 210 us
  starting transfers between devices  127 us (60%)
  other arithmetic  37.9 us (18%)
  local copies, waits for them, and re-layouts  32.4 us (15%)
  waiting for transfers between devices  9.83 us (5%)
  between operations  2.87 us (1%)
    ppermute x22, starting transfers between devices, padded_2(): lax.ppermute(lax.slice_in_dim(block, 0, width, axis=dim), axis, backward)  69.6 us
    ppermute x22, starting transfers between devices, padded_2(): lax.ppermute(lax.slice_in_dim(block, block.shape[dim] - width, None, axis...  57.5 us
    gather x3, local copies, waits for them, and re-layouts, local(): peer_values = fracture_wide[local_peer]  12.4 us
    gather x3, local copies, waits for them, and re-layouts, matrix_rows(): pressure_at = pressure.reshape(-1)[cell_index]  10.7 us
    scatter-add x3, other arithmetic, matrix_rows(): jax.ops.segment_sum(link_flux, cell_index, num_segments=pressure.size)  10.4 us
    ppermute x22, waiting for transfers between devices, padded_2(): lax.ppermute(lax.slice_in_dim(block, 0, width, axis=dim), axis, backward)  8.2 us
    concatenate x22, other arithmetic, padded_2(): block = jnp.concatenate([low, block, high], axis=dim)  7.15 us
  transfers between devices with their start and end apart: 44, of which 8 were waited for; matrix products, arithmetic and copies ran while one was open for 24% of the time, Pallas kernels for 0%

commit v1 on v0

v1 whole, which is shorter than its diff:
```python
import jax
import jax.numpy as jnp
from jax import lax
from jax.experimental import pallas as pl
from jax.experimental.pallas import tpu as pltpu
from jax.sharding import PartitionSpec as P

BLOCK = 4
OMEGA = 0.8
TILE = 8
LANES = 128
F32 = jnp.float32
BF16 = jnp.bfloat16


def pair_lists(count):
    even = [(i, i ^ 1) for i in range(count) if i ^ 1 < count]
    odd = [(i, i + 1 if i % 2 else i - 1) for i in range(1, count)]
    return even, [(a, b) for a, b in odd if 0 < b < count]


def swap_pairs(even_load, odd_load, axis):
    even, odd = pair_lists(lax.axis_size(axis))
    got = [lax.ppermute(even_load, axis, even)]
    if odd:
        got.append(lax.ppermute(odd_load, axis, odd))
    return got


def run(kernel, name, outs, args, scratch=(), smem=()):
    spec = pl.BlockSpec(memory_space=pltpu.VMEM)
    scalar = pl.BlockSpec(memory_space=pltpu.SMEM)
    return pl.pallas_call(
        kernel,
        name=name,
        out_shape=[jax.ShapeDtypeStruct(shape, dtype) for shape, dtype in outs],
        in_specs=[scalar if i in smem else spec for i in range(len(args))],
        out_specs=[spec] * len(outs),
        scratch_shapes=list(scratch),
        compiler_params=pltpu.CompilerParams(vmem_limit_bytes=24 << 20),
    )(*args)


def iota(shape, dim):
    return lax.broadcasted_iota(jnp.int32, shape, dim)


def own_node(cell):
    return cell // BLOCK


def side_node(cell):
    return cell // BLOCK + (-1 if cell % BLOCK < BLOCK // 2 else 1)


def own_nodes(cells):
    return lax.shift_right_arithmetic(cells, 2)


def side_nodes(cells):
    low = jnp.bitwise_and(cells, BLOCK - 1) < BLOCK // 2
    return own_nodes(cells) + jnp.where(low, -1, 1)


def node_masks(cells):
    index = iota((cells, LANES), 0)
    lane = iota((cells, LANES), 1)
    return own_nodes(index) + 2 == lane, side_nodes(index) + 2 == lane


def fold_lanes(value):
    total = value[:, :LANES]
    for start in range(LANES, value.shape[1], LANES):
        total = total + value[:, start : start + LANES]
    return total


def by_parity(is_even, even_value, odd_value):
    return jnp.where(jnp.full(even_value.shape, is_even, jnp.int32) > 0, even_value, odd_value)


def low_high(is_even, even_got, odd_got):
    low = by_parity(is_even, odd_got, even_got)
    high = by_parity(is_even, even_got, odd_got)
    return low, high


def restrict_tile(columns, rows, cell_rows, cell_cols):
    sums = {}
    for x, residual, weight in columns:
        for k in range(4):
            node = (own_node(x) if k % 2 == 0 else side_node(x)) + 2
            part = fold_lanes(weight(k) * residual)
            key = (k // 2, node)
            sums[key] = sums[key] + part if key in sums else part
    masks = node_masks(cell_cols)
    row_index = iota((TILE, LANES), 0)
    tile = jnp.zeros((TILE, LANES), F32)
    nodes = sorted({node for _, node in sums})
    wide = {}
    if rows:
        lane = iota((cell_rows, LANES), 1)
        for y, residual, weight in rows:
            for k in range(4):
                node = (own_node(y) if k < 2 else side_node(y)) + 2
                part = jnp.sum(fold_lanes(weight(k) * residual), axis=1, keepdims=True)
                part = jnp.where(lane == node, part, 0.0)
                wide[k % 2] = wide[k % 2] + part if k % 2 in wide else part
        x_index = iota((cell_rows, LANES), 0)
        x_nodes = (own_nodes(x_index) + 2, side_nodes(x_index) + 2)
    for node in nodes:
        total = jnp.zeros((cell_cols, LANES), F32)
        for kind in range(2):
            if (kind, node) in sums:
                lane_sum = jnp.sum(sums[(kind, node)], axis=1, keepdims=True)
                total = total + jnp.where(masks[kind], lane_sum, 0.0)
        line = jnp.sum(total, axis=0, keepdims=True)
        if rows:
            extra = jnp.where(x_nodes[0] == node, wide[0], 0.0) + jnp.where(
                x_nodes[1] == node, wide[1], 0.0
            )
            line = line + jnp.sum(extra, axis=0, keepdims=True)
        tile = jnp.where(row_index == node, line, tile)
    return tile


def join_rows(tile, low, high):
    row = iota((TILE, LANES), 0)
    half = TILE // 2
    return (
        tile
        + jnp.where(row < half, pltpu.roll(low, half, 0), 0.0)
        + jnp.where(row >= half, pltpu.roll(high, half, 0), 0.0)
    )


def join_lanes(tile, low, high):
    part = jnp.bitwise_and(iota((TILE, LANES), 1), TILE - 1)
    half = TILE // 2
    return (
        tile
        + jnp.where(part < half, pltpu.roll(low, LANES - half, 1), 0.0)
        + jnp.where(part >= half, pltpu.roll(high, half, 1), 0.0)
    )


def coarse_solve(tile, table):
    lane = iota((TILE, LANES), 1)
    diag = pltpu.roll(table, LANES - TILE, 1)
    live = (lane < TILE) & (diag > 0.0)
    first = jnp.where(live, tile / jnp.where(live, diag, 1.0), 0.0)
    near = (
        pltpu.roll(first, 1, 0),
        pltpu.roll(first, TILE - 1, 0),
        pltpu.roll(first, 1, 1),
        pltpu.roll(first, LANES - 1, 1),
    )
    second = first
    for direction in range(4):
        ratio = pltpu.roll(table, LANES - TILE * (2 + direction), 1)
        second = second + jnp.where(lane < TILE, ratio, 0.0) * near[direction]
    return second


class Fields:
    def __init__(self, second, cell_rows, cell_cols):
        masks = node_masks(cell_cols)
        self.columns = {}
        for node in range(1, TILE - 1):
            line = jnp.broadcast_to(second[node : node + 1, :], (cell_cols, LANES))
            for kind in range(2):
                self.columns[(kind, node)] = jnp.sum(
                    jnp.where(masks[kind], line, 0.0), axis=1, keepdims=True
                )
        x_index = iota((cell_rows, LANES), 0)
        self.wide = []
        for nodes in (own_nodes(x_index) + 2, side_nodes(x_index) + 2):
            value = jnp.zeros((cell_rows, LANES), F32)
            for node in range(1, TILE - 1):
                value = jnp.where(nodes == node, second[node : node + 1, :], value)
            self.wide.append(value)

    def column(self, x, weight):
        own, side = own_node(x) + 2, side_node(x) + 2
        return (
            weight(0) * self.columns[(0, own)]
            + weight(1) * self.columns[(0, side)]
            + weight(2) * self.columns[(1, own)]
            + weight(3) * self.columns[(1, side)]
        )

    def row(self, y, weight):
        lane = iota(self.wide[0].shape, 1)

        def pick(kind, node):
            return jnp.sum(jnp.where(lane == node, self.wide[kind], 0.0), axis=1, keepdims=True)

        own, side = own_node(y) + 2, side_node(y) + 2
        return (
            weight(0) * pick(0, own)
            + weight(1) * pick(1, own)
            + weight(2) * pick(0, side)
            + weight(3) * pick(1, side)
        )


def neighbour_sum(faces, x, left, centre, right, low_row, high_row):
    cols, depth = centre.shape
    row = iota(centre.shape, 0)
    lane = iota(centre.shape, 1)
    above = pltpu.roll(centre, cols - 1, 0)
    below = pltpu.roll(centre, 1, 0)
    above = jnp.where(row == cols - 1, 0.0 if high_row is None else high_row, above)
    below = jnp.where(row == 0, 0.0 if low_row is None else low_row, below)
    deep = jnp.where(lane == depth - 1, 0.0, pltpu.roll(centre, depth - 1, 1))
    shallow = jnp.where(lane == 0, 0.0, pltpu.roll(centre, 1, 1))
    total = faces[2, x] * above + faces[3, x] * below + faces[4, x] * deep + faces[5, x] * shallow
    if right is not None:
        total = total + faces[0, x] * right
    if left is not None:
        total = total + faces[1, x] * left
    return total


def split3(value):
    high = value.astype(BF16)
    rest = value - high.astype(F32)
    mid = rest.astype(BF16)
    return high, mid, (rest - mid.astype(F32)).astype(BF16)


def gather_cells(pressure, hot_row, hot_depth):
    picked = None
    for part in split3(pressure):
        product = jnp.dot(part, hot_depth, preferred_element_type=F32)
        picked = product if picked is None else picked + product
    return jnp.sum(picked * hot_row.astype(F32), axis=0, keepdims=True)


def scatter_cells(values, hot_row, hot_depth):
    total = None
    for part in split3(values):
        spread = hot_row * part
        product = lax.dot_general(
            spread, hot_depth, (((1,), (1,)), ((), ())), preferred_element_type=F32
        )
        total = product if total is None else total + product
    return total


def as_line(value):
    return jnp.concatenate([value[i : i + 1, :] for i in range(value.shape[0])], axis=1)


def as_rows(line, width):
    return jnp.concatenate(
        [line[:, start : start + width] for start in range(0, line.shape[1], width)], axis=0
    )


def local(
    matrix_source,
    accum,
    faces,
    basis,
    coarse_diag,
    coarse_ratio,
    frac_source,
    frac_accum,
    frac_link,
    frac_trans,
    frac_cell,
    frac_peer,
    frac_count,
):
    slots = frac_source.shape[0]
    cell_rows, cell_cols, depth = matrix_source.shape
    cells = cell_rows * cell_cols
    node_rows, node_cols = cell_rows // BLOCK, cell_cols // BLOCK
    assert node_rows + 4 == TILE and node_cols + 4 == TILE
    assert depth & (depth - 1) == 0 and cell_rows == cell_cols
    depth_bits = depth.bit_length() - 1
    lay_size = lax.axis_size("lay")
    lay_pairs = len([p for p in pair_lists(lay_size) if p])
    layer_rows = 4 * cell_cols
    load_one = (layer_rows + TILE, depth)
    slot_rows = slots // depth
    load_two = (cell_cols + 2 * TILE, depth)
    block = matrix_source.shape

    table = jnp.zeros((TILE, LANES), F32)
    table = lax.dynamic_update_slice(table, coarse_diag, (2, TILE + 2))
    for direction in range(4):
        table = lax.dynamic_update_slice(
            table, coarse_ratio[direction], (2, TILE * (2 + direction) + 2)
        )

    def is_even(axis):
        return 1 - jnp.bitwise_and(lax.axis_index(axis), 1)

    def lay_got(refs):
        got = [ref for ref in refs]
        return got if len(got) == 2 else [got[0], None]

    def kernel_a(basis_ref, source_ref, table_ref, tile_ref, *loads):
        def column(x):
            return x, source_ref[x], lambda k: basis_ref[k, x]

        tile = restrict_tile([column(x) for x in range(cell_rows)], [], cell_rows, cell_cols)
        tile = tile + table_ref[...]
        tile_ref[...] = tile
        even = is_even("lay")
        edges = (even * (cell_rows - 1), (1 - even) * (cell_rows - 1))
        for load, edge in zip(loads, edges):
            for k in range(4):
                load[k * cell_cols : (k + 1) * cell_cols, :] = basis_ref[k, edge]
            load[layer_rows:, :LANES] = tile
            load[layer_rows:, LANES:] = jnp.zeros((TILE, depth - LANES), F32)

    outs = [((TILE, LANES), F32)] + [(load_one, F32)] * lay_pairs
    tile_own, *loads = run(kernel_a, "restrict_source", outs, (basis, matrix_source, table))
    lay_one = swap_pairs(loads[0], loads[-1], "lay")

    def lay_sides(refs, window):
        even = is_even("lay")
        first = refs[0][window]
        second = refs[1][window] if len(refs) > 1 else jnp.zeros(first.shape, F32)
        return low_high(even, first, second)

    def blk_sides(even_ref, odd_ref, window):
        return low_high(is_even("blk"), even_ref[window], odd_ref[window])

    def kernel_e(tile_ref, basis_ref, *refs):
        got, (join_ref, even_ref, odd_ref) = refs[:-3], refs[-3:]
        low, high = lay_sides(got, (slice(layer_rows, layer_rows + TILE), slice(0, LANES)))
        joined = join_rows(tile_ref[...], low, high)
        join_ref[...] = joined
        even = is_even("blk")
        edges = (even * (cell_cols - 1), (1 - even) * (cell_cols - 1))
        for ref, edge in zip((even_ref, odd_ref), edges):
            for k in range(4):
                for x in range(cell_rows):
                    line = k * cell_rows + x
                    ref[line : line + 1, :] = basis_ref[k, x, pl.ds(edge, 1), :]
            ref[layer_rows:, :LANES] = joined
            ref[layer_rows:, LANES:] = jnp.zeros((TILE, depth - LANES), F32)

    outs = [((TILE, LANES), F32), (load_one, F32), (load_one, F32)]
    joined_one, even_one, odd_one = run(kernel_e, "join", outs, (tile_own, basis, *lay_one))
    blk_one = swap_pairs(even_one, odd_one, "blk")

    def kernel_p(
        faces_ref, accum_ref, cell_ref, link_ref, facc_ref, trans_ref, peer_ref, count_ref,
        diag_ref, scale_ref, row_ref, depth_ref, frac_ref, low_ref,
    ):
        slot = iota((1, slots), 1)
        live = (slot < count_ref[0]).astype(F32)
        couple = live * as_line(link_ref[...])
        frac_diag = as_line(facc_ref[...]) + couple
        for j in range(trans_ref.shape[0]):
            frac_diag = frac_diag + trans_ref[j : j + 1, :]
        frac_ref[0:1, :] = couple
        frac_ref[1:2, :] = OMEGA * live / frac_diag
        cell = as_line(cell_ref[...])
        at_row = lax.shift_right_logical(cell, depth_bits)
        at_depth = jnp.bitwise_and(cell, depth - 1)
        hot_row = (iota((cells, slots), 0) == at_row).astype(F32).astype(BF16)
        hot_depth = (iota((depth, slots), 0) == at_depth).astype(F32).astype(BF16)
        row_ref[...] = hot_row
        depth_ref[...] = hot_depth
        linked = scatter_cells(couple, hot_row, hot_depth)
        for x in range(cell_rows):
            diag = accum_ref[x]
            for d in range(6):
                diag = diag + faces_ref[d, x]
            diag = diag + linked[x * cell_cols : (x + 1) * cell_cols, :]
            diag_ref[x] = diag
            scale_ref[x] = OMEGA / diag
        owner = lax.axis_index("blk") * lay_size + lax.axis_index("lay")
        peer = peer_ref[...] - (owner - 1) * slots
        peer = jnp.concatenate([peer[j : j + 1, :] for j in range(peer.shape[0])], axis=1)
        low_ref[...] = (
            (iota((LANES, peer.shape[1]), 0) == jnp.bitwise_and(peer, LANES - 1))
            .astype(F32)
            .astype(BF16)
        )
        frac_ref[2:4, :] = as_rows(lax.shift_right_logical(peer, 7), slots).astype(F32)

    links = frac_trans.shape[0]
    outs = [
        (block, F32),
        (block, F32),
        ((cells, slots), BF16),
        ((depth, slots), BF16),
        ((TILE, slots), F32),
        ((LANES, links * slots), BF16),
    ]
    small = (slots // LANES, LANES)
    diag, scale, hot_row, hot_depth, frac_pack, hot_low = run(
        kernel_p,
        "prepare",
        outs,
        (
            faces,
            accum,
            frac_cell.reshape(small),
            frac_link.reshape(small),
            frac_accum.reshape(small),
            frac_trans,
            frac_peer,
            frac_count,
        ),
        smem=(7,),
    )

    layer = (slice(0, layer_rows), slice(0, depth))

    def rims_of(lay_refs, blk_even, blk_odd):
        lay_low, lay_high = lay_sides(lay_refs, layer)
        blk_low, blk_high = blk_sides(blk_even, blk_odd, layer)

        def pick(value):
            return lambda k: value[k * cell_cols : (k + 1) * cell_cols, :]

        return pick(lay_low), pick(lay_high), pick(blk_low), pick(blk_high)

    def kernel_b(
        faces_ref, basis_ref, source_ref, diag_ref, scale_ref, row_ref, depth_ref, frac_ref,
        fsrc_ref, joined_ref, blk_even, blk_odd, *refs,
    ):
        lay_refs = refs[:lay_pairs]
        p2_ref, right_ref, f_ref, tile_ref, second_ref = refs[lay_pairs : lay_pairs + 5]
        loads = refs[lay_pairs + 5 : -2]
        p1_ref, link_ref = refs[-2:]
        at_tile = (slice(layer_rows, layer_rows + TILE), slice(0, LANES))
        low, high = blk_sides(blk_even, blk_odd, at_tile)
        table = join_lanes(joined_ref[...], low, high)
        second_ref[...] = table
        fields = Fields(coarse_solve(table, table), cell_rows, cell_cols)
        x_low, x_high, y_low, y_high = rims_of(lay_refs, blk_even, blk_odd)

        def weight(x):
            return lambda k: basis_ref[k, x]

        for x in range(cell_rows):
            p1_ref[x] = fields.column(x, weight(x))
        left_rim = fields.column(-1, x_low)
        right_rim = fields.column(cell_rows, x_high)
        low_rim = fields.row(-1, y_low)
        high_rim = fields.row(cell_cols, y_high)

        flat = p1_ref[...].reshape(cells, depth)
        pressure_at = gather_cells(flat, row_ref[...], depth_ref[...])
        couple = frac_ref[0:1, :]
        fracture = frac_ref[1:2, :] * (as_line(fsrc_ref[...]) + couple * pressure_at)
        f_ref[...] = fracture
        linked = scatter_cells(couple * fracture, row_ref[...], depth_ref[...])
        link_ref[...] = linked.reshape(block)

        for x in range(cell_rows):
            centre = p1_ref[x]
            left = p1_ref[x - 1] if x else left_rim
            right = p1_ref[x + 1] if x + 1 < cell_rows else right_rim
            around = neighbour_sum(
                faces_ref, x, left, centre, right, low_rim[x : x + 1, :], high_rim[x : x + 1, :]
            )
            p2_ref[x] = (1.0 - OMEGA) * centre + scale_ref[x] * (source_ref[x] + around)

        columns = []
        low_lines, high_lines = [], []
        for x in range(cell_rows):
            centre = p2_ref[x]
            forced = source_ref[x] + link_ref[x]
            right_ref[x] = forced
            left = p2_ref[x - 1] if x else None
            right = p2_ref[x + 1] if x + 1 < cell_rows else None
            around = neighbour_sum(faces_ref, x, left, centre, right, None, None)
            columns.append((x, forced - diag_ref[x] * centre + around, weight(x)))
            low_lines.append(faces_ref[3, x, 0:1, :] * p2_ref[x, 0:1, :])
            high_lines.append(
                faces_ref[2, x, cell_cols - 1 : cell_cols, :]
                * p2_ref[x, cell_cols - 1 : cell_cols, :]
            )
        columns.append((-1, faces_ref[1, 0] * p2_ref[0], x_low))
        last = cell_rows - 1
        columns.append((cell_rows, faces_ref[0, last] * p2_ref[last], x_high))
        rows = [
            (-1, jnp.concatenate(low_lines, axis=0), y_low),
            (cell_cols, jnp.concatenate(high_lines, axis=0), y_high),
        ]
        tile = restrict_tile(columns, rows, cell_rows, cell_cols)
        tile_ref[...] = tile
        even = is_even("lay")
        edges = (even * (cell_rows - 1), (1 - even) * (cell_rows - 1))
        for load, edge in zip(loads, edges):
            load[:cell_cols, :] = p2_ref[edge]
            load[cell_cols : cell_cols + TILE, :LANES] = tile
            load[cell_cols : cell_cols + TILE, LANES:] = jnp.zeros((TILE, depth - LANES), F32)
            load[cell_cols + TILE :, :] = jnp.zeros((TILE, depth), F32)
            load[cell_cols + TILE : cell_cols + TILE + slot_rows, :] = as_rows(fracture, depth)

    outs = [(block, F32), (block, F32), ((1, slots), F32), ((TILE, LANES), F32), ((TILE, LANES), F32)]
    outs = outs + [(load_two, F32)] * lay_pairs
    frac_source_rows = frac_source.reshape(small)
    pressure, forced, fracture, tile_two, table_all, *loads = run(
        kernel_b,
        "cycle",
        outs,
        (
            faces, basis, matrix_source, diag, scale, hot_row, hot_depth, frac_pack,
            frac_source_rows, joined_one, *blk_one, *lay_one,
        ),
        scratch=(pltpu.VMEM(block, F32), pltpu.VMEM(block, F32)),
    )
    lay_two = swap_pairs(loads[0], loads[-1], "lay")

    tile_rows = (slice(cell_cols, cell_cols + TILE), slice(0, LANES))
    frac_rows = (slice(cell_cols + TILE, cell_cols + TILE + slot_rows), slice(0, depth))

    def kernel_f(tile_ref, p_ref, *refs):
        got, (join_ref, even_ref, odd_ref) = refs[:-3], refs[-3:]
        low, high = lay_sides(got, tile_rows)
        joined = join_rows(tile_ref[...], low, high)
        join_ref[...] = joined
        even = is_even("blk")
        edges = (even * (cell_cols - 1), (1 - even) * (cell_cols - 1))
        for ref, edge in zip((even_ref, odd_ref), edges):
            for x in range(cell_rows):
                ref[x : x + 1, :] = p_ref[x, pl.ds(edge, 1), :]
            ref[cell_cols : cell_cols + TILE, :LANES] = joined
            ref[cell_cols : cell_cols + TILE, LANES:] = jnp.zeros((TILE, depth - LANES), F32)
            ref[cell_cols + TILE :, :] = got[0][cell_cols + TILE :, :]

    outs = [((TILE, LANES), F32), (load_two, F32), (load_two, F32)]
    joined_two, even_two, odd_two = run(
        kernel_f, "join_two", outs, (tile_two, pressure, *lay_two)
    )
    blk_two = swap_pairs(even_two, odd_two, "blk")
    ring = []
    if lay_size != 2:
        owners = lax.axis_size("blk") * lay_size
        ahead = [(i, i + 1) for i in range(owners - 1)]
        line = fracture.reshape(slot_rows, depth)
        ring = [
            lax.ppermute(line, ("blk", "lay"), ahead),
            lax.ppermute(line, ("blk", "lay"), [(b, a) for a, b in ahead]),
        ]

    def kernel_c(
        faces_ref, basis_ref, forced_ref, scale_ref, row_ref, depth_ref, frac_ref, low_ref,
        fsrc_ref, trans_ref, p2_ref, f_ref, joined_ref, table_ref,
        one_even, one_odd, two_even, two_odd, *refs,
    ):
        lay_first, lay_second = refs[:lay_pairs], refs[lay_pairs : 2 * lay_pairs]
        ring_refs = refs[2 * lay_pairs : -3]
        p_out, f_out, p3_ref = refs[-3:]
        low, high = blk_sides(two_even, two_odd, tile_rows)
        tile = join_lanes(joined_ref[...], low, high)
        fields = Fields(coarse_solve(tile, table_ref[...]), cell_rows, cell_cols)
        x_low, x_high, y_low, y_high = rims_of(lay_first, one_even, one_odd)
        window = (slice(0, cell_cols), slice(0, depth))
        p_left, p_right = lay_sides(lay_second, window)
        p_low, p_high = blk_sides(two_even, two_odd, window)

        for x in range(cell_rows):
            p3_ref[x] = p2_ref[x] + fields.column(x, lambda k: basis_ref[k, x])
        left_rim = p_left + fields.column(-1, x_low)
        right_rim = p_right + fields.column(cell_rows, x_high)
        low_rim = p_low + fields.row(-1, y_low)
        high_rim = p_high + fields.row(cell_cols, y_high)
        for x in range(cell_rows):
            centre = p3_ref[x]
            left = p3_ref[x - 1] if x else left_rim
            right = p3_ref[x + 1] if x + 1 < cell_rows else right_rim
            around = neighbour_sum(
                faces_ref, x, left, centre, right, low_rim[x : x + 1, :], high_rim[x : x + 1, :]
            )
            p_out[x] = (1.0 - OMEGA) * centre + scale_ref[x] * (forced_ref[x] + around)

        flat = p3_ref[...].reshape(cells, depth)
        pressure_at = gather_cells(flat, row_ref[...], depth_ref[...])
        mine = as_rows(f_ref[...], LANES)
        if ring_refs:
            before, after = ring_refs[0][...], ring_refs[1][...]
        else:
            partner = lay_second[0][frac_rows]
            from_low, from_high = blk_sides(two_even, two_odd, frac_rows)
            before = by_parity(is_even("lay"), from_low, partner)
            after = by_parity(is_even("lay"), partner, from_high)
        width = mine.shape[0]
        wide = jnp.concatenate(
            [as_rows(as_line(before), LANES), mine, as_rows(as_line(after), LANES)]
            + [jnp.zeros((-3 * width % TILE, LANES), F32)] * (3 * width % TILE > 0),
            axis=0,
        )
        peer_high = as_line(frac_ref[2:4, :])
        picked = None
        for part in split3(wide):
            product = jnp.dot(part, low_ref[...], preferred_element_type=F32)
            picked = product if picked is None else picked + product
        match = iota(picked.shape, 0).astype(F32) == peer_high
        peers = jnp.sum(jnp.where(match, picked, 0.0), axis=0, keepdims=True)
        flux = as_line(fsrc_ref[...]) + frac_ref[0:1, :] * pressure_at
        for j in range(links):
            flux = flux + trans_ref[j : j + 1, :] * peers[:, j * slots : (j + 1) * slots]
        result = (1.0 - OMEGA) * f_ref[...] + frac_ref[1:2, :] * flux
        f_out[...] = as_rows(result, LANES)

    final, frac_final = run(
        kernel_c,
        "finish",
        [(block, F32), (small, F32)],
        (
            faces, basis, forced, scale, hot_row, hot_depth, frac_pack, hot_low,
            frac_source_rows, frac_trans, pressure, fracture, joined_two, table_all,
            *blk_one, *blk_two, *lay_one, *lay_two, *ring,
        ),
        scratch=(pltpu.VMEM(block, F32),),
    )
    return final, frac_final.reshape(slots)


def solution(mesh):
    return jax.shard_map(
        local,
        mesh=mesh,
        in_specs=(
            P("lay", "blk", None),
            P("lay", "blk", None),
            P(None, "lay", "blk", None),
            P(None, "lay", "blk", None),
            P("lay", "blk"),
            P(None, "lay", "blk"),
            P(("blk", "lay")),
            P(("blk", "lay")),
            P(("blk", "lay")),
            P(None, ("blk", "lay")),
            P(("blk", "lay")),
            P(None, ("blk", "lay")),
            P(("blk", "lay")),
        ),
        out_specs=(P("lay", "blk", None), P(("blk", "lay"))),
        check_vma=False,
    )
```

time: 213 us -> 30.1 us (0.14); the launches traced: 210 us -> 29.8 us
  starting transfers between devices: 127 us -> 8.89 us
  other arithmetic: 37.9 us -> 0 us
  local copies, waits for them, and re-layouts: 32.4 us -> 5.64 us
  Pallas kernels: 0 us -> 4.16 us
    ppermute x44 -> x6, starting transfers between devices: 127 us -> 8.89 us  [the longest x2 7.12 us: swap_pairs(): got.append(lax.ppermute(odd_load, axis, odd))]
    gather x6 -> x0, local copies, waits for them, and re-layouts: 23.1 us -> none  [the longest x3 12.4 us: local(): peer_values = fracture_wide[local_peer]]
    scatter-add x4 -> x0, other arithmetic: 13.9 us -> none  [the longest x3 10.4 us: matrix_rows(): jax.ops.segment_sum(link_flux, cell_index, num_segments=pressure.size)]
    concatenate x22 -> x0, other arithmetic: 7.15 us -> none  [padded_2(): block = jnp.concatenate([low, block, high], axis=dim)]
    reduce_sum x12 -> x0, other arithmetic: 6.83 us -> none  [the longest x2 2.86 us: restrict_terms(): node_sums = jnp.sum(basis * residual[None], axis=3)]
    pallas_call x0 -> x6, Pallas kernels: none -> 4.16 us  [run(): pl.pallas_call(kernel, name=name, out_shape=[jax.ShapeDtypeStruct(shape,...]
    add x8 -> x0, other arithmetic: 3.89 us -> none  [the longest x2 2.93 us: local(): pressure = pressure + OMEGA * (matrix_source - rows_now) / matrix_diag]
    slice x22 -> x0, local copies, waits for them, and re-layouts: 3.78 us -> none  [the longest x12 3.32 us: padded_2(): lax.slice_in_dim(block, block.shape[dim] - width, None, axis=dim)]
  transfers between devices with their start and end apart: 44 -> 6, of which waited for: 8 -> 4; matrix products, arithmetic and copies ran while one was open for 24% -> 0% of each run, Pallas kernels for 0% -> 2%
where the time goes in v1:
time: 30.1 us; the launch traced here: 29.8 us
  waiting for transfers between devices  9.64 us (32%)
  starting transfers between devices  8.89 us (30%)
  local copies, waits for them, and re-layouts  5.64 us (19%)
  Pallas kernels  4.16 us (14%)
  between operations  1.48 us (5%)
    ppermute x2, waiting for transfers between devices, swap_pairs(): got.append(lax.ppermute(odd_load, axis, odd))  7.14 us
    ppermute x2, starting transfers between devices, swap_pairs(): got.append(lax.ppermute(odd_load, axis, odd))  7.12 us
    pallas_call x6, Pallas kernels, run(): pl.pallas_call(kernel, name=name, out_shape=[jax.ShapeDtypeStruct(shape,...  4.16 us
    ppermute x4, waiting for transfers between devices, swap_pairs(): got = [lax.ppermute(even_load, axis, even)]  2.5 us
    unnamed x24, local copies, waits for them, and re-layouts  2.22 us
    dynamic_update_slice x4, local copies, waits for them, and re-layouts, local(): lax.dynamic_update_slice(table, coarse_ratio[direction], (2, TILE * (2 +...  1.91 us
    ppermute x4, starting transfers between devices, swap_pairs(): got = [lax.ppermute(even_load, axis, even)]  1.77 us
    squeeze x1, local copies, waits for them, and re-layouts, local(): coarse_ratio[direction]  0.76 us
  transfers between devices with their start and end apart: 6, of which 4 were waited for; matrix products, arithmetic and copies ran while one was open for 0% of the time, Pallas kernels for 2%

profile of v1, /device:TPU:8, one launch (start us, length us, event | category | flops | bytes accessed | tf_op | source)
XLA Modules:
  0.0 29.8 jit_solution(743369658123039834)
XLA Ops:
  0.6 0.0 copy-start.6
  0.6 0.0 copy-start.8
  0.7 0.0 copy-start.9
  0.7 0.0 copy-start.10
  0.7 0.0 copy-start.11
  0.7 0.8 %slice_bitcast_fusion = (f32[4,4]{1,0:T(4,128)S(1)}, f32[4,4]{1,0:T(4,128)S(1)}, f32[4,4]{1,0:T(4,128)S(1)}, f32[4,4]{1,0:T(4,128)S(1)}) fusion(f32[4,4,4]{2,1,0:T(4,128)} %param.18), kind=kLoop, calls=%fused_computation | loop fusion | bytes 512 | tf_op jit(solution)/shard_map/squeeze | solution.py:295
  1.4 0.8 %dynamic_update_slice.15 = f32[8,128]{1,0:T(8,128)S(1)} pad(f32[4,4]{1,0:T(4,128)} %param.17, f32[]{:T(128)} %constant.6.clone.1), padding=2_2x10_114 | pad | bytes 4164 | tf_op jit(solution)/shard_map/dynamic_update_slice | solution.py:292
  2.2 0.4 %dynamic_update_slice.16 = f32[8,128]{1,0:T(8,128)S(1)} dynamic-update-slice(f32[8,128]{1,0:T(8,128)S(1)} %dynamic_update_slice.15, f32[4,4]{1,0:T(4,128)S(1)} %get-tuple-element.48, s32[]{:T(128)} %constant.0.clone.1, s32[]{:T(128)} %constant.1.clone.1) | dynamic-update-slice | bytes 132 | tf_op jit(solution)/shard_map/dynamic_update_slice | solution.py:294
  2.6 0.5 %dynamic_update_slice.17 = f32[8,128]{1,0:T(8,128)S(1)} dynamic-update-slice(f32[8,128]{1,0:T(8,128)S(1)} %dynamic_update_slice.16, f32[4,4]{1,0:T(4,128)S(1)} %get-tuple-element.47, s32[]{:T(128)} %constant.0.clone.1, s32[]{:T(128)} %constant.2.clone.1) | dynamic-update-slice | bytes 132 | tf_op jit(solution)/shard_map/dynamic_update_slice | solution.py:294
  3.1 0.5 %dynamic_update_slice.18 = f32[8,128]{1,0:T(8,128)S(1)} dynamic-update-slice(f32[8,128]{1,0:T(8,128)S(1)} %dynamic_update_slice.17, f32[4,4]{1,0:T(4,128)S(1)} %get-tuple-element.49, s32[]{:T(128)} %constant.0.clone.1, s32[]{:T(128)} %constant.3.clone.1) | dynamic-update-slice | bytes 132 | tf_op jit(solution)/shard_map/dynamic_update_slice | solution.py:294
  3.6 0.5 %dynamic_update_slice.19.table_ref = f32[8,128]{1,0:T(8,128)S(1)} dynamic-update-slice(f32[8,128]{1,0:T(8,128)S(1)} %dynamic_update_slice.18, f32[4,4]{1,0:T(4,128)S(1)} %get-tuple-element.46, s32[]{:T(128)} %constant.0.clone.1, s32[]{:T(128)} %constant.4.clone.1) | dynamic-update-slice | bytes 132 | tf_op jit(solution)/shard_map/dynamic_update_slice | solution.py:294
  4.1 0.0 copy-start
  4.1 1.2 %copy-done = f32[4,16,16,256]{3,2,1,0:T(8,128)S(1)} copy-done((f32[4,16,16,256]{3,2,1,0:T(8,128)S(1)}, f32[4,16,16,256]{3,2,1,0:T(8,128)}, u32[]{:S(2)}) %copy-start) | copy-done | bytes 1048600
  5.3 0.0 copy-start.3
  5.3 0.9 %copy-done.3 = f32[16,16,256]{2,1,0:T(8,128)S(1)} copy-done((f32[16,16,256]{2,1,0:T(8,128)S(1)}, f32[16,16,256]{2,1,0:T(8,128)}, u32[]{:S(2)}) %copy-start.3) | copy-done | bytes 262168
  6.3 0.0 copy-start.2
  6.3 0.0 copy-start.5
  6.3 0.2 restrict_source.1
  6.5 0.0 copy-start.1
  6.5 0.0 copy-start.4
  6.5 0.0 copy-start.7
  6.5 0.1 collective-permute-start
  6.6 1.3 %collective-permute-done.refs_0_ = f32[72,256]{1,0:T(8,128)S(1)} collective-permute-done((f32[72,256]{1,0:T(8,128)S(1)}, f32[72,256]{1,0:T(8,128)S(1)}, u32[]{:S(2)}, u32[]{:S(2)}) %collective-permute-start) | collective-permute-done | bytes 73760 | tf_op jit(solution)/shard_map/ppermute | solution.py:24
  7.8 0.1 join.1
  7.9 1.6 %collective-permute-start.1 = (f32[72,256]{1,0:T(8,128)S(1)}, f32[72,256]{1,0:T(8,128)S(1)}, u32[]{:S(2)}, u32[]{:S(2)}) collective-permute-start(f32[72,256]{1,0:T(8,128)S(1)} %get-tuple-element.32), channel_id=1, source_target_pairs={{0,2},{2,0},{4,6},{6,4},{8,10},{10,8},{12,14},{14,12},{16,18},{18,... | collective-permute-start | bytes 221192 | tf_op jit(solution)/shard_map/ppermute | solution.py:24
  9.5 3.3 %collective-permute-start.2 = (f32[72,256]{1,0:T(8,128)S(1)}, f32[72,256]{1,0:T(8,128)S(1)}, u32[]{:S(2)}, u32[]{:S(2)}) collective-permute-start(f32[72,256]{1,0:T(8,128)S(1)} %get-tuple-element.33), channel_id=1, source_target_pairs={{2,4},{4,2},{6,8},{8,6},{10,12},{12,10},{14,16},{16,14},{18,20},{2... | collective-permute-start | bytes 221192 | tf_op jit(solution)/shard_map/ppermute | solution.py:26
  13.4 0.0 copy-done.6
  13.4 0.0 copy-done.8
  13.4 0.0 copy-done.9
  13.4 0.0 copy-done.10
  13.4 0.0 copy-done.11
  13.4 0.0 copy-done.2
  13.4 0.0 copy-done.5
  13.5 0.6 %prepare.1 = (f32[16,16,256]{2,1,0:T(8,128)S(1)}, f32[16,16,256]{2,1,0:T(8,128)S(1)}, bf16[256,512]{1,0:T(8,128)(2,1)S(1)}, bf16[256,512]{1,0:T(8,128)(2,1)S(1)}...) custom-call(f32[6,16,16,256]{3,2,1,0:T(8,128)S(1)} %copy-done.2, f32[16,16,256]{2,1,0:T(8,128)S(1)} %copy-done.5, ...), custom_call_target="tpu_custom_call" | custom-call | tf_op jit(solution)/shard_map/prepare/pallas_call | solution.py:33
  14.0 0.0 collective-permute-done.1.blk_even.one_even
  14.1 3.4 %collective-permute-done.2.blk_odd.one_odd = f32[72,256]{1,0:T(8,128)S(1)} collective-permute-done((f32[72,256]{1,0:T(8,128)S(1)}, f32[72,256]{1,0:T(8,128)S(1)}, u32[]{:S(2)}, u32[]{:S(2)}) %collective-permute-start.2) | collective-permute-done | bytes 73760 | tf_op jit(solution)/shard_map/ppermute | solution.py:26
  17.5 0.0 copy-done.1
  17.5 0.0 copy-done.4
  17.5 0.0 copy-done.7
  17.5 1.8 %cycle.1 = (f32[16,16,256]{2,1,0:T(8,128)S(1)}, f32[16,16,256]{2,1,0:T(8,128)S(1)}, f32[1,512]{1,0:T(1,128)S(1)}, f32[8,128]{1,0:T(8,128)S(1)}, f32[8,128]{1,0:T(8,128)S(1)}, /*index=5*/f32[32,256]{1,0:T(8,128)S(1)}) custom-call(f32[6,16,16,256]{3,2,1,0:T(8,128)S(1)} %copy-done.2, f32[4,16,16,256]{3,2,1,0:T(8,128)S(1)} %copy-done.1, ...), custom_call_target="tpu_custom_call" | custom-call | tf_op jit(solution)/shard_map/cycle/pallas_call | solution.py:33
  19.3 0.1 collective-permute-start.3
  19.4 1.2 %collective-permute-done.3.refs_0_.refs_1_ = f32[32,256]{1,0:T(8,128)S(1)} collective-permute-done((f32[32,256]{1,0:T(8,128)S(1)}, f32[32,256]{1,0:T(8,128)S(1)}, u32[]{:S(2)}, u32[]{:S(2)}) %collective-permute-start.3) | collective-permute-done | bytes 32800 | tf_op jit(solution)/shard_map/ppermute | solution.py:24
  20.6 0.1 collective-permute-start.4
  20.7 3.8 %collective-permute-start.5 = (f32[32,256]{1,0:T(8,128)S(1)}, f32[32,256]{1,0:T(8,128)S(1)}, u32[]{:S(2)}, u32[]{:S(2)}) collective-permute-start(f32[32,256]{1,0:T(8,128)S(1)} %get-tuple-element.43), channel_id=1, source_target_pairs={{2,4},{4,2},{6,8},{8,6},{10,12},{12,10},{14,16},{16,14},{18,20},{2... | collective-permute-start | bytes 98312 | tf_op jit(solution)/shard_map/ppermute | solution.py:26
  24.5 0.0 collective-permute-done.4.two_even
  24.6 3.7 %collective-permute-done.5.two_odd = f32[32,256]{1,0:T(8,128)S(1)} collective-permute-done((f32[32,256]{1,0:T(8,128)S(1)}, f32[32,256]{1,0:T(8,128)S(1)}, u32[]{:S(2)}, u32[]{:S(2)}) %collective-permute-start.5) | collective-permute-done | bytes 32800 | tf_op jit(solution)/shard_map/ppermute | solution.py:26
  28.3 1.5 %finish.1 = (f32[16,16,256]{2,1,0:T(8,128)}, f32[4,128]{1,0:T(4,128)}) custom-call(f32[6,16,16,256]{3,2,1,0:T(8,128)S(1)} %copy-done.2, f32[4,16,16,256]{3,2,1,0:T(8,128)S(1)} %copy-done.1, f32[16,16,256]{2,1,0:T(8,128)S(1)} %get-tuple-element.34.forced_ref, f32[16,16,256]{2,1,0:T(8,128)S(1)} %get-tuple-element.25.scale_ref, ...), custom_call_target="tpu_custom_call" | custom-call | tf_op jit(solution)/shard_map/finish/pallas_call | solution.py:33
  (1 shorter events, 0.0 us)
Async XLA Ops:
  0.6 12.8 %copy-start.6 = (f32[2,512]{1,0:T(2,128)S(1)}, f32[2,512]{1,0:T(2,128)}, u32[]{:S(2)}) copy-start(f32[2,512]{1,0:T(2,128)} %trans_ref.3) | copy-start | bytes 12292
  0.6 12.8 %copy-start.8 = (s32[2,512]{1,0:T(2,128)S(1)}, s32[2,512]{1,0:T(2,128)}, u32[]{:S(2)}) copy-start(s32[2,512]{1,0:T(2,128)} %peer_ref.1) | copy-start | bytes 12292
  0.7 12.8 %copy-start.9 = (s32[512]{0:T(512)S(1)}, s32[512]{0:T(512)}, u32[]{:S(2)}) copy-start(s32[512]{0:T(512)} %param.23) | copy-start | bytes 6148
  0.7 12.8 %copy-start.10 = (f32[512]{0:T(512)S(1)}, f32[512]{0:T(512)}, u32[]{:S(2)}) copy-start(f32[512]{0:T(512)} %param.21) | copy-start | bytes 6148
  0.7 12.8 %copy-start.11 = (f32[512]{0:T(512)S(1)}, f32[512]{0:T(512)}, u32[]{:S(2)}) copy-start(f32[512]{0:T(512)} %param.20) | copy-start | bytes 6148
  4.1 1.2 %copy-start = (f32[4,16,16,256]{3,2,1,0:T(8,128)S(1)}, f32[4,16,16,256]{3,2,1,0:T(8,128)}, u32[]{:S(2)}) copy-start(f32[4,16,16,256]{3,2,1,0:T(8,128)} %basis_ref.7) | copy-start | bytes 3145732
  5.3 0.9 %copy-start.3 = (f32[16,16,256]{2,1,0:T(8,128)S(1)}, f32[16,16,256]{2,1,0:T(8,128)}, u32[]{:S(2)}) copy-start(f32[16,16,256]{2,1,0:T(8,128)} %source_ref.3) | copy-start | bytes 786436
  6.3 7.1 %copy-start.2 = (f32[6,16,16,256]{3,2,1,0:T(8,128)S(1)}, f32[6,16,16,256]{3,2,1,0:T(8,128)}, u32[]{:S(2)}) copy-start(f32[6,16,16,256]{3,2,1,0:T(8,128)} %faces_ref.5) | copy-start | bytes 4718596
  6.3 7.2 %copy-start.5 = (f32[16,16,256]{2,1,0:T(8,128)S(1)}, f32[16,16,256]{2,1,0:T(8,128)}, u32[]{:S(2)}) copy-start(f32[16,16,256]{2,1,0:T(8,128)} %accum_ref.1) | copy-start | bytes 786436
  6.5 11.0 %copy-start.1 = (f32[4,16,16,256]{3,2,1,0:T(8,128)S(1)}, f32[4,16,16,256]{3,2,1,0:T(8,128)}, u32[]{:S(2)}) copy-start(f32[4,16,16,256]{3,2,1,0:T(8,128)} %basis_ref.7) | copy-start | bytes 3145732
  6.5 11.0 %copy-start.4 = (f32[16,16,256]{2,1,0:T(8,128)S(1)}, f32[16,16,256]{2,1,0:T(8,128)}, u32[]{:S(2)}) copy-start(f32[16,16,256]{2,1,0:T(8,128)} %source_ref.3) | copy-start | bytes 786436
  6.5 11.0 %copy-start.7 = (f32[512]{0:T(512)S(1)}, f32[512]{0:T(512)}, u32[]{:S(2)}) copy-start(f32[512]{0:T(512)} %param.19) | copy-start | bytes 6148
  6.5 1.3 %collective-permute-start = (f32[72,256]{1,0:T(8,128)S(1)}, f32[72,256]{1,0:T(8,128)S(1)}, u32[]{:S(2)}, u32[]{:S(2)}) collective-permute-start(f32[72,256]{1,0:T(8,128)S(1)} %get-tuple-element.30), channel_id=1, source_target_pairs={{0,1},{1,0},{2,3},{3,2},{4,5},{5,4},{6,7},{7,6},{8,9},{9,8},{10,11... | collective-permute-start | bytes 221192 | tf_op jit(solution)/shard_map/ppermute | solution.py:24
  7.9 6.1 %collective-permute-start.1 = (f32[72,256]{1,0:T(8,128)S(1)}, f32[72,256]{1,0:T(8,128)S(1)}, u32[]{:S(2)}, u32[]{:S(2)}) collective-permute-start(f32[72,256]{1,0:T(8,128)S(1)} %get-tuple-element.32), channel_id=1, source_target_pairs={{0,2},{2,0},{4,6},{6,4},{8,10},{10,8},{12,14},{14,12},{16,18},{18,... | collective-permute-start | bytes 221192 | tf_op jit(solution)/shard_map/ppermute | solution.py:24
  9.5 8.0 %collective-permute-start.2 = (f32[72,256]{1,0:T(8,128)S(1)}, f32[72,256]{1,0:T(8,128)S(1)}, u32[]{:S(2)}, u32[]{:S(2)}) collective-permute-start(f32[72,256]{1,0:T(8,128)S(1)} %get-tuple-element.33), channel_id=1, source_target_pairs={{2,4},{4,2},{6,8},{8,6},{10,12},{12,10},{14,16},{16,14},{18,20},{2... | collective-permute-start | bytes 221192 | tf_op jit(solution)/shard_map/ppermute | solution.py:26
  19.3 1.3 %collective-permute-start.3 = (f32[32,256]{1,0:T(8,128)S(1)}, f32[32,256]{1,0:T(8,128)S(1)}, u32[]{:S(2)}, u32[]{:S(2)}) collective-permute-start(f32[32,256]{1,0:T(8,128)S(1)} %get-tuple-element.39), channel_id=1, source_target_pairs={{0,1},{1,0},{2,3},{3,2},{4,5},{5,4},{6,7},{7,6},{8,9},{9,8},{10,11... | collective-permute-start | bytes 98312 | tf_op jit(solution)/shard_map/ppermute | solution.py:24
  20.6 4.0 %collective-permute-start.4 = (f32[32,256]{1,0:T(8,128)S(1)}, f32[32,256]{1,0:T(8,128)S(1)}, u32[]{:S(2)}, u32[]{:S(2)}) collective-permute-start(f32[32,256]{1,0:T(8,128)S(1)} %get-tuple-element.42), channel_id=1, source_target_pairs={{0,2},{2,0},{4,6},{6,4},{8,10},{10,8},{12,14},{14,12},{16,18},{18,... | collective-permute-start | bytes 98312 | tf_op jit(solution)/shard_map/ppermute | solution.py:24
  20.7 7.6 %collective-permute-start.5 = (f32[32,256]{1,0:T(8,128)S(1)}, f32[32,256]{1,0:T(8,128)S(1)}, u32[]{:S(2)}, u32[]{:S(2)}) collective-permute-start(f32[32,256]{1,0:T(8,128)S(1)} %get-tuple-element.43), channel_id=1, source_target_pairs={{2,4},{4,2},{6,8},{8,6},{10,12},{12,10},{14,16},{16,14},{18,20},{2... | collective-permute-start | bytes 98312 | tf_op jit(solution)/shard_map/ppermute | solution.py:26

commit v2 on v1

--- a/solution.py
+++ b/solution.py
@@ -27,15 +27,19 @@
     return got
 
 
-def run(kernel, name, outs, args, scratch=(), smem=()):
+def run(kernel, outs, args, scratch=(), smem=(), in_place=(), out_place=()):
     spec = pl.BlockSpec(memory_space=pltpu.VMEM)
     scalar = pl.BlockSpec(memory_space=pltpu.SMEM)
+    there = pl.BlockSpec(memory_space=pltpu.HBM)
+
+    def place(i):
+        return scalar if i in smem else there if i in in_place else spec
+
     return pl.pallas_call(
         kernel,
-        name=name,
         out_shape=[jax.ShapeDtypeStruct(shape, dtype) for shape, dtype in outs],
-        in_specs=[scalar if i in smem else spec for i in range(len(args))],
-        out_specs=[spec] * len(outs),
+        in_specs=[place(i) for i in range(len(args))],
+        out_specs=[there if i in out_place else spec for i in range(len(outs))],
         scratch_shapes=list(scratch),
         compiler_params=pltpu.CompilerParams(vmem_limit_bytes=24 << 20),
     )(*args)
@@ -248,6 +252,26 @@
     return total
 
 
+def nodes_at_slots(second, hot_node, node_weight):
+    picked = None
+    for part in split3(second):
+        product = jnp.dot(part, hot_node, preferred_element_type=F32)
+        picked = product if picked is None else picked + product
+    total = jnp.sum(picked * node_weight, axis=0, keepdims=True)
+    half = total.shape[1] // 2
+    return total[:, :half] + total[:, half:]
+
+
+def slots_at_nodes(values, hot_node, node_weight):
+    total = None
+    for part in split3(node_weight * jnp.concatenate([values, values], axis=1)):
+        product = lax.dot_general(
+            part, hot_node, (((1,), (1,)), ((), ())), preferred_element_type=F32
+        )
+        total = product if total is None else total + product
+    return total
+
+
 def as_line(value):
     return jnp.concatenate([value[i : i + 1, :] for i in range(value.shape[0])], axis=1)
 
@@ -288,26 +312,59 @@
     load_two = (cell_cols + 2 * TILE, depth)
     block = matrix_source.shape
 
-    table = jnp.zeros((TILE, LANES), F32)
-    table = lax.dynamic_update_slice(table, coarse_diag, (2, TILE + 2))
-    for direction in range(4):
-        table = lax.dynamic_update_slice(
-            table, coarse_ratio[direction], (2, TILE * (2 + direction) + 2)
-        )
-
     def is_even(axis):
         return 1 - jnp.bitwise_and(lax.axis_index(axis), 1)
 
-    def lay_got(refs):
-        got = [ref for ref in refs]
-        return got if len(got) == 2 else [got[0], None]
-
-    def kernel_a(basis_ref, source_ref, table_ref, tile_ref, *loads):
+    piece = BLOCK
+    pieces = cell_rows // piece
+
+    def kernel_a(basis_hbm, source_hbm, cdiag_hbm, ratio_hbm, basis_ref, source_ref, tile_ref, *refs):
+        loads, (cdiag_ref, ratio_ref, sems, small_sems) = refs[:-4], refs[-4:]
+        copies = []
+        for i in range(pieces):
+            part = pl.ds(i * piece, piece)
+            copies.append(
+                (
+                    pltpu.make_async_copy(source_hbm.at[part], source_ref.at[part], sems.at[0, i]),
+                    pltpu.make_async_copy(
+                        basis_hbm.at[:, part], basis_ref.at[:, part], sems.at[1, i]
+                    ),
+                )
+            )
+        small_copies = [
+            pltpu.make_async_copy(cdiag_hbm, cdiag_ref, small_sems.at[0]),
+            pltpu.make_async_copy(ratio_hbm, ratio_ref, small_sems.at[1]),
+        ]
+        for pair in copies + [small_copies]:
+            for copy in pair:
+                copy.start()
+
+        def widen(value):
+            lines = jnp.concatenate(
+                [
+                    jnp.zeros((node_rows, 2), F32),
+                    value,
+                    jnp.zeros((node_rows, TILE - 2 - node_cols), F32),
+                ],
+                axis=1,
+            )
+            edge = jnp.zeros((2, TILE), F32)
+            return jnp.concatenate([edge, lines, edge], axis=0)
+
         def column(x):
+            if x % piece == 0:
+                for copy in copies[x // piece]:
+                    copy.wait()
             return x, source_ref[x], lambda k: basis_ref[k, x]
 
-        tile = restrict_tile([column(x) for x in range(cell_rows)], [], cell_rows, cell_cols)
-        tile = tile + table_ref[...]
+        tile = restrict_tile((column(x) for x in range(cell_rows)), [], cell_rows, cell_cols)
+        for copy in small_copies:
+            copy.wait()
+        parts = [jnp.zeros((TILE, TILE), F32), widen(cdiag_ref[...])]
+        parts = parts + [widen(ratio_ref[d]) for d in range(4)]
+        parts.append(jnp.zeros((TILE, LANES - TILE * len(parts)), F32))
+        table = jnp.concatenate(parts, axis=1)
+        tile = tile + table
         tile_ref[...] = tile
         even = is_even("lay")
         edges = (even * (cell_rows - 1), (1 - even) * (cell_rows - 1))
@@ -317,8 +374,22 @@
             load[layer_rows:, :LANES] = tile
             load[layer_rows:, LANES:] = jnp.zeros((TILE, depth - LANES), F32)
 
-    outs = [((TILE, LANES), F32)] + [(load_one, F32)] * lay_pairs
-    tile_own, *loads = run(kernel_a, "restrict_source", outs, (basis, matrix_source, table))
+    outs = [(basis.shape, F32), (block, F32), ((TILE, LANES), F32)] + [(load_one, F32)] * lay_pairs
+    basis, matrix_source, tile_own, *loads = run(
+        kernel_a,
+        outs,
+        [
+            pltpu.with_memory_space_constraint(value, pltpu.HBM)
+            for value in (basis, matrix_source, coarse_diag, coarse_ratio)
+        ],
+        scratch=(
+            pltpu.VMEM(coarse_diag.shape, F32),
+            pltpu.VMEM(coarse_ratio.shape, F32),
+            pltpu.SemaphoreType.DMA((2, pieces)),
+            pltpu.SemaphoreType.DMA((2,)),
+        ),
+        in_place=(0, 1, 2, 3),
+    )
     lay_one = swap_pairs(loads[0], loads[-1], "lay")
 
     def lay_sides(refs, window):
@@ -346,12 +417,12 @@
             ref[layer_rows:, LANES:] = jnp.zeros((TILE, depth - LANES), F32)
 
     outs = [((TILE, LANES), F32), (load_one, F32), (load_one, F32)]
-    joined_one, even_one, odd_one = run(kernel_e, "join", outs, (tile_own, basis, *lay_one))
+    joined_one, even_one, odd_one = run(kernel_e, outs, (tile_own, basis, *lay_one))
     blk_one = swap_pairs(even_one, odd_one, "blk")
 
     def kernel_p(
-        faces_ref, accum_ref, cell_ref, link_ref, facc_ref, trans_ref, peer_ref, count_ref,
-        diag_ref, scale_ref, row_ref, depth_ref, frac_ref, low_ref,
+        faces_ref, accum_ref, basis_ref, cell_ref, link_ref, facc_ref, trans_ref, peer_ref,
+        count_ref, diag_ref, scale_ref, row_ref, depth_ref, frac_ref, low_ref, node_ref, weight_ref,
     ):
         slot = iota((1, slots), 1)
         live = (slot < count_ref[0]).astype(F32)
@@ -376,6 +447,21 @@
             diag = diag + linked[x * cell_cols : (x + 1) * cell_cols, :]
             diag_ref[x] = diag
             scale_ref[x] = OMEGA / diag
+        across = lax.shift_right_logical(at_row, cell_cols.bit_length() - 1)
+        along = jnp.bitwise_and(at_row, cell_cols - 1)
+        line = iota((TILE, slots), 0)
+        lane = iota((LANES, slots), 0)
+        near = (own_nodes(across) + 2 == line, side_nodes(across) + 2 == line)
+        for j, nodes in enumerate((own_nodes(along), side_nodes(along))):
+            node_ref[:, j * slots : (j + 1) * slots] = (
+                (lane == nodes + 2).astype(F32).astype(BF16)
+            )
+            total = None
+            for i in range(2):
+                flat = basis_ref[2 * j + i].reshape(cells, depth)
+                part = jnp.where(near[i], gather_cells(flat, hot_row, hot_depth), 0.0)
+                total = part if total is None else total + part
+            weight_ref[:, j * slots : (j + 1) * slots] = total
         owner = lax.axis_index("blk") * lay_size + lax.axis_index("lay")
         peer = peer_ref[...] - (owner - 1) * slots
         peer = jnp.concatenate([peer[j : j + 1, :] for j in range(peer.shape[0])], axis=1)
@@ -394,15 +480,17 @@
         ((depth, slots), BF16),
         ((TILE, slots), F32),
         ((LANES, links * slots), BF16),
+        ((LANES, 2 * slots), BF16),
+        ((TILE, 2 * slots), F32),
     ]
     small = (slots // LANES, LANES)
-    diag, scale, hot_row, hot_depth, frac_pack, hot_low = run(
+    diag, scale, hot_row, hot_depth, frac_pack, hot_low, hot_node, node_weight = run(
         kernel_p,
-        "prepare",
         outs,
         (
             faces,
             accum,
+            basis,
             frac_cell.reshape(small),
             frac_link.reshape(small),
             frac_accum.reshape(small),
@@ -410,7 +498,7 @@
             frac_peer,
             frac_count,
         ),
-        smem=(7,),
+        smem=(8,),
     )
 
     layer = (slice(0, layer_rows), slice(0, depth))
@@ -425,18 +513,19 @@
         return pick(lay_low), pick(lay_high), pick(blk_low), pick(blk_high)
 
     def kernel_b(
-        faces_ref, basis_ref, source_ref, diag_ref, scale_ref, row_ref, depth_ref, frac_ref,
+        faces_ref, basis_ref, source_ref, diag_ref, scale_ref, node_ref, weight_ref, frac_ref,
         fsrc_ref, joined_ref, blk_even, blk_odd, *refs,
     ):
         lay_refs = refs[:lay_pairs]
-        p2_ref, right_ref, f_ref, tile_ref, second_ref = refs[lay_pairs : lay_pairs + 5]
-        loads = refs[lay_pairs + 5 : -2]
-        p1_ref, link_ref = refs[-2:]
+        p2_ref, f_ref, tile_ref, second_ref = refs[lay_pairs : lay_pairs + 4]
+        loads = refs[lay_pairs + 4 : -1]
+        p1_ref = refs[-1]
         at_tile = (slice(layer_rows, layer_rows + TILE), slice(0, LANES))
         low, high = blk_sides(blk_even, blk_odd, at_tile)
         table = join_lanes(joined_ref[...], low, high)
         second_ref[...] = table
-        fields = Fields(coarse_solve(table, table), cell_rows, cell_cols)
+        second = coarse_solve(table, table)
+        fields = Fields(second, cell_rows, cell_cols)
         x_low, x_high, y_low, y_high = rims_of(lay_refs, blk_even, blk_odd)
 
         def weight(x):
@@ -449,13 +538,11 @@
         low_rim = fields.row(-1, y_low)
         high_rim = fields.row(cell_cols, y_high)
 
-        flat = p1_ref[...].reshape(cells, depth)
-        pressure_at = gather_cells(flat, row_ref[...], depth_ref[...])
         couple = frac_ref[0:1, :]
+        pressure_at = nodes_at_slots(second, node_ref[...], weight_ref[...])
         fracture = frac_ref[1:2, :] * (as_line(fsrc_ref[...]) + couple * pressure_at)
         f_ref[...] = fracture
-        linked = scatter_cells(couple * fracture, row_ref[...], depth_ref[...])
-        link_ref[...] = linked.reshape(block)
+        linked = slots_at_nodes(couple * fracture, node_ref[...], weight_ref[...])
 
         for x in range(cell_rows):
             centre = p1_ref[x]
@@ -470,12 +557,10 @@
         low_lines, high_lines = [], []
         for x in range(cell_rows):
             centre = p2_ref[x]
-            forced = source_ref[x] + link_ref[x]
-            right_ref[x] = forced
             left = p2_ref[x - 1] if x else None
             right = p2_ref[x + 1] if x + 1 < cell_rows else None
             around = neighbour_sum(faces_ref, x, left, centre, right, None, None)
-            columns.append((x, forced - diag_ref[x] * centre + around, weight(x)))
+            columns.append((x, source_ref[x] - diag_ref[x] * centre + around, weight(x)))
             low_lines.append(faces_ref[3, x, 0:1, :] * p2_ref[x, 0:1, :])
             high_lines.append(
                 faces_ref[2, x, cell_cols - 1 : cell_cols, :]
@@ -488,7 +573,7 @@
             (-1, jnp.concatenate(low_lines, axis=0), y_low),
             (cell_cols, jnp.concatenate(high_lines, axis=0), y_high),
         ]
-        tile = restrict_tile(columns, rows, cell_rows, cell_cols)
+        tile = restrict_tile(columns, rows, cell_rows, cell_cols) + linked
         tile_ref[...] = tile
         even = is_even("lay")
         edges = (even * (cell_rows - 1), (1 - even) * (cell_rows - 1))
@@ -499,18 +584,17 @@
             load[cell_cols + TILE :, :] = jnp.zeros((TILE, depth), F32)
             load[cell_cols + TILE : cell_cols + TILE + slot_rows, :] = as_rows(fracture, depth)
 
-    outs = [(block, F32), (block, F32), ((1, slots), F32), ((TILE, LANES), F32), ((TILE, LANES), F32)]
+    outs = [(block, F32), ((1, slots), F32), ((TILE, LANES), F32), ((TILE, LANES), F32)]
     outs = outs + [(load_two, F32)] * lay_pairs
     frac_source_rows = frac_source.reshape(small)
-    pressure, forced, fracture, tile_two, table_all, *loads = run(
+    pressure, fracture, tile_two, second_one, *loads = run(
         kernel_b,
-        "cycle",
         outs,
         (
-            faces, basis, matrix_source, diag, scale, hot_row, hot_depth, frac_pack,
+            faces, basis, matrix_source, diag, scale, hot_node, node_weight, frac_pack,
             frac_source_rows, joined_one, *blk_one, *lay_one,
         ),
-        scratch=(pltpu.VMEM(block, F32), pltpu.VMEM(block, F32)),
+        scratch=(pltpu.VMEM(block, F32),),
     )
     lay_two = swap_pairs(loads[0], loads[-1], "lay")
 
@@ -532,10 +616,21 @@
             ref[cell_cols + TILE :, :] = got[0][cell_cols + TILE :, :]
 
     outs = [((TILE, LANES), F32), (load_two, F32), (load_two, F32)]
-    joined_two, even_two, odd_two = run(
-        kernel_f, "join_two", outs, (tile_two, pressure, *lay_two)
-    )
+    joined_two, even_two, odd_two = run(kernel_f, outs, (tile_two, pressure, *lay_two))
     blk_two = swap_pairs(even_two, odd_two, "blk")
+
+    def kernel_m(source_ref, p2_ref, f_ref, row_ref, depth_ref, frac_ref, forced_ref, at_ref):
+        hot_row, hot_depth = row_ref[...], depth_ref[...]
+        linked = scatter_cells(frac_ref[0:1, :] * f_ref[...], hot_row, hot_depth)
+        for x in range(cell_rows):
+            forced_ref[x] = source_ref[x] + linked[x * cell_cols : (x + 1) * cell_cols, :]
+        at_ref[...] = gather_cells(p2_ref[...].reshape(cells, depth), hot_row, hot_depth)
+
+    forced, slot_pressure = run(
+        kernel_m,
+        [(block, F32), ((1, slots), F32)],
+        (matrix_source, pressure, fracture, hot_row, hot_depth, frac_pack),
+    )
     ring = []
     if lay_size != 2:
         owners = lax.axis_size("blk") * lay_size
@@ -547,16 +642,17 @@
         ]
 
     def kernel_c(
-        faces_ref, basis_ref, forced_ref, scale_ref, row_ref, depth_ref, frac_ref, low_ref,
-        fsrc_ref, trans_ref, p2_ref, f_ref, joined_ref, table_ref,
+        faces_ref, basis_ref, forced_ref, scale_ref, node_ref, weight_ref, frac_ref, low_ref,
+        fsrc_ref, trans_ref, p2_ref, f_ref, at_ref, joined_ref, table_ref,
         one_even, one_odd, two_even, two_odd, *refs,
     ):
         lay_first, lay_second = refs[:lay_pairs], refs[lay_pairs : 2 * lay_pairs]
-        ring_refs = refs[2 * lay_pairs : -3]
-        p_out, f_out, p3_ref = refs[-3:]
+        ring_refs = refs[2 * lay_pairs : -6]
+        p_hbm, f_hbm, p3_ref, p_out, f_out, sems = refs[-6:]
         low, high = blk_sides(two_even, two_odd, tile_rows)
         tile = join_lanes(joined_ref[...], low, high)
-        fields = Fields(coarse_solve(tile, table_ref[...]), cell_rows, cell_cols)
+        second = coarse_solve(tile, table_ref[...])
+        fields = Fields(second, cell_rows, cell_cols)
         x_low, x_high, y_low, y_high = rims_of(lay_first, one_even, one_odd)
         window = (slice(0, cell_cols), slice(0, depth))
         p_left, p_right = lay_sides(lay_second, window)
@@ -568,17 +664,7 @@
         right_rim = p_right + fields.column(cell_rows, x_high)
         low_rim = p_low + fields.row(-1, y_low)
         high_rim = p_high + fields.row(cell_cols, y_high)
-        for x in range(cell_rows):
-            centre = p3_ref[x]
-            left = p3_ref[x - 1] if x else left_rim
-            right = p3_ref[x + 1] if x + 1 < cell_rows else right_rim
-            around = neighbour_sum(
-                faces_ref, x, left, centre, right, low_rim[x : x + 1, :], high_rim[x : x + 1, :]
-            )
-            p_out[x] = (1.0 - OMEGA) * centre + scale_ref[x] * (forced_ref[x] + around)
-
-        flat = p3_ref[...].reshape(cells, depth)
-        pressure_at = gather_cells(flat, row_ref[...], depth_ref[...])
+        pressure_at = at_ref[...] + nodes_at_slots(second, node_ref[...], weight_ref[...])
         mine = as_rows(f_ref[...], LANES)
         if ring_refs:
             before, after = ring_refs[0][...], ring_refs[1][...]
@@ -605,17 +691,42 @@
             flux = flux + trans_ref[j : j + 1, :] * peers[:, j * slots : (j + 1) * slots]
         result = (1.0 - OMEGA) * f_ref[...] + frac_ref[1:2, :] * flux
         f_out[...] = as_rows(result, LANES)
+        copies = []
+        for x in range(cell_rows):
+            centre = p3_ref[x]
+            left = p3_ref[x - 1] if x else left_rim
+            right = p3_ref[x + 1] if x + 1 < cell_rows else right_rim
+            around = neighbour_sum(
+                faces_ref, x, left, centre, right, low_rim[x : x + 1, :], high_rim[x : x + 1, :]
+            )
+            p_out[x] = (1.0 - OMEGA) * centre + scale_ref[x] * (forced_ref[x] + around)
+            if (x + 1) % piece == 0:
+                part = pl.ds(x + 1 - piece, piece)
+                copies.append(
+                    pltpu.make_async_copy(p_out.at[part], p_hbm.at[part], sems.at[x // piece])
+                )
+                copies[-1].start()
+                if x + 1 == 2 * piece:
+                    copies.append(pltpu.make_async_copy(f_out, f_hbm, sems.at[pieces]))
+                    copies[-1].start()
+        for copy in copies:
+            copy.wait()
 
     final, frac_final = run(
         kernel_c,
-        "finish",
         [(block, F32), (small, F32)],
         (
-            faces, basis, forced, scale, hot_row, hot_depth, frac_pack, hot_low,
-            frac_source_rows, frac_trans, pressure, fracture, joined_two, table_all,
+            faces, basis, forced, scale, hot_node, node_weight, frac_pack, hot_low,
+            frac_source_rows, frac_trans, pressure, fracture, slot_pressure, joined_two, second_one,
             *blk_one, *blk_two, *lay_one, *lay_two, *ring,
         ),
-        scratch=(pltpu.VMEM(block, F32),),
+        scratch=(
+            pltpu.VMEM(block, F32),
+            pltpu.VMEM(block, F32),
+            pltpu.VMEM(small, F32),
+            pltpu.SemaphoreType.DMA((pieces + 1,)),
+        ),
+        out_place=(0, 1),
     )
     return final, frac_final.reshape(slots)
 

time: 30.1 us -> 25.3 us (0.84)
  local copies, waits for them, and re-layouts: 5.64 us -> 0.04 us
  Pallas kernels: 4.16 us -> 6.62 us
  waiting for transfers between devices: 9.64 us -> 8.06 us
    dynamic_update_slice x5 -> x0, local copies, waits for them, and re-layouts: 2.66 us -> none  [the longest x4 1.91 us: local(): lax.dynamic_update_slice(table, coarse_ratio[direction], (2, TILE * (2 +...]
    pallas_call x6 -> x7, Pallas kernels: 4.16 us -> 6.62 us  [run(): pl.pallas_call(kernel, out_shape=[jax.ShapeDtypeStruct(shape, dtype) for...]
    unnamed x24 -> x16, local copies, waits for them, and re-layouts: 2.22 us -> 0.04 us
    ppermute x2, waiting for transfers between devices: 7.14 us -> 5.6 us  [swap_pairs(): got.append(lax.ppermute(odd_load, axis, odd))]
    squeeze x1 -> x0, local copies, waits for them, and re-layouts: 0.76 us -> none  [local(): coarse_ratio[direction]]
  transfers between devices with their start and end apart: 6 -> 6, of which waited for: 4 -> 4; matrix products, arithmetic and copies ran while one was open for 0% -> 0% of each run, Pallas kernels for 2% -> 9%
where the time goes in v2:
time: 25.3 us; the launch traced here: 25.1 us
  starting transfers between devices  8.89 us (35%)
  waiting for transfers between devices  8.06 us (32%)
  Pallas kernels  6.62 us (26%)
  between operations  1.49 us (6%)
    ppermute x2, starting transfers between devices, swap_pairs(): got.append(lax.ppermute(odd_load, axis, odd))  7.12 us
    pallas_call x7, Pallas kernels, run(): pl.pallas_call(kernel, out_shape=[jax.ShapeDtypeStruct(shape, dtype) for...  6.62 us
    ppermute x2, waiting for transfers between devices, swap_pairs(): got.append(lax.ppermute(odd_load, axis, odd))  5.6 us
    ppermute x4, waiting for transfers between devices, swap_pairs(): got = [lax.ppermute(even_load, axis, even)]  2.45 us
    ppermute x4, starting transfers between devices, swap_pairs(): got = [lax.ppermute(even_load, axis, even)]  1.77 us
  transfers between devices with their start and end apart: 6, of which 4 were waited for; matrix products, arithmetic and copies ran while one was open for 0% of the time, Pallas kernels for 9%

profile of v2, /device:TPU:8, one launch (start us, length us, event | category | flops | bytes accessed | tf_op | source)
XLA Modules:
  0.0 25.1 jit_solution(18080390006370304376)
XLA Ops:
  0.6 0.0 copy-start
  0.6 0.0 copy-start.2
  0.7 0.0 copy-start.4
  0.7 0.0 copy-start.5
  0.7 0.0 copy-start.6
  0.7 0.0 copy-start.7
  0.7 0.0 copy-start.1
  0.7 1.8 %shard_map.140 = (f32[4,16,16,256]{3,2,1,0:T(8,128)S(1)}, f32[16,16,256]{2,1,0:T(8,128)S(1)}, f32[8,128]{1,0:T(8,128)S(1)}, f32[72,256]{1,0:T(8,128)S(1)}) custom-call(f32[4,16,16,256]{3,2,1,0:T(8,128)} %basis_hbm.1, f32[16,16,256]{2,1,0:T(8,128)} %source_hbm.1, f32[4,4]{1,0:T(4,128)} %cdiag_hbm.1, f32[4,4,4]{2,1,0:T(4,128)} %ratio_hbm.1), custom_call_target="tpu_custom_call" | custom-call | tf_op jit(solution)/shard_map/pallas_call | solution.py:38
  2.5 0.1 collective-permute-start
  2.5 1.3 %collective-permute-done.refs_0_ = f32[72,256]{1,0:T(8,128)S(1)} collective-permute-done((f32[72,256]{1,0:T(8,128)S(1)}, f32[72,256]{1,0:T(8,128)S(1)}, u32[]{:S(2)}, u32[]{:S(2)}) %collective-permute-start) | collective-permute-done | bytes 73760 | tf_op jit(solution)/shard_map/ppermute | solution.py:24
  3.8 0.1 shard_map.142
  3.9 0.0 copy-start.3
  3.9 1.6 %collective-permute-start.1 = (f32[72,256]{1,0:T(8,128)S(1)}, f32[72,256]{1,0:T(8,128)S(1)}, u32[]{:S(2)}, u32[]{:S(2)}) collective-permute-start(f32[72,256]{1,0:T(8,128)S(1)} %get-tuple-element.39), channel_id=1, source_target_pairs={{0,2},{2,0},{4,6},{6,4},{8,10},{10,8},{12,14},{14,12},{16,18},{18,... | collective-permute-start | bytes 221192 | tf_op jit(solution)/shard_map/ppermute | solution.py:24
  5.5 3.3 %collective-permute-start.2 = (f32[72,256]{1,0:T(8,128)S(1)}, f32[72,256]{1,0:T(8,128)S(1)}, u32[]{:S(2)}, u32[]{:S(2)}) collective-permute-start(f32[72,256]{1,0:T(8,128)S(1)} %get-tuple-element.40), channel_id=1, source_target_pairs={{2,4},{4,2},{6,8},{8,6},{10,12},{12,10},{14,16},{16,14},{18,20},{2... | collective-permute-start | bytes 221192 | tf_op jit(solution)/shard_map/ppermute | solution.py:26
  9.4 0.0 copy-done
  9.4 0.0 copy-done.2
  9.4 0.0 copy-done.4
  9.4 0.0 copy-done.5
  9.4 0.0 copy-done.6
  9.4 0.0 copy-done.7
  9.4 0.0 copy-done.1
  9.4 1.5 %shard_map.141 = (f32[16,16,256]{2,1,0:T(8,128)S(1)}, f32[16,16,256]{2,1,0:T(8,128)S(1)}, bf16[256,512]{1,0:T(8,128)(2,1)S(1)}, bf16[256,512]{1,0:T(8,128)(2,1)S...) custom-call(f32[6,16,16,256]{3,2,1,0:T(8,128)S(1)} %copy-done, ...), custom_call_target="tpu_custom_call" | custom-call | tf_op jit(solution)/shard_map/pallas_call | solution.py:38
  11.0 0.0 collective-permute-done.1.blk_even.one_even
  11.0 2.5 %collective-permute-done.2.blk_odd.one_odd = f32[72,256]{1,0:T(8,128)S(1)} collective-permute-done((f32[72,256]{1,0:T(8,128)S(1)}, f32[72,256]{1,0:T(8,128)S(1)}, u32[]{:S(2)}, u32[]{:S(2)}) %collective-permute-start.2) | collective-permute-done | bytes 73760 | tf_op jit(solution)/shard_map/ppermute | solution.py:26
  13.5 0.0 copy-done.3
  13.5 1.2 %shard_map.143 = (f32[16,16,256]{2,1,0:T(8,128)S(1)}, f32[1,512]{1,0:T(1,128)S(1)}, f32[8,128]{1,0:T(8,128)S(1)}, f32[8,128]{1,0:T(8,128)S(1)}, f32[32,256]{1,0:T(8,128)S(1)}) custom-call(f32[6,16,16,256]{3,2,1,0:T(8,128)S(1)} %copy-done, f32[4,16,16,256]{3,2,1,0:T(8,128)S(1)} %get-tuple-element.29.basis_ref, ...), custom_call_target="tpu_custom_call" | custom-call | tf_op jit(solution)/shard_map/pallas_call | solution.py:38
  14.7 0.1 collective-permute-start.3
  14.8 1.2 %collective-permute-done.3.refs_0_.refs_1_ = f32[32,256]{1,0:T(8,128)S(1)} collective-permute-done((f32[32,256]{1,0:T(8,128)S(1)}, f32[32,256]{1,0:T(8,128)S(1)}, u32[]{:S(2)}, u32[]{:S(2)}) %collective-permute-start.3) | collective-permute-done | bytes 32800 | tf_op jit(solution)/shard_map/ppermute | solution.py:24
  16.0 0.1 collective-permute-start.4
  16.1 3.9 %collective-permute-start.5 = (f32[32,256]{1,0:T(8,128)S(1)}, f32[32,256]{1,0:T(8,128)S(1)}, u32[]{:S(2)}, u32[]{:S(2)}) collective-permute-start(f32[32,256]{1,0:T(8,128)S(1)} %get-tuple-element.53), channel_id=1, source_target_pairs={{2,4},{4,2},{6,8},{8,6},{10,12},{12,10},{14,16},{16,14},{18,20},{2... | collective-permute-start | bytes 98312 | tf_op jit(solution)/shard_map/ppermute | solution.py:26
  20.0 0.6 %shard_map.144 = (f32[16,16,256]{2,1,0:T(8,128)S(1)}, f32[1,512]{1,0:T(1,128)S(1)}) custom-call(f32[16,16,256]{2,1,0:T(8,128)S(1)} %get-tuple-element.30.source_ref, f32[16,16,256]{2,1,0:T(8,128)S(1)} %get-tuple-element.41.p2_ref.p_ref, f32[1,512]{1,0:T(1,128)S(1)} %get-tuple-element.42.f_ref, bf16[256,512]{1,0:T(8,128)(2,1)S(1)} %get-tuple-element.43.row_ref, ...), custom_call_target="tpu_custom_call" | custom-call | tf_op jit(solution)/shard_map/pallas_call | solution.py:38
  20.6 0.0 collective-permute-done.4.two_even
  20.6 3.1 %collective-permute-done.5.two_odd = f32[32,256]{1,0:T(8,128)S(1)} collective-permute-done((f32[32,256]{1,0:T(8,128)S(1)}, f32[32,256]{1,0:T(8,128)S(1)}, u32[]{:S(2)}, u32[]{:S(2)}) %collective-permute-start.5) | collective-permute-done | bytes 32800 | tf_op jit(solution)/shard_map/ppermute | solution.py:26
  23.7 1.4 %shard_map.146 = (f32[16,16,256]{2,1,0:T(8,128)}, f32[4,128]{1,0:T(4,128)}) custom-call(f32[6,16,16,256]{3,2,1,0:T(8,128)S(1)} %copy-done, f32[4,16,16,256]{3,2,1,0:T(8,128)S(1)} %get-tuple-element.29.basis_ref, f32[16,16,256]{2,1,0:T(8,128)S(1)} %get-tuple-element.45.forced_ref, f32[16,16,256]{2,1,0:T(8,128)S(1)} %get-tuple-element.32.scale_ref, ...), custom_call_target="tpu_custom_call" | custom-call | tf_op jit(solution)/shard_map/pallas_call | solution.py:38
  (1 shorter events, 0.0 us)
Async XLA Ops:
  0.6 8.7 %copy-start = (f32[6,16,16,256]{3,2,1,0:T(8,128)S(1)}, f32[6,16,16,256]{3,2,1,0:T(8,128)}, u32[]{:S(2)}) copy-start(f32[6,16,16,256]{3,2,1,0:T(8,128)} %faces_ref.5) | copy-start | bytes 4718596
  0.6 8.7 %copy-start.2 = (f32[2,512]{1,0:T(2,128)S(1)}, f32[2,512]{1,0:T(2,128)}, u32[]{:S(2)}) copy-start(f32[2,512]{1,0:T(2,128)} %trans_ref.3) | copy-start | bytes 12292
  0.7 8.7 %copy-start.4 = (s32[2,512]{1,0:T(2,128)S(1)}, s32[2,512]{1,0:T(2,128)}, u32[]{:S(2)}) copy-start(s32[2,512]{1,0:T(2,128)} %peer_ref.1) | copy-start | bytes 12292
  0.7 8.7 %copy-start.5 = (s32[512]{0:T(512)S(1)}, s32[512]{0:T(512)}, u32[]{:S(2)}) copy-start(s32[512]{0:T(512)} %param.23) | copy-start | bytes 6148
  0.7 8.7 %copy-start.6 = (f32[512]{0:T(512)S(1)}, f32[512]{0:T(512)}, u32[]{:S(2)}) copy-start(f32[512]{0:T(512)} %param.21) | copy-start | bytes 6148
  0.7 8.7 %copy-start.7 = (f32[512]{0:T(512)S(1)}, f32[512]{0:T(512)}, u32[]{:S(2)}) copy-start(f32[512]{0:T(512)} %param.20) | copy-start | bytes 6148
  0.7 8.7 %copy-start.1 = (f32[16,16,256]{2,1,0:T(8,128)S(1)}, f32[16,16,256]{2,1,0:T(8,128)}, u32[]{:S(2)}) copy-start(f32[16,16,256]{2,1,0:T(8,128)} %accum_ref.1) | copy-start | bytes 786436
  2.5 1.3 %collective-permute-start = (f32[72,256]{1,0:T(8,128)S(1)}, f32[72,256]{1,0:T(8,128)S(1)}, u32[]{:S(2)}, u32[]{:S(2)}) collective-permute-start(f32[72,256]{1,0:T(8,128)S(1)} %get-tuple-element.37), channel_id=1, source_target_pairs={{0,1},{1,0},{2,3},{3,2},{4,5},{5,4},{6,7},{7,6},{8,9},{9,8},{10,11... | collective-permute-start | bytes 221192 | tf_op jit(solution)/shard_map/ppermute | solution.py:24
  3.9 9.6 %copy-start.3 = (f32[512]{0:T(512)S(1)}, f32[512]{0:T(512)}, u32[]{:S(2)}) copy-start(f32[512]{0:T(512)} %param.19) | copy-start | bytes 6148
  3.9 7.1 %collective-permute-start.1 = (f32[72,256]{1,0:T(8,128)S(1)}, f32[72,256]{1,0:T(8,128)S(1)}, u32[]{:S(2)}, u32[]{:S(2)}) collective-permute-start(f32[72,256]{1,0:T(8,128)S(1)} %get-tuple-element.39), channel_id=1, source_target_pairs={{0,2},{2,0},{4,6},{6,4},{8,10},{10,8},{12,14},{14,12},{16,18},{18,... | collective-permute-start | bytes 221192 | tf_op jit(solution)/shard_map/ppermute | solution.py:24
  5.5 8.0 %collective-permute-start.2 = (f32[72,256]{1,0:T(8,128)S(1)}, f32[72,256]{1,0:T(8,128)S(1)}, u32[]{:S(2)}, u32[]{:S(2)}) collective-permute-start(f32[72,256]{1,0:T(8,128)S(1)} %get-tuple-element.40), channel_id=1, source_target_pairs={{2,4},{4,2},{6,8},{8,6},{10,12},{12,10},{14,16},{16,14},{18,20},{2... | collective-permute-start | bytes 221192 | tf_op jit(solution)/shard_map/ppermute | solution.py:26
  14.7 1.3 %collective-permute-start.3 = (f32[32,256]{1,0:T(8,128)S(1)}, f32[32,256]{1,0:T(8,128)S(1)}, u32[]{:S(2)}, u32[]{:S(2)}) collective-permute-start(f32[32,256]{1,0:T(8,128)S(1)} %get-tuple-element.49), channel_id=1, source_target_pairs={{0,1},{1,0},{2,3},{3,2},{4,5},{5,4},{6,7},{7,6},{8,9},{9,8},{10,11... | collective-permute-start | bytes 98312 | tf_op jit(solution)/shard_map/ppermute | solution.py:24
  16.0 4.6 %collective-permute-start.4 = (f32[32,256]{1,0:T(8,128)S(1)}, f32[32,256]{1,0:T(8,128)S(1)}, u32[]{:S(2)}, u32[]{:S(2)}) collective-permute-start(f32[32,256]{1,0:T(8,128)S(1)} %get-tuple-element.52), channel_id=1, source_target_pairs={{0,2},{2,0},{4,6},{6,4},{8,10},{10,8},{12,14},{14,12},{16,18},{18,... | collective-permute-start | bytes 98312 | tf_op jit(solution)/shard_map/ppermute | solution.py:24
  16.1 7.6 %collective-permute-start.5 = (f32[32,256]{1,0:T(8,128)S(1)}, f32[32,256]{1,0:T(8,128)S(1)}, u32[]{:S(2)}, u32[]{:S(2)}) collective-permute-start(f32[32,256]{1,0:T(8,128)S(1)} %get-tuple-element.53), channel_id=1, source_target_pairs={{2,4},{4,2},{6,8},{8,6},{10,12},{12,10},{14,16},{16,14},{18,20},{2... | collective-permute-start | bytes 98312 | tf_op jit(solution)/shard_map/ppermute | solution.py:26

commit v3 on v2

v3 whole, which is shorter than its diff:
```python
import jax
import jax.numpy as jnp
from jax import lax
from jax.experimental import pallas as pl
from jax.experimental.pallas import tpu as pltpu
from jax.sharding import PartitionSpec as P

BLOCK = 4
OMEGA = 0.8
TILE = 8
LANES = 128
F32 = jnp.float32
BF16 = jnp.bfloat16


def pair_lists(count):
    even = [(i, i ^ 1) for i in range(count) if i ^ 1 < count]
    odd = [(i, i + 1 if i % 2 else i - 1) for i in range(1, count)]
    return even, [(a, b) for a, b in odd if 0 < b < count]


def swap_pairs(even_load, odd_load, axis):
    even, odd = pair_lists(lax.axis_size(axis))
    got = [lax.ppermute(even_load, axis, even)]
    if odd:
        got.append(lax.ppermute(odd_load, axis, odd))
    return got


def run(kernel, outs, args, scratch=(), smem=(), in_place=(), out_place=()):
    spec = pl.BlockSpec(memory_space=pltpu.VMEM)
    scalar = pl.BlockSpec(memory_space=pltpu.SMEM)
    there = pl.BlockSpec(memory_space=pltpu.HBM)

    def place(i):
        return scalar if i in smem else there if i in in_place else spec

    return pl.pallas_call(
        kernel,
        out_shape=[jax.ShapeDtypeStruct(shape, dtype) for shape, dtype in outs],
        in_specs=[place(i) for i in range(len(args))],
        out_specs=[there if i in out_place else spec for i in range(len(outs))],
        scratch_shapes=list(scratch),
        compiler_params=pltpu.CompilerParams(vmem_limit_bytes=24 << 20),
    )(*args)


def iota(shape, dim):
    return lax.broadcasted_iota(jnp.int32, shape, dim)


def own_node(cell):
    return cell // BLOCK


def side_node(cell):
    return cell // BLOCK + (-1 if cell % BLOCK < BLOCK // 2 else 1)


def near_terms(x):
    own, near = own_node(x) + 2, side_node(x) + 2
    terms = [(0, 0, own), (1, 0, near), (2, 1, own), (3, 1, near), (4, 2, own), (5, 2, near)]
    if 0 < x % BLOCK < BLOCK - 1:
        terms = terms + [(6, 0, 2 * own - near), (7, 1, 2 * own - near)]
    return terms


def own_nodes(cells):
    return lax.shift_right_arithmetic(cells, 2)


def side_nodes(cells):
    low = jnp.bitwise_and(cells, BLOCK - 1) < BLOCK // 2
    return own_nodes(cells) + jnp.where(low, -1, 1)


def node_masks(cells):
    index = iota((cells, LANES), 0)
    lane = iota((cells, LANES), 1)
    own, side = own_nodes(index) + 2, side_nodes(index) + 2
    return own == lane, side == lane, 2 * own - side == lane


def fold_lanes(value):
    total = value[:, :LANES]
    for start in range(LANES, value.shape[1], LANES):
        total = total + value[:, start : start + LANES]
    return total


def by_parity(is_even, even_value, odd_value):
    return jnp.where(jnp.full(even_value.shape, is_even, jnp.int32) > 0, even_value, odd_value)


def low_high(is_even, even_got, odd_got):
    low = by_parity(is_even, odd_got, even_got)
    high = by_parity(is_even, even_got, odd_got)
    return low, high


def basis_terms(x, residual, weight):
    own, near = own_node(x) + 2, side_node(x) + 2
    nodes = (own, near, own, near)
    return residual, [(k // 2, nodes[k], weight(k)) for k in range(4)]


def restrict_tile(columns, rows, cell_rows, cell_cols):
    sums = {}
    for value, terms in columns:
        for kind, node, weight in terms:
            part = fold_lanes(weight * value)
            key = (kind, node)
            sums[key] = sums[key] + part if key in sums else part
    masks = node_masks(cell_cols)
    row_index = iota((TILE, LANES), 0)
    tile = jnp.zeros((TILE, LANES), F32)
    nodes = sorted({node for _, node in sums})
    wide = {}
    if rows:
        lane = iota((cell_rows, LANES), 1)
        for y, residual, weight in rows():
            for k in range(4):
                node = (own_node(y) if k < 2 else side_node(y)) + 2
                part = jnp.sum(fold_lanes(weight(k) * residual), axis=1, keepdims=True)
                part = jnp.where(lane == node, part, 0.0)
                wide[k % 2] = wide[k % 2] + part if k % 2 in wide else part
        x_index = iota((cell_rows, LANES), 0)
        x_nodes = (own_nodes(x_index) + 2, side_nodes(x_index) + 2)
    for node in nodes:
        total = jnp.zeros((cell_cols, LANES), F32)
        for kind in range(3):
            if (kind, node) in sums:
                lane_sum = jnp.sum(sums[(kind, node)], axis=1, keepdims=True)
                total = total + jnp.where(masks[kind], lane_sum, 0.0)
        line = jnp.sum(total, axis=0, keepdims=True)
        if rows:
            extra = jnp.where(x_nodes[0] == node, wide[0], 0.0) + jnp.where(
                x_nodes[1] == node, wide[1], 0.0
            )
            line = line + jnp.sum(extra, axis=0, keepdims=True)
        tile = jnp.where(row_index == node, line, tile)
    return tile


def join_rows(tile, low, high):
    row = iota((TILE, LANES), 0)
    half = TILE // 2
    return (
        tile
        + jnp.where(row < half, pltpu.roll(low, half, 0), 0.0)
        + jnp.where(row >= half, pltpu.roll(high, half, 0), 0.0)
    )


def join_lanes(tile, low, high):
    part = jnp.bitwise_and(iota((TILE, LANES), 1), TILE - 1)
    half = TILE // 2
    return (
        tile
        + jnp.where(part < half, pltpu.roll(low, LANES - half, 1), 0.0)
        + jnp.where(part >= half, pltpu.roll(high, half, 1), 0.0)
    )


def coarse_parts(table):
    lane = iota((TILE, LANES), 1)
    diag = pltpu.roll(table, LANES - TILE, 1)
    live = (lane < TILE) & (diag > 0.0)
    parts = [jnp.where(live, 1.0 / jnp.where(live, diag, 1.0), 0.0)]
    for direction in range(4):
        ratio = pltpu.roll(table, LANES - TILE * (2 + direction), 1)
        parts.append(jnp.where(lane < TILE, ratio, 0.0))
    return parts


def coarse_solve(tile, parts):
    first = tile * parts[0]
    near = (
        pltpu.roll(first, 1, 0),
        pltpu.roll(first, TILE - 1, 0),
        pltpu.roll(first, 1, 1),
        pltpu.roll(first, LANES - 1, 1),
    )
    second = first
    for direction in range(4):
        second = second + parts[1 + direction] * near[direction]
    return second


class Fields:
    def __init__(self, second, cell_rows, cell_cols):
        masks = node_masks(cell_cols)
        self.columns = {}
        for node in range(1, TILE - 1):
            line = jnp.broadcast_to(second[node : node + 1, :], (cell_cols, LANES))
            for kind in range(3):
                self.columns[(kind, node)] = jnp.sum(
                    jnp.where(masks[kind], line, 0.0), axis=1, keepdims=True
                )
        x_index = iota((cell_rows, LANES), 0)
        self.wide = []
        for nodes in (own_nodes(x_index) + 2, side_nodes(x_index) + 2):
            value = jnp.zeros((cell_rows, LANES), F32)
            for node in range(1, TILE - 1):
                value = jnp.where(nodes == node, second[node : node + 1, :], value)
            self.wide.append(value)

    def column(self, x, weight):
        own, side = own_node(x) + 2, side_node(x) + 2
        return (
            weight(0) * self.columns[(0, own)]
            + weight(1) * self.columns[(0, side)]
            + weight(2) * self.columns[(1, own)]
            + weight(3) * self.columns[(1, side)]
        )

    def terms(self, x, weight):
        total = None
        for table, kind, node in near_terms(x):
            part = weight(table) * self.columns[(kind, node)]
            total = part if total is None else total + part
        return total

    def row(self, y, weight):
        lane = iota(self.wide[0].shape, 1)

        def pick(kind, node):
            return jnp.sum(jnp.where(lane == node, self.wide[kind], 0.0), axis=1, keepdims=True)

        own, side = own_node(y) + 2, side_node(y) + 2
        return (
            weight(0) * pick(0, own)
            + weight(1) * pick(1, own)
            + weight(2) * pick(0, side)
            + weight(3) * pick(1, side)
        )


def shift_rows(value):
    row = iota((TILE, value.shape[1]), 0)
    parts = [value[i : i + TILE, :] for i in range(0, value.shape[0], TILE)]
    up = [pltpu.roll(part, TILE - 1, 0) for part in parts]
    down = [pltpu.roll(part, 1, 0) for part in parts]
    above = [
        jnp.where(row == TILE - 1, end, part) for end, part in zip(up[1:] + [0.0], up)
    ]
    below = [jnp.where(row == 0, end, part) for end, part in zip([0.0] + down[:-1], down)]
    return jnp.concatenate(above, axis=0), jnp.concatenate(below, axis=0)


def neighbour_sum(faces, x, left, centre, right):
    depth = centre.shape[1]
    above, below = shift_rows(centre)
    total = faces[2, x] * above + faces[3, x] * below
    total = total + faces[4, x] * pltpu.roll(centre, depth - 1, 1)
    total = total + faces[5, x] * pltpu.roll(centre, 1, 1)
    if right is not None:
        total = total + faces[0, x] * right
    if left is not None:
        total = total + faces[1, x] * left
    return total


def add_edge_rows(value, low_row, high_row):
    row = iota((TILE, value.shape[1]), 0)
    low = value[:TILE, :] + jnp.where(row == 0, low_row, 0.0)
    high = value[-TILE:, :] + jnp.where(row == TILE - 1, high_row, 0.0)
    return jnp.concatenate([low, value[TILE:-TILE, :], high] if value.shape[0] > 2 * TILE else [low, high], axis=0)


def split3(value):
    high = value.astype(BF16)
    rest = value - high.astype(F32)
    mid = rest.astype(BF16)
    return high, mid, (rest - mid.astype(F32)).astype(BF16)


def stacked(values, count=3):
    return jnp.concatenate([part for value in values for part in split3(value)[:count]], axis=0)


def unstack(product, rows, count=3):
    parts = [product[i : i + rows, :] for i in range(0, product.shape[0], rows)]
    return [sum(parts[i + 1 : i + count], parts[i]) for i in range(0, len(parts), count)]


def gather_cells(fields, hot_row, hot_depth, count=3):
    product = jnp.dot(stacked(fields, count), hot_depth, preferred_element_type=F32)
    at_row = hot_row.astype(F32)
    return [
        jnp.sum(picked * at_row, axis=0, keepdims=True)
        for picked in unstack(product, fields[0].shape[0], count)
    ]


def scatter_cells(values, hot_row, hot_depth):
    spread = jnp.concatenate([hot_row * part for part in split3(values)], axis=0)
    product = lax.dot_general(
        spread, hot_depth, (((1,), (1,)), ((), ())), preferred_element_type=F32
    )
    return unstack(product, hot_row.shape[0])[0]


def nodes_at_slots(second, hot_node, node_weight):
    product = jnp.dot(stacked([second]), hot_node, preferred_element_type=F32)
    picked = unstack(product, TILE)[0]
    total = jnp.sum(picked * node_weight, axis=0, keepdims=True)
    half = total.shape[1] // 2
    return total[:, :half] + total[:, half:]


def slots_at_nodes(values, hot_node, node_weight):
    weighted = node_weight * jnp.concatenate([values, values], axis=1)
    product = lax.dot_general(
        stacked([weighted]), hot_node, (((1,), (1,)), ((), ())), preferred_element_type=F32
    )
    return unstack(product, TILE)[0]


def as_line(value):
    return jnp.concatenate([value[i : i + 1, :] for i in range(value.shape[0])], axis=1)


def as_rows(line, width):
    return jnp.concatenate(
        [line[:, start : start + width] for start in range(0, line.shape[1], width)], axis=0
    )


def local(
    matrix_source,
    accum,
    faces,
    basis,
    coarse_diag,
    coarse_ratio,
    frac_source,
    frac_accum,
    frac_link,
    frac_trans,
    frac_cell,
    frac_peer,
    frac_count,
):
    slots = frac_source.shape[0]
    cell_rows, cell_cols, depth = matrix_source.shape
    cells = cell_rows * cell_cols
    node_rows, node_cols = cell_rows // BLOCK, cell_cols // BLOCK
    assert node_rows + 4 == TILE and node_cols + 4 == TILE
    assert depth & (depth - 1) == 0 and cell_rows == cell_cols
    depth_bits = depth.bit_length() - 1
    lay_size = lax.axis_size("lay")
    lay_pairs = len([p for p in pair_lists(lay_size) if p])
    layer_rows = 4 * cell_cols
    load_one = (layer_rows + TILE, depth)
    slot_rows = slots // depth
    load_two = (cell_cols + 2 * TILE, depth)
    block = matrix_source.shape

    def is_even(axis):
        return 1 - jnp.bitwise_and(lax.axis_index(axis), 1)

    piece = BLOCK
    pieces = cell_rows // piece

    small = (slots // LANES, LANES)
    slot_arrays = [frac_cell.reshape(small)]
    slot_kinds = len(slot_arrays)

    def kernel_a(basis_hbm, source_hbm, cdiag_hbm, ratio_hbm, *refs):
        slot_hbm, refs = refs[:slot_kinds], refs[slot_kinds:]
        (basis_ref, source_ref, tile_ref), refs = refs[:3], refs[3:]
        slot_refs, refs = refs[:slot_kinds], refs[slot_kinds:]
        loads, (cdiag_ref, ratio_ref, sems, small_sems) = refs[:-4], refs[-4:]
        copies = []
        for i in range(pieces):
            part = pl.ds(i * piece, piece)
            copies.append(
                (
                    pltpu.make_async_copy(source_hbm.at[part], source_ref.at[part], sems.at[0, i]),
                    pltpu.make_async_copy(
                        basis_hbm.at[:, part], basis_ref.at[:, part], sems.at[1, i]
                    ),
                )
            )
        small_copies = [
            pltpu.make_async_copy(cdiag_hbm, cdiag_ref, small_sems.at[0]),
            pltpu.make_async_copy(ratio_hbm, ratio_ref, small_sems.at[1]),
        ]
        for i, (there, here) in enumerate(zip(slot_hbm, slot_refs)):
            small_copies.append(pltpu.make_async_copy(there, here, small_sems.at[2 + i]))
        for pair in copies + [small_copies]:
            for copy in pair:
                copy.start()

        def widen(value):
            lines = jnp.concatenate(
                [
                    jnp.zeros((node_rows, 2), F32),
                    value,
                    jnp.zeros((node_rows, TILE - 2 - node_cols), F32),
                ],
                axis=1,
            )
            edge = jnp.zeros((2, TILE), F32)
            return jnp.concatenate([edge, lines, edge], axis=0)

        def column(x):
            if x % piece == 0:
                for copy in copies[x // piece]:
                    copy.wait()
            return basis_terms(x, source_ref[x], lambda k: basis_ref[k, x])

        tile = restrict_tile((column(x) for x in range(cell_rows)), None, cell_rows, cell_cols)
        for copy in small_copies:
            copy.wait()
        parts = [jnp.zeros((TILE, TILE), F32), widen(cdiag_ref[...])]
        parts = parts + [widen(ratio_ref[d]) for d in range(4)]
        parts.append(jnp.zeros((TILE, LANES - TILE * len(parts)), F32))
        table = jnp.concatenate(parts, axis=1)
        tile = tile + table
        tile_ref[...] = tile
        even = is_even("lay")
        edges = (even * (cell_rows - 1), (1 - even) * (cell_rows - 1))
        for load, edge in zip(loads, edges):
            for k in range(4):
                load[k * cell_cols : (k + 1) * cell_cols, :] = basis_ref[k, edge]
            load[layer_rows:, :LANES] = tile
            load[layer_rows:, LANES:] = jnp.zeros((TILE, depth - LANES), F32)

    outs = [(basis.shape, F32), (block, F32), ((TILE, LANES), F32)]
    outs = outs + [(value.shape, value.dtype) for value in slot_arrays]
    outs = outs + [(load_one, F32)] * lay_pairs
    basis, matrix_source, tile_own, *rest = run(
        kernel_a,
        outs,
        [
            pltpu.with_memory_space_constraint(value, pltpu.HBM)
            for value in (basis, matrix_source, coarse_diag, coarse_ratio, *slot_arrays)
        ],
        scratch=(
            pltpu.VMEM(coarse_diag.shape, F32),
            pltpu.VMEM(coarse_ratio.shape, F32),
            pltpu.SemaphoreType.DMA((2, pieces)),
            pltpu.SemaphoreType.DMA((2 + slot_kinds,)),
        ),
        in_place=range(4 + slot_kinds),
    )
    slot_cell, *loads = rest
    slot_source = frac_source.reshape(small)
    lay_one = swap_pairs(loads[0], loads[-1], "lay")

    def lay_sides(refs, window):
        even = is_even("lay")
        first = refs[0][window]
        second = refs[1][window] if len(refs) > 1 else jnp.zeros(first.shape, F32)
        return low_high(even, first, second)

    def blk_sides(even_ref, odd_ref, window):
        return low_high(is_even("blk"), even_ref[window], odd_ref[window])

    def kernel_e(tile_ref, basis_ref, *refs):
        got, (join_ref, even_ref, odd_ref) = refs[:-3], refs[-3:]
        low, high = lay_sides(got, (slice(layer_rows, layer_rows + TILE), slice(0, LANES)))
        joined = join_rows(tile_ref[...], low, high)
        join_ref[...] = joined
        even = is_even("blk")
        edges = (even * (cell_cols - 1), (1 - even) * (cell_cols - 1))
        for ref, edge in zip((even_ref, odd_ref), edges):
            for k in range(4):
                for x in range(cell_rows):
                    line = k * cell_rows + x
                    ref[line : line + 1, :] = basis_ref[k, x, pl.ds(edge, 1), :]
            ref[layer_rows:, :LANES] = joined
            ref[layer_rows:, LANES:] = jnp.zeros((TILE, depth - LANES), F32)

    outs = [((TILE, LANES), F32), (load_one, F32), (load_one, F32)]
    joined_one, even_one, odd_one = run(kernel_e, outs, (tile_own, basis, *lay_one))
    blk_one = swap_pairs(even_one, odd_one, "blk")

    links = frac_trans.shape[0]

    def kernel_p(
        basis_ref, cell_ref, row_ref, depth_ref, node_ref, weight_ref
    ):
        cell = as_line(cell_ref[...])
        at_row = lax.shift_right_logical(cell, depth_bits)
        at_depth = jnp.bitwise_and(cell, depth - 1)
        hot_row = (iota((cells, slots), 0) == at_row).astype(F32).astype(BF16)
        hot_depth = (iota((depth, slots), 0) == at_depth).astype(F32).astype(BF16)
        row_ref[...] = hot_row
        depth_ref[...] = hot_depth
        fields = [basis_ref[k].reshape(cells, depth) for k in range(4)]
        weights = gather_cells(fields, hot_row, hot_depth, 2)
        along = jnp.bitwise_and(at_row, cell_cols - 1)
        across = lax.shift_right_logical(at_row, cell_cols.bit_length() - 1)
        lane = iota((LANES, slots), 0)
        line = iota((TILE, slots), 0)
        match = (own_nodes(across) + 2 == line, side_nodes(across) + 2 == line)
        for j, nodes in enumerate((own_nodes(along), side_nodes(along))):
            part = slice(j * slots, (j + 1) * slots)
            node_ref[:, part] = (lane == nodes + 2).astype(F32).astype(BF16)
            weight_ref[:, part] = jnp.where(match[0], weights[2 * j], 0.0) + jnp.where(
                match[1], weights[2 * j + 1], 0.0
            )

    outs = [
        ((cells, slots), BF16),
        ((depth, slots), BF16),
        ((LANES, 2 * slots), BF16),
        ((TILE, 2 * slots), F32),
    ]
    hot_row, hot_depth, hot_node, node_weight = run(kernel_p, outs, (basis, slot_cell))

    tables = 8

    def kernel_q(
        faces_hbm, accum_hbm, basis_ref, source_ref, row_ref, depth_ref, link_ref, facc_ref,
        trans_ref, count_ref, sface_ref, forward_ref, back_ref, ssource_ref, scale_ref, edge_ref,
        sedge_ref, frac_ref, faces_ref, accum_ref, linked_ref, sems,
    ):
        copies = []
        for i in range(pieces):
            part = pl.ds(i * piece, piece)
            copies.append(
                (
                    pltpu.make_async_copy(accum_hbm.at[part], accum_ref.at[part], sems.at[0, i]),
                    pltpu.make_async_copy(
                        faces_hbm.at[:, part], faces_ref.at[:, part], sems.at[1, i]
                    ),
                )
            )
        for pair in copies:
            for copy in pair:
                copy.start()
        live = (iota((1, slots), 1) < count_ref[0]).astype(F32)
        couple = live * as_line(link_ref[...])
        frac_diag = as_line(facc_ref[...]) + couple
        for j in range(links):
            frac_diag = frac_diag + trans_ref[j : j + 1, :]
        frac_ref[0:1, :] = couple
        frac_ref[1:2, :] = OMEGA * live / frac_diag
        linked_ref[...] = scatter_cells(couple, row_ref[...], depth_ref[...])

        lane = iota((cell_cols, depth), 1)
        place = jnp.bitwise_and(iota((cell_cols, depth), 0), BLOCK - 1)
        for x in range(cell_rows):
            if x % piece == 0:
                for copy in copies[x // piece]:
                    copy.wait()
            diag = accum_ref[x] + linked_ref[x * cell_cols : (x + 1) * cell_cols, :]
            for d in range(6):
                diag = diag + faces_ref[d, x]
            scale = OMEGA / diag
            scale_ref[x] = scale
            ssource_ref[x] = scale * source_ref[x]
            deep = jnp.where(lane < depth - 1, faces_ref[4, x], 0.0)
            shallow = jnp.where(lane > 0, faces_ref[5, x], 0.0)
            for d in range(4):
                sface_ref[d, x] = scale * faces_ref[d, x]
            sface_ref[4, x] = scale * deep
            sface_ref[5, x] = scale * shallow
            near = {}
            for k in range(4):
                value = basis_ref[k, x]
                near[k] = (
                    deep * pltpu.roll(value, depth - 1, 1)
                    + shallow * pltpu.roll(value, 1, 1)
                    - diag * value
                )
            for i in range(2):
                own_up, own_down = shift_rows(basis_ref[i, x])
                side_up, side_down = shift_rows(basis_ref[2 + i, x])
                far = None
                for face, own, side, swap_at, far_at in (
                    (faces_ref[3, x], own_down, side_down, 0, BLOCK // 2),
                    (faces_ref[2, x], own_up, side_up, BLOCK - 1, BLOCK // 2 - 1),
                ):
                    own, side = face * own, face * side
                    swap, beyond = place == swap_at, place == far_at
                    near[i] = near[i] + jnp.where(swap, side, own)
                    near[2 + i] = near[2 + i] + jnp.where(
                        swap, own, jnp.where(beyond, 0.0, side)
                    )
                    far = jnp.where(beyond, side, 0.0 if far is None else far)
                near[4 + i] = far
            nodes = (own_node(x), side_node(x), 2 * own_node(x) - side_node(x))
            for other, d in ((x - 1, 1), (x + 1, 0)):
                if not 0 <= other < cell_rows:
                    continue
                face = faces_ref[d, x]
                for i, node in enumerate((own_node(other), side_node(other))):
                    kind = nodes.index(node)
                    for j in range(2):
                        table = kind + 2 * j if kind < 2 else 6 + j
                        part = face * basis_ref[2 * j + i, other]
                        near[table] = near[table] + part if table in near else part
            for table, _, _ in near_terms(x):
                back_ref[table, x] = near[table]
                value = scale * near[table]
                forward_ref[table, x] = basis_ref[table, x] + value if table < 4 else value
            edge_ref[2, x : x + 1, :] = faces_ref[3, x, 0:1, :]
            edge_ref[3, x : x + 1, :] = faces_ref[2, x, cell_cols - 1 : cell_cols, :]
            sedge_ref[0, x : x + 1, :] = sface_ref[3, x, 0:1, :]
            sedge_ref[1, x : x + 1, :] = sface_ref[2, x, cell_cols - 1 : cell_cols, :]
        edge_ref[0] = faces_ref[1, 0]
        edge_ref[1] = faces_ref[0, cell_rows - 1]

    outs = [
        (faces.shape, F32),
        ((tables, *block), F32),
        ((tables, *block), F32),
        (block, F32),
        (block, F32),
        ((4, cell_cols, depth), F32),
        ((2, cell_rows, depth), F32),
        ((TILE, slots), F32),
    ]
    sfaces, forward, back, ssource, scale, edge_faces, sedges, frac_pack = run(
        kernel_q,
        outs,
        (
            pltpu.with_memory_space_constraint(faces, pltpu.HBM),
            pltpu.with_memory_space_constraint(accum, pltpu.HBM),
            basis,
            matrix_source,
            hot_row,
            hot_depth,
            frac_link.reshape(small),
            frac_accum.reshape(small),
            frac_trans,
            frac_count,
        ),
        smem=(9,),
        scratch=(
            pltpu.VMEM(faces.shape, F32),
            pltpu.VMEM(block, F32),
            pltpu.VMEM((cells, depth), F32),
            pltpu.SemaphoreType.DMA((2, pieces)),
        ),
        in_place=(0, 1),
    )

    layer = (slice(0, layer_rows), slice(0, depth))

    def rims_of(lay_refs, blk_even, blk_odd):
        lay_low, lay_high = lay_sides(lay_refs, layer)
        blk_low, blk_high = blk_sides(blk_even, blk_odd, layer)

        def pick(value):
            return lambda k: value[k * cell_cols : (k + 1) * cell_cols, :]

        return pick(lay_low), pick(lay_high), pick(blk_low), pick(blk_high)

    last = cell_rows - 1

    def kernel_b(
        sface_ref, forward_ref, back_ref, ssource_ref, edge_ref, sedge_ref, node_ref, weight_ref,
        frac_ref, fsrc_ref, own_ref, joined_ref, blk_even, blk_odd, *refs,
    ):
        lay_refs = refs[:lay_pairs]
        p2_ref, rows_ref, f_ref, tile_ref, parts_ref = refs[lay_pairs : lay_pairs + 5]
        loads = refs[lay_pairs + 5 :]
        at_tile = (slice(layer_rows, layer_rows + TILE), slice(0, LANES))
        low, high = blk_sides(blk_even, blk_odd, at_tile)
        table = join_lanes(joined_ref[...], low, high)
        parts = coarse_parts(table)
        for i, part in enumerate(parts):
            parts_ref[i] = part
        second = coarse_solve(table, parts)
        fields = Fields(second, cell_rows, cell_cols)
        x_low, x_high, y_low, y_high = rims_of(lay_refs, blk_even, blk_odd)
        left_rim = sface_ref[1, 0] * fields.column(-1, x_low)
        right_rim = sface_ref[0, last] * fields.column(cell_rows, x_high)
        low_rim = sedge_ref[0] * fields.row(-1, y_low)
        high_rim = sedge_ref[1] * fields.row(cell_cols, y_high)

        couple = frac_ref[0:1, :]
        pressure_at = nodes_at_slots(second, node_ref[...], weight_ref[...])
        fracture = frac_ref[1:2, :] * (as_line(fsrc_ref[...]) + couple * pressure_at)
        f_ref[...] = fracture
        linked = slots_at_nodes(couple * fracture, node_ref[...], weight_ref[...])

        def columns():
            for x in range(cell_rows):
                value = ssource_ref[x] + fields.terms(x, lambda t: forward_ref[t, x])
                if x == 0:
                    value = value + left_rim
                if x == last:
                    value = value + right_rim
                value = add_edge_rows(value, low_rim[x : x + 1, :], high_rim[x : x + 1, :])
                p2_ref[x] = value
                rows_ref[0, x : x + 1, :] = value[0:1, :]
                rows_ref[1, x : x + 1, :] = value[cell_cols - 1 : cell_cols, :]
                if x == 0:
                    yield basis_terms(-1, edge_ref[0] * value, x_low)
                if x == last:
                    yield basis_terms(cell_rows, edge_ref[1] * value, x_high)
                yield value, [(kind, node, back_ref[t, x]) for t, kind, node in near_terms(x)]

        def rows():
            yield -1, edge_ref[2] * rows_ref[0], y_low
            yield cell_cols, edge_ref[3] * rows_ref[1], y_high

        tile = restrict_tile(columns(), rows, cell_rows, cell_cols) + linked
        tile = tile + jnp.where(iota((TILE, LANES), 1) < TILE, own_ref[...], 0.0)
        tile_ref[...] = tile
        even = is_even("lay")
        edges = (even * last, (1 - even) * last)
        for load, edge in zip(loads, edges):
            load[:cell_cols, :] = p2_ref[edge]
            load[cell_cols : cell_cols + TILE, :LANES] = tile
            load[cell_cols : cell_cols + TILE, LANES:] = jnp.zeros((TILE, depth - LANES), F32)
            load[cell_cols + TILE :, :] = jnp.zeros((TILE, depth), F32)
            load[cell_cols + TILE : cell_cols + TILE + slot_rows, :] = as_rows(fracture, depth)

    parts_shape = (5, TILE, LANES)
    row_pair = (2, cell_rows, depth)
    outs = [(block, F32), (row_pair, F32), ((1, slots), F32), ((TILE, LANES), F32)]
    outs = outs + [(parts_shape, F32)] + [(load_two, F32)] * lay_pairs
    pressure, edge_rows, fracture, tile_two, coarse, *loads = run(
        kernel_b,
        outs,
        (
            sfaces, forward, back, ssource, edge_faces, sedges, hot_node, node_weight,
            frac_pack, slot_source, tile_own, joined_one, *blk_one, *lay_one,
        ),
    )
    lay_two = swap_pairs(loads[0], loads[-1], "lay")

    tile_rows = (slice(cell_cols, cell_cols + TILE), slice(0, LANES))
    frac_rows = (slice(cell_cols + TILE, cell_cols + TILE + slot_rows), slice(0, depth))

    def kernel_f(tile_ref, rows_ref, *refs):
        got, (join_ref, even_ref, odd_ref) = refs[:-3], refs[-3:]
        low, high = lay_sides(got, tile_rows)
        joined = join_rows(tile_ref[...], low, high)
        join_ref[...] = joined
        even = is_even("blk")
        even_ref[:cell_cols, :] = rows_ref[even]
        odd_ref[:cell_cols, :] = rows_ref[1 - even]
        for ref in (even_ref, odd_ref):
            ref[cell_cols : cell_cols + TILE, :LANES] = joined
            ref[cell_cols : cell_cols + TILE, LANES:] = jnp.zeros((TILE, depth - LANES), F32)
            ref[cell_cols + TILE :, :] = got[0][cell_cols + TILE :, :]

    outs = [((TILE, LANES), F32), (load_two, F32), (load_two, F32)]
    joined_two, even_two, odd_two = run(kernel_f, outs, (tile_two, edge_rows, *lay_two))
    blk_two = swap_pairs(even_two, odd_two, "blk")

    def kernel_m(
        sface_ref, ssource_ref, scale_ref, p2_ref, f_ref, row_ref, depth_ref, frac_ref, peer_ref,
        base_ref, at_ref, high_ref, low_ref,
    ):
        owner = lax.axis_index("blk") * lay_size + lax.axis_index("lay")
        peer = as_line(peer_ref[...] - (owner - 1) * slots)
        low_ref[...] = (
            (iota((LANES, peer.shape[1]), 0) == jnp.bitwise_and(peer, LANES - 1))
            .astype(F32)
            .astype(BF16)
        )
        high_ref[...] = lax.shift_right_logical(peer, 7)
        hot_row, hot_depth = row_ref[...], depth_ref[...]
        flat = p2_ref[...].reshape(cells, depth)
        at_ref[...] = gather_cells([flat], hot_row, hot_depth)[0]
        linked = scatter_cells(frac_ref[0:1, :] * f_ref[...], hot_row, hot_depth)
        for x in range(cell_rows):
            centre = p2_ref[x]
            left = p2_ref[x - 1] if x else None
            right = p2_ref[x + 1] if x < last else None
            around = neighbour_sum(sface_ref, x, left, centre, right)
            part = linked[x * cell_cols : (x + 1) * cell_cols, :]
            base_ref[x] = ssource_ref[x] + scale_ref[x] * part + (1.0 - OMEGA) * centre + around

    outs = [
        (block, F32),
        ((1, slots), F32),
        ((1, links * slots), jnp.int32),
        ((LANES, links * slots), BF16),
    ]
    base, slot_pressure, peer_high, hot_low = run(
        kernel_m,
        outs,
        (sfaces, ssource, scale, pressure, fracture, hot_row, hot_depth, frac_pack, frac_peer),
    )
    ring = []
    if lay_size != 2:
        owners = lax.axis_size("blk") * lay_size
        ahead = [(i, i + 1) for i in range(owners - 1)]
        line = fracture.reshape(slot_rows, depth)
        ring = [
            lax.ppermute(line, ("blk", "lay"), ahead),
            lax.ppermute(line, ("blk", "lay"), [(b, a) for a, b in ahead]),
        ]

    def kernel_c(
        sface_ref, forward_ref, base_ref, sedge_ref, node_ref, weight_ref, frac_ref, high_ref,
        low_ref, fsrc_ref, trans_ref, f_ref, at_ref, joined_ref, parts_ref,
        one_even, one_odd, two_even, two_odd, *refs,
    ):
        lay_first, lay_second = refs[:lay_pairs], refs[lay_pairs : 2 * lay_pairs]
        ring_refs = refs[2 * lay_pairs : -5]
        p_hbm, f_hbm, p_out, f_out, sems = refs[-5:]
        low, high = blk_sides(two_even, two_odd, tile_rows)
        tile = join_lanes(joined_ref[...], low, high)
        second = coarse_solve(tile, [parts_ref[i] for i in range(5)])
        fields = Fields(second, cell_rows, cell_cols)
        x_low, x_high, y_low, y_high = rims_of(lay_first, one_even, one_odd)
        window = (slice(0, cell_cols), slice(0, depth))
        p_left, p_right = lay_sides(lay_second, window)
        p_low, p_high = blk_sides(two_even, two_odd, window)

        left_rim = sface_ref[1, 0] * (p_left + fields.column(-1, x_low))
        right_rim = sface_ref[0, last] * (p_right + fields.column(cell_rows, x_high))
        low_rim = sedge_ref[0] * (p_low + fields.row(-1, y_low))
        high_rim = sedge_ref[1] * (p_high + fields.row(cell_cols, y_high))
        pressure_at = at_ref[...] + nodes_at_slots(second, node_ref[...], weight_ref[...])
        mine = as_rows(f_ref[...], LANES)
        if ring_refs:
            before, after = ring_refs[0][...], ring_refs[1][...]
        else:
            partner = lay_second[0][frac_rows]
            from_low, from_high = blk_sides(two_even, two_odd, frac_rows)
            before = by_parity(is_even("lay"), from_low, partner)
            after = by_parity(is_even("lay"), partner, from_high)
        width = mine.shape[0]
        wide = jnp.concatenate(
            [as_rows(as_line(before), LANES), mine, as_rows(as_line(after), LANES)]
            + [jnp.zeros((-3 * width % TILE, LANES), F32)] * (3 * width % TILE > 0),
            axis=0,
        )
        product = jnp.dot(stacked([wide]), low_ref[...], preferred_element_type=F32)
        picked = unstack(product, wide.shape[0])[0]
        match = iota(picked.shape, 0) == high_ref[...]
        peers = jnp.sum(jnp.where(match, picked, 0.0), axis=0, keepdims=True)
        flux = as_line(fsrc_ref[...]) + frac_ref[0:1, :] * pressure_at
        for j in range(links):
            flux = flux + trans_ref[j : j + 1, :] * peers[:, j * slots : (j + 1) * slots]
        result = (1.0 - OMEGA) * f_ref[...] + frac_ref[1:2, :] * flux
        copies = []
        for x in range(cell_rows):
            value = base_ref[x] + fields.terms(x, lambda t: forward_ref[t, x])
            if x == 0:
                value = value + left_rim
            if x == last:
                value = value + right_rim
            p_out[x] = add_edge_rows(value, low_rim[x : x + 1, :], high_rim[x : x + 1, :])
            if (x + 1) % piece == 0:
                part = pl.ds(x + 1 - piece, piece)
                copies.append(
                    pltpu.make_async_copy(p_out.at[part], p_hbm.at[part], sems.at[x // piece])
                )
                copies[-1].start()
        f_out[...] = as_rows(result, LANES)
        copies.append(pltpu.make_async_copy(f_out, f_hbm, sems.at[pieces]))
        copies[-1].start()
        for copy in copies:
            copy.wait()

    final, frac_final = run(
        kernel_c,
        [(block, F32), (small, F32)],
        (
            sfaces, forward, base, sedges, hot_node, node_weight, frac_pack, peer_high,
            hot_low, slot_source, frac_trans, fracture, slot_pressure, joined_two, coarse,
            *blk_one, *blk_two, *lay_one, *lay_two, *ring,
        ),
        scratch=(
            pltpu.VMEM(block, F32),
            pltpu.VMEM(small, F32),
            pltpu.SemaphoreType.DMA((pieces + 1,)),
        ),
        out_place=(0, 1),
    )
    return final, frac_final.reshape(slots)


def solution(mesh):
    return jax.shard_map(
        local,
        mesh=mesh,
        in_specs=(
            P("lay", "blk", None),
            P("lay", "blk", None),
            P(None, "lay", "blk", None),
            P(None, "lay", "blk", None),
            P("lay", "blk"),
            P(None, "lay", "blk"),
            P(("blk", "lay")),
            P(("blk", "lay")),
            P(("blk", "lay")),
            P(None, ("blk", "lay")),
            P(("blk", "lay")),
            P(None, ("blk", "lay")),
            P(("blk", "lay")),
        ),
        out_specs=(P("lay", "blk", None), P(("blk", "lay"))),
        check_vma=False,
    )
```

time: 25.3 us -> 25.8 us (1.020)
  Pallas kernels: 6.62 us -> 8.22 us
  waiting for transfers between devices: 8.06 us -> 6.85 us
    pallas_call x7 -> x8, Pallas kernels: 6.62 us -> 8.22 us  [run(): pl.pallas_call(kernel, out_shape=[jax.ShapeDtypeStruct(shape, dtype) for...]
    ppermute x4, starting transfers between devices: 1.77 us -> 3.02 us  [swap_pairs(): got = [lax.ppermute(even_load, axis, even)]]
    ppermute x2, waiting for transfers between devices: 5.6 us -> 4.4 us  [swap_pairs(): got.append(lax.ppermute(odd_load, axis, odd))]
    ppermute x2, starting transfers between devices: 7.12 us -> 6.03 us  [swap_pairs(): got.append(lax.ppermute(odd_load, axis, odd))]
  transfers between devices with their start and end apart: 6 -> 6, of which waited for: 4 -> 4; matrix products, arithmetic and copies ran while one was open for 0% -> 0% of each run, Pallas kernels for 9% -> 17%
where the time goes in v3:
time: 25.8 us; the launch traced here: 25.6 us
  starting transfers between devices  9.05 us (35%)
  Pallas kernels  8.22 us (32%)
  waiting for transfers between devices  6.85 us (27%)
  between operations  1.44 us (6%)
    pallas_call x8, Pallas kernels, run(): pl.pallas_call(kernel, out_shape=[jax.ShapeDtypeStruct(shape, dtype) for...  8.22 us
    ppermute x2, starting transfers between devices, swap_pairs(): got.append(lax.ppermute(odd_load, axis, odd))  6.03 us
    ppermute x2, waiting for transfers between devices, swap_pairs(): got.append(lax.ppermute(odd_load, axis, odd))  4.4 us
    ppermute x4, starting transfers between devices, swap_pairs(): got = [lax.ppermute(even_load, axis, even)]  3.02 us
    ppermute x4, waiting for transfers between devices, swap_pairs(): got = [lax.ppermute(even_load, axis, even)]  2.45 us
  transfers between devices with their start and end apart: 6, of which 4 were waited for; matrix products, arithmetic and copies ran while one was open for 0% of the time, Pallas kernels for 17%

profile of v3, /device:TPU:8, one launch (start us, length us, event | category | flops | bytes accessed | tf_op | source)
XLA Modules:
  0.0 25.6 jit_solution(12166433860924818556)
XLA Ops:
  0.6 0.0 copy-start.3
  0.6 0.0 copy-start.4
  0.7 0.0 copy-start
  0.7 1.7 %shard_map.140 = (f32[4,16,16,256]{3,2,1,0:T(8,128)S(1)}, f32[16,16,256]{2,1,0:T(8,128)S(1)}, f32[8,128]{1,0:T(8,128)S(1)}, s32[4,128]{1,0:T(4,128)S(1)}, f32[72,256]{1,0:T(8,128)S(1)}) custom-call(f32[4,16,16,256]{3,2,1,0:T(8,128)} %basis_hbm.1, f32[16,16,256]{2,1,0:T(8,128)} %source_hbm.1, f32[4,4]{1,0:T(4,128)} %cdiag_hbm.1, f32[4,4,4]{2,1,0:T(4,128)} %ratio_hbm.1, ...), custom_call_target="tpu_custom_call" | custom-call | tf_op jit(solution)/shard_map/pallas_call | solution.py:38
  2.4 0.1 collective-permute-start
  2.4 1.3 %collective-permute-done.refs_0_ = f32[72,256]{1,0:T(8,128)S(1)} collective-permute-done((f32[72,256]{1,0:T(8,128)S(1)}, f32[72,256]{1,0:T(8,128)S(1)}, u32[]{:S(2)}, u32[]{:S(2)}) %collective-permute-start) | collective-permute-done | bytes 73760 | tf_op jit(solution)/shard_map/ppermute | solution.py:24
  3.7 0.1 shard_map.143
  3.8 1.6 %collective-permute-start.1 = (f32[72,256]{1,0:T(8,128)S(1)}, f32[72,256]{1,0:T(8,128)S(1)}, u32[]{:S(2)}, u32[]{:S(2)}) collective-permute-start(f32[72,256]{1,0:T(8,128)S(1)} %get-tuple-element.55), channel_id=1, source_target_pairs={{0,2},{2,0},{4,6},{6,4},{8,10},{10,8},{12,14},{14,12},{16,18},{18,... | collective-permute-start | bytes 221192 | tf_op jit(solution)/shard_map/ppermute | solution.py:24
  5.3 3.3 %collective-permute-start.2 = (f32[72,256]{1,0:T(8,128)S(1)}, f32[72,256]{1,0:T(8,128)S(1)}, u32[]{:S(2)}, u32[]{:S(2)}) collective-permute-start(f32[72,256]{1,0:T(8,128)S(1)} %get-tuple-element.56), channel_id=1, source_target_pairs={{2,4},{4,2},{6,8},{8,6},{10,12},{12,10},{14,16},{16,14},{18,20},{2... | collective-permute-start | bytes 221192 | tf_op jit(solution)/shard_map/ppermute | solution.py:26
  8.6 0.9 %shard_map.141 = (bf16[256,512]{1,0:T(8,128)(2,1)S(1)}, bf16[256,512]{1,0:T(8,128)(2,1)S(1)}, bf16[128,1024]{1,0:T(8,128)(2,1)S(1)}, f32[8,1024]{1,0:T(8,128)S(1)}) custom-call(f32[4,16,16,256]{3,2,1,0:T(8,128)S(1)} %get-tuple-element.37.basis_ref, s32[4,128]{1,0:T(4,128)S(1)} %get-tuple-element.39.cell_ref), custom_call_target="tpu_custom_call" | custom-call | tf_op jit(solution)/shard_map/pallas_call | solution.py:38
  9.5 0.0 copy-start.1
  10.2 0.0 copy-done.3
  10.2 0.0 copy-done.4
  10.2 0.0 copy-done
  10.2 2.8 %shard_map.142 = (f32[6,16,16,256]{3,2,1,0:T(8,128)S(1)}, f32[8,16,16,256]{3,2,1,0:T(8,128)S(1)}, f32[8,16,16,256]{3,2,1,0:T(8,128)S(1)}, f32[16,16,256]{2,1,0:T...) custom-call(f32[6,16,16,256]{3,2,1,0:T(8,128)} %faces_hbm.1, ...), custom_call_target="tpu_custom_call" | custom-call | tf_op jit(solution)/shard_map/pallas_call | solution.py:38
  13.0 0.0 collective-permute-done.1.blk_even.one_even
  13.0 0.4 %collective-permute-done.2.blk_odd.one_odd = f32[72,256]{1,0:T(8,128)S(1)} collective-permute-done((f32[72,256]{1,0:T(8,128)S(1)}, f32[72,256]{1,0:T(8,128)S(1)}, u32[]{:S(2)}, u32[]{:S(2)}) %collective-permute-start.2) | collective-permute-done | bytes 73760 | tf_op jit(solution)/shard_map/ppermute | solution.py:26
  13.4 0.0 copy-done.1
  13.4 0.0 copy-start.2
  13.4 0.9 %shard_map.144 = (f32[16,16,256]{2,1,0:T(8,128)S(1)}, f32[2,16,256]{2,1,0:T(8,128)S(1)}, f32[1,512]{1,0:T(1,128)S(1)}, f32[8,128]{1,0:T(8,128)S(1)}, f32[5,8,128]{2,1,0:T(8,128)S(1)}, /*index=5*/f32[32,256]{1,0:T(8,128)S(1)}) custom-call(f32[6,16,16,256]{3,2,1,0:T(8,128)S(1)} %get-tuple-element.42.sface_ref, ...), custom_call_target="tpu_custom_call" | custom-call | tf_op jit(solution)/shard_map/pallas_call | solution.py:38
  14.2 0.1 collective-permute-start.3
  14.3 1.2 %collective-permute-done.3.refs_0_.refs_1_ = f32[32,256]{1,0:T(8,128)S(1)} collective-permute-done((f32[32,256]{1,0:T(8,128)S(1)}, f32[32,256]{1,0:T(8,128)S(1)}, u32[]{:S(2)}, u32[]{:S(2)}) %collective-permute-start.3) | collective-permute-done | bytes 32800 | tf_op jit(solution)/shard_map/ppermute | solution.py:24
  15.5 1.3 %collective-permute-start.4 = (f32[32,256]{1,0:T(8,128)S(1)}, f32[32,256]{1,0:T(8,128)S(1)}, u32[]{:S(2)}, u32[]{:S(2)}) collective-permute-start(f32[32,256]{1,0:T(8,128)S(1)} %get-tuple-element.68), channel_id=1, source_target_pairs={{0,2},{2,0},{4,6},{6,4},{8,10},{10,8},{12,14},{14,12},{16,18},{18,... | collective-permute-start | bytes 98312 | tf_op jit(solution)/shard_map/ppermute | solution.py:24
  16.9 2.8 %collective-permute-start.5 = (f32[32,256]{1,0:T(8,128)S(1)}, f32[32,256]{1,0:T(8,128)S(1)}, u32[]{:S(2)}, u32[]{:S(2)}) collective-permute-start(f32[32,256]{1,0:T(8,128)S(1)} %get-tuple-element.69), channel_id=1, source_target_pairs={{2,4},{4,2},{6,8},{8,6},{10,12},{12,10},{14,16},{16,14},{18,20},{2... | collective-permute-start | bytes 98312 | tf_op jit(solution)/shard_map/ppermute | solution.py:26
  19.6 0.0 copy-done.2
  19.6 0.8 %shard_map.145 = (f32[16,16,256]{2,1,0:T(8,128)S(1)}, f32[1,512]{1,0:T(1,128)S(1)}, s32[1,1024]{1,0:T(1,128)S(1)}, bf16[128,1024]{1,0:T(8,128)(2,1)S(1)}) custom-call(f32[6,16,16,256]{3,2,1,0:T(8,128)S(1)} %get-tuple-element.42.sface_ref, f32[16,16,256]{2,1,0:T(8,128)S(1)} %get-tuple-element.44.ssource_ref, f32[16,16,256]{2,1,0:T(8,128)S(1)} %get-tuple-element.45.scale_ref, ...), custom_call_target="tpu_custom_call" | custom-call | tf_op jit(solution)/shard_map/pallas_call | solution.py:38
  20.4 0.0 collective-permute-done.4.two_even
  20.4 4.0 %collective-permute-done.5.two_odd = f32[32,256]{1,0:T(8,128)S(1)} collective-permute-done((f32[32,256]{1,0:T(8,128)S(1)}, f32[32,256]{1,0:T(8,128)S(1)}, u32[]{:S(2)}, u32[]{:S(2)}) %collective-permute-start.5) | collective-permute-done | bytes 32800 | tf_op jit(solution)/shard_map/ppermute | solution.py:26
  24.4 1.1 %shard_map.147 = (f32[16,16,256]{2,1,0:T(8,128)}, f32[4,128]{1,0:T(4,128)}) custom-call(f32[6,16,16,256]{3,2,1,0:T(8,128)S(1)} %get-tuple-element.42.sface_ref, f32[8,16,16,256]{3,2,1,0:T(8,128)S(1)} %get-tuple-element.43.forward_ref, f32[16,16,256]{2,1,0:T(8,128)S(1)} %get-tuple-element.59.base_ref, f32[2,16,256]{2,1,0:T(8,128)S(1)} %get-tuple-element.48.sedge_ref, ...), custom_call_target="tpu_custom_call" | custom-call | tf_op jit(solution)/shard_map/pallas_call | solution.py:38
  (1 shorter events, 0.0 us)
Async XLA Ops:
  0.6 9.5 %copy-start.3 = (f32[512]{0:T(512)S(1)}, f32[512]{0:T(512)}, u32[]{:S(2)}) copy-start(f32[512]{0:T(512)} %param.21) | copy-start | bytes 6148
  0.6 9.5 %copy-start.4 = (f32[512]{0:T(512)S(1)}, f32[512]{0:T(512)}, u32[]{:S(2)}) copy-start(f32[512]{0:T(512)} %param.20) | copy-start | bytes 6148
  0.7 9.5 %copy-start = (f32[2,512]{1,0:T(2,128)S(1)}, f32[2,512]{1,0:T(2,128)}, u32[]{:S(2)}) copy-start(f32[2,512]{1,0:T(2,128)} %trans_ref.3) | copy-start | bytes 12292
  2.4 1.3 %collective-permute-start = (f32[72,256]{1,0:T(8,128)S(1)}, f32[72,256]{1,0:T(8,128)S(1)}, u32[]{:S(2)}, u32[]{:S(2)}) collective-permute-start(f32[72,256]{1,0:T(8,128)S(1)} %get-tuple-element.53), channel_id=1, source_target_pairs={{0,1},{1,0},{2,3},{3,2},{4,5},{5,4},{6,7},{7,6},{8,9},{9,8},{10,11... | collective-permute-start | bytes 221192 | tf_op jit(solution)/shard_map/ppermute | solution.py:24
  3.8 9.2 %collective-permute-start.1 = (f32[72,256]{1,0:T(8,128)S(1)}, f32[72,256]{1,0:T(8,128)S(1)}, u32[]{:S(2)}, u32[]{:S(2)}) collective-permute-start(f32[72,256]{1,0:T(8,128)S(1)} %get-tuple-element.55), channel_id=1, source_target_pairs={{0,2},{2,0},{4,6},{6,4},{8,10},{10,8},{12,14},{14,12},{16,18},{18,... | collective-permute-start | bytes 221192 | tf_op jit(solution)/shard_map/ppermute | solution.py:24
  5.3 8.0 %collective-permute-start.2 = (f32[72,256]{1,0:T(8,128)S(1)}, f32[72,256]{1,0:T(8,128)S(1)}, u32[]{:S(2)}, u32[]{:S(2)}) collective-permute-start(f32[72,256]{1,0:T(8,128)S(1)} %get-tuple-element.56), channel_id=1, source_target_pairs={{2,4},{4,2},{6,8},{8,6},{10,12},{12,10},{14,16},{16,14},{18,20},{2... | collective-permute-start | bytes 221192 | tf_op jit(solution)/shard_map/ppermute | solution.py:26
  9.5 3.9 %copy-start.1 = (f32[512]{0:T(512)S(1)}, f32[512]{0:T(512)}, u32[]{:S(2)}) copy-start(f32[512]{0:T(512)} %param.19) | copy-start | bytes 6148
  13.4 6.3 %copy-start.2 = (s32[2,512]{1,0:T(2,128)S(1)}, s32[2,512]{1,0:T(2,128)}, u32[]{:S(2)}) copy-start(s32[2,512]{1,0:T(2,128)} %peer_ref.1) | copy-start | bytes 12292
  14.2 1.3 %collective-permute-start.3 = (f32[32,256]{1,0:T(8,128)S(1)}, f32[32,256]{1,0:T(8,128)S(1)}, u32[]{:S(2)}, u32[]{:S(2)}) collective-permute-start(f32[32,256]{1,0:T(8,128)S(1)} %get-tuple-element.65), channel_id=1, source_target_pairs={{0,1},{1,0},{2,3},{3,2},{4,5},{5,4},{6,7},{7,6},{8,9},{9,8},{10,11... | collective-permute-start | bytes 98312 | tf_op jit(solution)/shard_map/ppermute | solution.py:24
  15.5 4.9 %collective-permute-start.4 = (f32[32,256]{1,0:T(8,128)S(1)}, f32[32,256]{1,0:T(8,128)S(1)}, u32[]{:S(2)}, u32[]{:S(2)}) collective-permute-start(f32[32,256]{1,0:T(8,128)S(1)} %get-tuple-element.68), channel_id=1, source_target_pairs={{0,2},{2,0},{4,6},{6,4},{8,10},{10,8},{12,14},{14,12},{16,18},{18,... | collective-permute-start | bytes 98312 | tf_op jit(solution)/shard_map/ppermute | solution.py:24
  16.9 7.6 %collective-permute-start.5 = (f32[32,256]{1,0:T(8,128)S(1)}, f32[32,256]{1,0:T(8,128)S(1)}, u32[]{:S(2)}, u32[]{:S(2)}) collective-permute-start(f32[32,256]{1,0:T(8,128)S(1)} %get-tuple-element.69), channel_id=1, source_target_pairs={{2,4},{4,2},{6,8},{8,6},{10,12},{12,10},{14,16},{16,14},{18,20},{2... | collective-permute-start | bytes 98312 | tf_op jit(solution)/shard_map/ppermute | solution.py:26

commit v4 on v3

--- a/solution.py
+++ b/solution.py
@@ -321,6 +321,18 @@
     return jnp.concatenate([value[i : i + 1, :] for i in range(value.shape[0])], axis=1)
 
 
+def pack_slots(tile, line):
+    rows = as_rows(line, LANES)
+    wide = jnp.concatenate([pltpu.roll(rows, LANES // 2, 1), rows], axis=0)
+    return jnp.where(iota((TILE, LANES), 1) < LANES // 2, tile, wide)
+
+
+def unpack_slots(tile):
+    half = TILE // 2
+    low = iota((half, LANES), 1) < LANES // 2
+    return jnp.where(low, pltpu.roll(tile[:half, :], LANES // 2, 1), tile[half:, :])
+
+
 def as_rows(line, width):
     return jnp.concatenate(
         [line[:, start : start + width] for start in range(0, line.shape[1], width)], axis=0
@@ -351,10 +363,12 @@
     depth_bits = depth.bit_length() - 1
     lay_size = lax.axis_size("lay")
     lay_pairs = len([p for p in pair_lists(lay_size) if p])
-    layer_rows = 4 * cell_cols
-    load_one = (layer_rows + TILE, depth)
-    slot_rows = slots // depth
-    load_two = (cell_cols + 2 * TILE, depth)
+    spans = [slice(start, start + LANES) for start in range(0, depth, LANES)]
+    layer_rows = 4 * len(spans) * cell_cols
+    load_one = (layer_rows + TILE, LANES)
+    edge_size = len(spans) * cell_cols
+    load_two = (edge_size + TILE, LANES)
+    assert slots == TILE * LANES // 2
     block = matrix_source.shape
 
     def is_even(axis):
@@ -389,7 +403,7 @@
         ]
         for i, (there, here) in enumerate(zip(slot_hbm, slot_refs)):
             small_copies.append(pltpu.make_async_copy(there, here, small_sems.at[2 + i]))
-        for pair in copies + [small_copies]:
+        for pair in copies[:1] + [small_copies] + copies[1:]:
             for copy in pair:
                 copy.start()
 
@@ -411,22 +425,24 @@
                     copy.wait()
             return basis_terms(x, source_ref[x], lambda k: basis_ref[k, x])
 
-        tile = restrict_tile((column(x) for x in range(cell_rows)), None, cell_rows, cell_cols)
         for copy in small_copies:
             copy.wait()
         parts = [jnp.zeros((TILE, TILE), F32), widen(cdiag_ref[...])]
         parts = parts + [widen(ratio_ref[d]) for d in range(4)]
         parts.append(jnp.zeros((TILE, LANES - TILE * len(parts)), F32))
         table = jnp.concatenate(parts, axis=1)
+
+        tile = restrict_tile((column(x) for x in range(cell_rows)), None, cell_rows, cell_cols)
         tile = tile + table
         tile_ref[...] = tile
         even = is_even("lay")
         edges = (even * (cell_rows - 1), (1 - even) * (cell_rows - 1))
         for load, edge in zip(loads, edges):
             for k in range(4):
-                load[k * cell_cols : (k + 1) * cell_cols, :] = basis_ref[k, edge]
-            load[layer_rows:, :LANES] = tile
-            load[layer_rows:, LANES:] = jnp.zeros((TILE, depth - LANES), F32)
+                for i, span in enumerate(spans):
+                    start = (k * len(spans) + i) * cell_cols
+                    load[start : start + cell_cols, :] = basis_ref[k, edge, :, span]
+            load[layer_rows:, :] = tile
 
     outs = [(basis.shape, F32), (block, F32), ((TILE, LANES), F32)]
     outs = outs + [(value.shape, value.dtype) for value in slot_arrays]
@@ -469,10 +485,11 @@
         for ref, edge in zip((even_ref, odd_ref), edges):
             for k in range(4):
                 for x in range(cell_rows):
-                    line = k * cell_rows + x
-                    ref[line : line + 1, :] = basis_ref[k, x, pl.ds(edge, 1), :]
-            ref[layer_rows:, :LANES] = joined
-            ref[layer_rows:, LANES:] = jnp.zeros((TILE, depth - LANES), F32)
+                    row = basis_ref[k, x, pl.ds(edge, 1), :]
+                    for i, span in enumerate(spans):
+                        line = (k * len(spans) + i) * cell_rows + x
+                        ref[line : line + 1, :] = row[:, span]
+            ref[layer_rows:, :] = joined
 
     outs = [((TILE, LANES), F32), (load_one, F32), (load_one, F32)]
     joined_one, even_one, odd_one = run(kernel_e, outs, (tile_own, basis, *lay_one))
@@ -515,24 +532,10 @@
     tables = 8
 
     def kernel_q(
-        faces_hbm, accum_hbm, basis_ref, source_ref, row_ref, depth_ref, link_ref, facc_ref,
+        faces_ref, accum_ref, basis_ref, source_ref, row_ref, depth_ref, link_ref, facc_ref,
         trans_ref, count_ref, sface_ref, forward_ref, back_ref, ssource_ref, scale_ref, edge_ref,
-        sedge_ref, frac_ref, faces_ref, accum_ref, linked_ref, sems,
+        sedge_ref, frac_ref, linked_ref,
     ):
-        copies = []
-        for i in range(pieces):
-            part = pl.ds(i * piece, piece)
-            copies.append(
-                (
-                    pltpu.make_async_copy(accum_hbm.at[part], accum_ref.at[part], sems.at[0, i]),
-                    pltpu.make_async_copy(
-                        faces_hbm.at[:, part], faces_ref.at[:, part], sems.at[1, i]
-                    ),
-                )
-            )
-        for pair in copies:
-            for copy in pair:
-                copy.start()
         live = (iota((1, slots), 1) < count_ref[0]).astype(F32)
         couple = live * as_line(link_ref[...])
         frac_diag = as_line(facc_ref[...]) + couple
@@ -545,9 +548,6 @@
         lane = iota((cell_cols, depth), 1)
         place = jnp.bitwise_and(iota((cell_cols, depth), 0), BLOCK - 1)
         for x in range(cell_rows):
-            if x % piece == 0:
-                for copy in copies[x // piece]:
-                    copy.wait()
             diag = accum_ref[x] + linked_ref[x * cell_cols : (x + 1) * cell_cols, :]
             for d in range(6):
                 diag = diag + faces_ref[d, x]
@@ -620,8 +620,8 @@
         kernel_q,
         outs,
         (
-            pltpu.with_memory_space_constraint(faces, pltpu.HBM),
-            pltpu.with_memory_space_constraint(accum, pltpu.HBM),
+            faces,
+            accum,
             basis,
             matrix_source,
             hot_row,
@@ -632,23 +632,26 @@
             frac_count,
         ),
         smem=(9,),
-        scratch=(
-            pltpu.VMEM(faces.shape, F32),
-            pltpu.VMEM(block, F32),
-            pltpu.VMEM((cells, depth), F32),
-            pltpu.SemaphoreType.DMA((2, pieces)),
-        ),
-        in_place=(0, 1),
-    )
-
-    layer = (slice(0, layer_rows), slice(0, depth))
+        scratch=(pltpu.VMEM((cells, depth), F32),),
+    )
+
+    layer = (slice(0, layer_rows), slice(0, LANES))
+
+    def widen_layer(value, start):
+        first = start * edge_size
+        parts = [
+            value[first + i * cell_cols : first + (i + 1) * cell_cols, :]
+            for i in range(len(spans))
+        ]
+        return jnp.concatenate(parts, axis=1)
+
 
     def rims_of(lay_refs, blk_even, blk_odd):
         lay_low, lay_high = lay_sides(lay_refs, layer)
         blk_low, blk_high = blk_sides(blk_even, blk_odd, layer)
 
         def pick(value):
-            return lambda k: value[k * cell_cols : (k + 1) * cell_cols, :]
+            return lambda k: widen_layer(value, k)
 
         return pick(lay_low), pick(lay_high), pick(blk_low), pick(blk_high)
 
@@ -708,11 +711,9 @@
         even = is_even("lay")
         edges = (even * last, (1 - even) * last)
         for load, edge in zip(loads, edges):
-            load[:cell_cols, :] = p2_ref[edge]
-            load[cell_cols : cell_cols + TILE, :LANES] = tile
-            load[cell_cols : cell_cols + TILE, LANES:] = jnp.zeros((TILE, depth - LANES), F32)
-            load[cell_cols + TILE :, :] = jnp.zeros((TILE, depth), F32)
-            load[cell_cols + TILE : cell_cols + TILE + slot_rows, :] = as_rows(fracture, depth)
+            for i, span in enumerate(spans):
+                load[i * cell_cols : (i + 1) * cell_cols, :] = p2_ref[edge, :, span]
+            load[edge_size:, :] = pack_slots(tile, fracture)
 
     parts_shape = (5, TILE, LANES)
     row_pair = (2, cell_rows, depth)
@@ -728,21 +729,19 @@
     )
     lay_two = swap_pairs(loads[0], loads[-1], "lay")
 
-    tile_rows = (slice(cell_cols, cell_cols + TILE), slice(0, LANES))
-    frac_rows = (slice(cell_cols + TILE, cell_cols + TILE + slot_rows), slice(0, depth))
+    tail_rows = (slice(edge_size, edge_size + TILE), slice(0, LANES))
 
     def kernel_f(tile_ref, rows_ref, *refs):
         got, (join_ref, even_ref, odd_ref) = refs[:-3], refs[-3:]
-        low, high = lay_sides(got, tile_rows)
+        low, high = lay_sides(got, tail_rows)
         joined = join_rows(tile_ref[...], low, high)
         join_ref[...] = joined
         even = is_even("blk")
-        even_ref[:cell_cols, :] = rows_ref[even]
-        odd_ref[:cell_cols, :] = rows_ref[1 - even]
-        for ref in (even_ref, odd_ref):
-            ref[cell_cols : cell_cols + TILE, :LANES] = joined
-            ref[cell_cols : cell_cols + TILE, LANES:] = jnp.zeros((TILE, depth - LANES), F32)
-            ref[cell_cols + TILE :, :] = got[0][cell_cols + TILE :, :]
+        tail = jnp.where(iota((TILE, LANES), 1) < LANES // 2, joined, got[0][tail_rows])
+        for ref, side in ((even_ref, even), (odd_ref, 1 - even)):
+            for i, span in enumerate(spans):
+                ref[i * cell_rows : (i + 1) * cell_rows, :] = rows_ref[side, :, span]
+            ref[edge_size:, :] = tail
 
     outs = [((TILE, LANES), F32), (load_two, F32), (load_two, F32)]
     joined_two, even_two, odd_two = run(kernel_f, outs, (tile_two, edge_rows, *lay_two))
@@ -787,7 +786,7 @@
     if lay_size != 2:
         owners = lax.axis_size("blk") * lay_size
         ahead = [(i, i + 1) for i in range(owners - 1)]
-        line = fracture.reshape(slot_rows, depth)
+        line = fracture.reshape(small)
         ring = [
             lax.ppermute(line, ("blk", "lay"), ahead),
             lax.ppermute(line, ("blk", "lay"), [(b, a) for a, b in ahead]),
@@ -801,14 +800,14 @@
         lay_first, lay_second = refs[:lay_pairs], refs[lay_pairs : 2 * lay_pairs]
         ring_refs = refs[2 * lay_pairs : -5]
         p_hbm, f_hbm, p_out, f_out, sems = refs[-5:]
-        low, high = blk_sides(two_even, two_odd, tile_rows)
+        low, high = blk_sides(two_even, two_odd, tail_rows)
         tile = join_lanes(joined_ref[...], low, high)
         second = coarse_solve(tile, [parts_ref[i] for i in range(5)])
         fields = Fields(second, cell_rows, cell_cols)
         x_low, x_high, y_low, y_high = rims_of(lay_first, one_even, one_odd)
-        window = (slice(0, cell_cols), slice(0, depth))
-        p_left, p_right = lay_sides(lay_second, window)
-        p_low, p_high = blk_sides(two_even, two_odd, window)
+        window = (slice(0, edge_size), slice(0, LANES))
+        p_left, p_right = [widen_layer(value, 0) for value in lay_sides(lay_second, window)]
+        p_low, p_high = [widen_layer(value, 0) for value in blk_sides(two_even, two_odd, window)]
 
         left_rim = sface_ref[1, 0] * (p_left + fields.column(-1, x_low))
         right_rim = sface_ref[0, last] * (p_right + fields.column(cell_rows, x_high))
@@ -819,13 +818,12 @@
         if ring_refs:
             before, after = ring_refs[0][...], ring_refs[1][...]
         else:
-            partner = lay_second[0][frac_rows]
-            from_low, from_high = blk_sides(two_even, two_odd, frac_rows)
-            before = by_parity(is_even("lay"), from_low, partner)
-            after = by_parity(is_even("lay"), partner, from_high)
+            partner = lay_second[0][tail_rows]
+            before = unpack_slots(by_parity(is_even("lay"), low, partner))
+            after = unpack_slots(by_parity(is_even("lay"), partner, high))
         width = mine.shape[0]
         wide = jnp.concatenate(
-            [as_rows(as_line(before), LANES), mine, as_rows(as_line(after), LANES)]
+            [before, mine, after]
             + [jnp.zeros((-3 * width % TILE, LANES), F32)] * (3 * width % TILE > 0),
             axis=0,
         )

time: 25.8 us -> 24.6 us (0.953)
  Pallas kernels: 8.22 us -> 7.12 us
    ppermute x4, starting transfers between devices: 3.02 us -> 1.91 us  [swap_pairs(): got = [lax.ppermute(even_load, axis, even)]]
    pallas_call x8, Pallas kernels: 8.22 us -> 7.12 us  [run(): pl.pallas_call(kernel, out_shape=[jax.ShapeDtypeStruct(shape, dtype) for...]
    ppermute x2, starting transfers between devices: 6.03 us -> 6.99 us  [swap_pairs(): got.append(lax.ppermute(odd_load, axis, odd))]
  transfers between devices with their start and end apart: 6 -> 6, of which waited for: 4 -> 4; matrix products, arithmetic and copies ran while one was open for 0% -> 0% of each run, Pallas kernels for 17% -> 13%
where the time goes in v4:
time: 24.6 us; the launch traced here: 24.4 us
  starting transfers between devices  8.9 us (36%)
  Pallas kernels  7.12 us (29%)
  waiting for transfers between devices  6.86 us (28%)
  between operations  1.48 us (6%)
    pallas_call x8, Pallas kernels, run(): pl.pallas_call(kernel, out_shape=[jax.ShapeDtypeStruct(shape, dtype) for...  7.12 us
    ppermute x2, starting transfers between devices, swap_pairs(): got.append(lax.ppermute(odd_load, axis, odd))  6.99 us
    ppermute x2, waiting for transfers between devices, swap_pairs(): got.append(lax.ppermute(odd_load, axis, odd))  4.43 us
    ppermute x4, waiting for transfers between devices, swap_pairs(): got = [lax.ppermute(even_load, axis, even)]  2.43 us
    ppermute x4, starting transfers between devices, swap_pairs(): got = [lax.ppermute(even_load, axis, even)]  1.91 us
  transfers between devices with their start and end apart: 6, of which 4 were waited for; matrix products, arithmetic and copies ran while one was open for 0% of the time, Pallas kernels for 13%

profile of v4, /device:TPU:8, one launch (start us, length us, event | category | flops | bytes accessed | tf_op | source)
XLA Modules:
  0.0 24.4 jit_solution(12218873313197024791)
XLA Ops:
  0.6 0.0 copy-start.5
  0.6 0.0 copy-start.6
  0.7 0.0 copy-start.1
  0.7 0.0 copy-start
  0.7 0.0 copy-start.2
  0.7 1.6 %shard_map.140 = (f32[4,16,16,256]{3,2,1,0:T(8,128)S(1)}, f32[16,16,256]{2,1,0:T(8,128)S(1)}, f32[8,128]{1,0:T(8,128)S(1)}, s32[4,128]{1,0:T(4,128)S(1)}, f32[136,128]{1,0:T(8,128)S(1)}) custom-call(f32[4,16,16,256]{3,2,1,0:T(8,128)} %basis_hbm.1, f32[16,16,256]{2,1,0:T(8,128)} %source_hbm.1, f32[4,4]{1,0:T(4,128)} %cdiag_hbm.1, f32[4,4,4]{2,1,0:T(4,128)} %ratio_hbm.1, ...), custom_call_target="tpu_custom_call" | custom-call | tf_op jit(solution)/shard_map/pallas_call | solution.py:38
  2.3 0.1 collective-permute-start
  2.4 1.2 %collective-permute-done.refs_0_ = f32[136,128]{1,0:T(8,128)S(1)} collective-permute-done((f32[136,128]{1,0:T(8,128)S(1)}, f32[136,128]{1,0:T(8,128)S(1)}, u32[]{:S(2)}, u32[]{:S(2)}) %collective-permute-start) | collective-permute-done | bytes 69664 | tf_op jit(solution)/shard_map/ppermute | solution.py:24
  3.7 0.1 shard_map.143
  3.8 1.6 %collective-permute-start.1 = (f32[136,128]{1,0:T(8,128)S(1)}, f32[136,128]{1,0:T(8,128)S(1)}, u32[]{:S(2)}, u32[]{:S(2)}) collective-permute-start(f32[136,128]{1,0:T(8,128)S(1)} %get-tuple-element.55), channel_id=1, source_target_pairs={{0,2},{2,0},{4,6},{6,4},{8,10},{10,8},{12,14},{14,12},{16,18},{18,... | collective-permute-start | bytes 208904 | tf_op jit(solution)/shard_map/ppermute | solution.py:24
  5.4 3.3 %collective-permute-start.2 = (f32[136,128]{1,0:T(8,128)S(1)}, f32[136,128]{1,0:T(8,128)S(1)}, u32[]{:S(2)}, u32[]{:S(2)}) collective-permute-start(f32[136,128]{1,0:T(8,128)S(1)} %get-tuple-element.56), channel_id=1, source_target_pairs={{2,4},{4,2},{6,8},{8,6},{10,12},{12,10},{14,16},{16,14},{18,20},{2... | collective-permute-start | bytes 208904 | tf_op jit(solution)/shard_map/ppermute | solution.py:26
  8.6 0.9 %shard_map.141 = (bf16[256,512]{1,0:T(8,128)(2,1)S(1)}, bf16[256,512]{1,0:T(8,128)(2,1)S(1)}, bf16[128,1024]{1,0:T(8,128)(2,1)S(1)}, f32[8,1024]{1,0:T(8,128)S(1)}) custom-call(f32[4,16,16,256]{3,2,1,0:T(8,128)S(1)} %get-tuple-element.37.basis_ref, s32[4,128]{1,0:T(4,128)S(1)} %get-tuple-element.39.cell_ref), custom_call_target="tpu_custom_call" | custom-call | tf_op jit(solution)/shard_map/pallas_call | solution.py:38
  9.5 0.0 copy-start.3
  10.2 0.0 copy-done.5
  10.2 0.0 copy-done.6
  10.2 0.0 copy-done.1
  10.2 0.0 copy-done
  10.2 0.0 copy-done.2
  10.3 1.6 %shard_map.142 = (f32[6,16,16,256]{3,2,1,0:T(8,128)S(1)}, f32[8,16,16,256]{3,2,1,0:T(8,128)S(1)}, f32[8,16,16,256]{3,2,1,0:T(8,128)S(1)}, f32[16,16,256]{2,1,0:T...) custom-call(f32[6,16,16,256]{3,2,1,0:T(8,128)S(1)} %copy-done, ...), custom_call_target="tpu_custom_call" | custom-call | tf_op jit(solution)/shard_map/pallas_call | solution.py:38
  11.8 0.0 collective-permute-done.1.blk_even.one_even
  11.9 1.5 %collective-permute-done.2.blk_odd.one_odd = f32[136,128]{1,0:T(8,128)S(1)} collective-permute-done((f32[136,128]{1,0:T(8,128)S(1)}, f32[136,128]{1,0:T(8,128)S(1)}, u32[]{:S(2)}, u32[]{:S(2)}) %collective-permute-start.2) | collective-permute-done | bytes 69664 | tf_op jit(solution)/shard_map/ppermute | solution.py:26
  13.4 0.0 copy-done.3
  13.4 0.0 copy-start.4
  13.4 0.9 %shard_map.144 = (f32[16,16,256]{2,1,0:T(8,128)S(1)}, f32[2,16,256]{2,1,0:T(8,128)S(1)}, f32[1,512]{1,0:T(1,128)S(1)}, f32[8,128]{1,0:T(8,128)S(1)}, f32[5,8,128]{2,1,0:T(8,128)S(1)}, /*index=5*/f32[40,128]{1,0:T(8,128)S(1)}) custom-call(f32[6,16,16,256]{3,2,1,0:T(8,128)S(1)} %get-tuple-element.42.sface_ref, ...), custom_call_target="tpu_custom_call" | custom-call | tf_op jit(solution)/shard_map/pallas_call | solution.py:38
  14.2 0.1 collective-permute-start.3
  14.3 1.2 %collective-permute-done.3.refs_0_.refs_1_ = f32[40,128]{1,0:T(8,128)S(1)} collective-permute-done((f32[40,128]{1,0:T(8,128)S(1)}, f32[40,128]{1,0:T(8,128)S(1)}, u32[]{:S(2)}, u32[]{:S(2)}) %collective-permute-start.3) | collective-permute-done | bytes 20512 | tf_op jit(solution)/shard_map/ppermute | solution.py:24
  15.5 0.2 collective-permute-start.4
  15.7 3.7 %collective-permute-start.5 = (f32[40,128]{1,0:T(8,128)S(1)}, f32[40,128]{1,0:T(8,128)S(1)}, u32[]{:S(2)}, u32[]{:S(2)}) collective-permute-start(f32[40,128]{1,0:T(8,128)S(1)} %get-tuple-element.69), channel_id=1, source_target_pairs={{2,4},{4,2},{6,8},{8,6},{10,12},{12,10},{14,16},{16,14},{18,20},{2... | collective-permute-start | bytes 61448 | tf_op jit(solution)/shard_map/ppermute | solution.py:26
  19.4 0.0 copy-done.4
  19.5 0.8 %shard_map.145 = (f32[16,16,256]{2,1,0:T(8,128)S(1)}, f32[1,512]{1,0:T(1,128)S(1)}, s32[1,1024]{1,0:T(1,128)S(1)}, bf16[128,1024]{1,0:T(8,128)(2,1)S(1)}) custom-call(f32[6,16,16,256]{3,2,1,0:T(8,128)S(1)} %get-tuple-element.42.sface_ref, f32[16,16,256]{2,1,0:T(8,128)S(1)} %get-tuple-element.44.ssource_ref, f32[16,16,256]{2,1,0:T(8,128)S(1)} %get-tuple-element.45.scale_ref, ...), custom_call_target="tpu_custom_call" | custom-call | tf_op jit(solution)/shard_map/pallas_call | solution.py:38
  20.2 0.0 collective-permute-done.4.two_even
  20.3 2.9 %collective-permute-done.5.two_odd = f32[40,128]{1,0:T(8,128)S(1)} collective-permute-done((f32[40,128]{1,0:T(8,128)S(1)}, f32[40,128]{1,0:T(8,128)S(1)}, u32[]{:S(2)}, u32[]{:S(2)}) %collective-permute-start.5) | collective-permute-done | bytes 20512 | tf_op jit(solution)/shard_map/ppermute | solution.py:26
  23.2 1.2 %shard_map.147 = (f32[16,16,256]{2,1,0:T(8,128)}, f32[4,128]{1,0:T(4,128)}) custom-call(f32[6,16,16,256]{3,2,1,0:T(8,128)S(1)} %get-tuple-element.42.sface_ref, f32[8,16,16,256]{3,2,1,0:T(8,128)S(1)} %get-tuple-element.43.forward_ref, f32[16,16,256]{2,1,0:T(8,128)S(1)} %get-tuple-element.59.base_ref, f32[2,16,256]{2,1,0:T(8,128)S(1)} %get-tuple-element.48.sedge_ref, ...), custom_call_target="tpu_custom_call" | custom-call | tf_op jit(solution)/shard_map/pallas_call | solution.py:38
  (1 shorter events, 0.0 us)
Async XLA Ops:
  0.6 9.6 %copy-start.5 = (f32[512]{0:T(512)S(1)}, f32[512]{0:T(512)}, u32[]{:S(2)}) copy-start(f32[512]{0:T(512)} %param.21) | copy-start | bytes 6148
  0.6 9.6 %copy-start.6 = (f32[512]{0:T(512)S(1)}, f32[512]{0:T(512)}, u32[]{:S(2)}) copy-start(f32[512]{0:T(512)} %param.20) | copy-start | bytes 6148
  0.7 9.6 %copy-start.1 = (f32[16,16,256]{2,1,0:T(8,128)S(1)}, f32[16,16,256]{2,1,0:T(8,128)}, u32[]{:S(2)}) copy-start(f32[16,16,256]{2,1,0:T(8,128)} %accum_ref.1) | copy-start | bytes 786436
  0.7 9.6 %copy-start = (f32[6,16,16,256]{3,2,1,0:T(8,128)S(1)}, f32[6,16,16,256]{3,2,1,0:T(8,128)}, u32[]{:S(2)}) copy-start(f32[6,16,16,256]{3,2,1,0:T(8,128)} %faces_ref.1) | copy-start | bytes 4718596
  0.7 9.6 %copy-start.2 = (f32[2,512]{1,0:T(2,128)S(1)}, f32[2,512]{1,0:T(2,128)}, u32[]{:S(2)}) copy-start(f32[2,512]{1,0:T(2,128)} %trans_ref.3) | copy-start | bytes 12292
  2.3 1.3 %collective-permute-start = (f32[136,128]{1,0:T(8,128)S(1)}, f32[136,128]{1,0:T(8,128)S(1)}, u32[]{:S(2)}, u32[]{:S(2)}) collective-permute-start(f32[136,128]{1,0:T(8,128)S(1)} %get-tuple-element.53), channel_id=1, source_target_pairs={{0,1},{1,0},{2,3},{3,2},{4,5},{5,4},{6,7},{7,6},{8,9},{9,8},{10,11... | collective-permute-start | bytes 208904 | tf_op jit(solution)/shard_map/ppermute | solution.py:24
  3.8 8.0 %collective-permute-start.1 = (f32[136,128]{1,0:T(8,128)S(1)}, f32[136,128]{1,0:T(8,128)S(1)}, u32[]{:S(2)}, u32[]{:S(2)}) collective-permute-start(f32[136,128]{1,0:T(8,128)S(1)} %get-tuple-element.55), channel_id=1, source_target_pairs={{0,2},{2,0},{4,6},{6,4},{8,10},{10,8},{12,14},{14,12},{16,18},{18,... | collective-permute-start | bytes 208904 | tf_op jit(solution)/shard_map/ppermute | solution.py:24
  5.4 8.0 %collective-permute-start.2 = (f32[136,128]{1,0:T(8,128)S(1)}, f32[136,128]{1,0:T(8,128)S(1)}, u32[]{:S(2)}, u32[]{:S(2)}) collective-permute-start(f32[136,128]{1,0:T(8,128)S(1)} %get-tuple-element.56), channel_id=1, source_target_pairs={{2,4},{4,2},{6,8},{8,6},{10,12},{12,10},{14,16},{16,14},{18,20},{2... | collective-permute-start | bytes 208904 | tf_op jit(solution)/shard_map/ppermute | solution.py:26
  9.5 3.8 %copy-start.3 = (f32[512]{0:T(512)S(1)}, f32[512]{0:T(512)}, u32[]{:S(2)}) copy-start(f32[512]{0:T(512)} %param.19) | copy-start | bytes 6148
  13.4 6.1 %copy-start.4 = (s32[2,512]{1,0:T(2,128)S(1)}, s32[2,512]{1,0:T(2,128)}, u32[]{:S(2)}) copy-start(s32[2,512]{1,0:T(2,128)} %peer_ref.1) | copy-start | bytes 12292
  14.2 1.3 %collective-permute-start.3 = (f32[40,128]{1,0:T(8,128)S(1)}, f32[40,128]{1,0:T(8,128)S(1)}, u32[]{:S(2)}, u32[]{:S(2)}) collective-permute-start(f32[40,128]{1,0:T(8,128)S(1)} %get-tuple-element.65), channel_id=1, source_target_pairs={{0,1},{1,0},{2,3},{3,2},{4,5},{5,4},{6,7},{7,6},{8,9},{9,8},{10,11... | collective-permute-start | bytes 61448 | tf_op jit(solution)/shard_map/ppermute | solution.py:24
  15.5 4.7 %collective-permute-start.4 = (f32[40,128]{1,0:T(8,128)S(1)}, f32[40,128]{1,0:T(8,128)S(1)}, u32[]{:S(2)}, u32[]{:S(2)}) collective-permute-start(f32[40,128]{1,0:T(8,128)S(1)} %get-tuple-element.68), channel_id=1, source_target_pairs={{0,2},{2,0},{4,6},{6,4},{8,10},{10,8},{12,14},{14,12},{16,18},{18,... | collective-permute-start | bytes 61448 | tf_op jit(solution)/shard_map/ppermute | solution.py:24
  15.7 7.5 %collective-permute-start.5 = (f32[40,128]{1,0:T(8,128)S(1)}, f32[40,128]{1,0:T(8,128)S(1)}, u32[]{:S(2)}, u32[]{:S(2)}) collective-permute-start(f32[40,128]{1,0:T(8,128)S(1)} %get-tuple-element.69), channel_id=1, source_target_pairs={{2,4},{4,2},{6,8},{8,6},{10,12},{12,10},{14,16},{16,14},{18,20},{2... | collective-permute-start | bytes 61448 | tf_op jit(solution)/shard_map/ppermute | solution.py:26

commit v5 on v4

--- a/solution.py
+++ b/solution.py
@@ -27,7 +27,7 @@
     return got
 
 
-def run(kernel, outs, args, scratch=(), smem=(), in_place=(), out_place=()):
+def run(kernel, outs, args, scratch=(), smem=(), in_place=(), out_place=(), aliases={}):
     spec = pl.BlockSpec(memory_space=pltpu.VMEM)
     scalar = pl.BlockSpec(memory_space=pltpu.SMEM)
     there = pl.BlockSpec(memory_space=pltpu.HBM)
@@ -41,6 +41,7 @@
         in_specs=[place(i) for i in range(len(args))],
         out_specs=[there if i in out_place else spec for i in range(len(outs))],
         scratch_shapes=list(scratch),
+        input_output_aliases=aliases,
         compiler_params=pltpu.CompilerParams(vmem_limit_bytes=24 << 20),
     )(*args)
 
@@ -309,11 +310,9 @@
     return total[:, :half] + total[:, half:]
 
 
-def slots_at_nodes(values, hot_node, node_weight):
+def slots_at_nodes(values, node_hot, node_weight):
     weighted = node_weight * jnp.concatenate([values, values], axis=1)
-    product = lax.dot_general(
-        stacked([weighted]), hot_node, (((1,), (1,)), ((), ())), preferred_element_type=F32
-    )
+    product = jnp.dot(stacked([weighted]), node_hot, preferred_element_type=F32)
     return unstack(product, TILE)[0]
 
 
@@ -385,6 +384,7 @@
         slot_hbm, refs = refs[:slot_kinds], refs[slot_kinds:]
         (basis_ref, source_ref, tile_ref), refs = refs[:3], refs[3:]
         slot_refs, refs = refs[:slot_kinds], refs[slot_kinds:]
+        rim_refs, refs = refs[:2], refs[2:]
         loads, (cdiag_ref, ratio_ref, sems, small_sems) = refs[:-4], refs[-4:]
         copies = []
         for i in range(pieces):
@@ -419,10 +419,19 @@
             edge = jnp.zeros((2, TILE), F32)
             return jnp.concatenate([edge, lines, edge], axis=0)
 
+        blk_even = is_even("blk")
+        rim_edges = (blk_even * (cell_cols - 1), (1 - blk_even) * (cell_cols - 1))
+
         def column(x):
             if x % piece == 0:
                 for copy in copies[x // piece]:
                     copy.wait()
+            for ref, edge in zip(rim_refs, rim_edges):
+                for k in range(4):
+                    row = basis_ref[k, x, pl.ds(edge, 1), :]
+                    for i, span in enumerate(spans):
+                        line = (k * len(spans) + i) * cell_rows + x
+                        ref[line : line + 1, :] = row[:, span]
             return basis_terms(x, source_ref[x], lambda k: basis_ref[k, x])
 
         for copy in small_copies:
@@ -446,7 +455,7 @@
 
     outs = [(basis.shape, F32), (block, F32), ((TILE, LANES), F32)]
     outs = outs + [(value.shape, value.dtype) for value in slot_arrays]
-    outs = outs + [(load_one, F32)] * lay_pairs
+    outs = outs + [(load_one, F32)] * (2 + lay_pairs)
     basis, matrix_source, tile_own, *rest = run(
         kernel_a,
         outs,
@@ -462,7 +471,7 @@
         ),
         in_place=range(4 + slot_kinds),
     )
-    slot_cell, *loads = rest
+    slot_cell, rim_even, rim_odd, *loads = rest
     slot_source = frac_source.reshape(small)
     lay_one = swap_pairs(loads[0], loads[-1], "lay")
 
@@ -475,24 +484,18 @@
     def blk_sides(even_ref, odd_ref, window):
         return low_high(is_even("blk"), even_ref[window], odd_ref[window])
 
-    def kernel_e(tile_ref, basis_ref, *refs):
+    def kernel_e(tile_ref, rim_even_ref, rim_odd_ref, *refs):
         got, (join_ref, even_ref, odd_ref) = refs[:-3], refs[-3:]
         low, high = lay_sides(got, (slice(layer_rows, layer_rows + TILE), slice(0, LANES)))
         joined = join_rows(tile_ref[...], low, high)
         join_ref[...] = joined
-        even = is_even("blk")
-        edges = (even * (cell_cols - 1), (1 - even) * (cell_cols - 1))
-        for ref, edge in zip((even_ref, odd_ref), edges):
-            for k in range(4):
-                for x in range(cell_rows):
-                    row = basis_ref[k, x, pl.ds(edge, 1), :]
-                    for i, span in enumerate(spans):
-                        line = (k * len(spans) + i) * cell_rows + x
-                        ref[line : line + 1, :] = row[:, span]
-            ref[layer_rows:, :] = joined
+        even_ref[layer_rows:, :] = joined
+        odd_ref[layer_rows:, :] = joined
 
     outs = [((TILE, LANES), F32), (load_one, F32), (load_one, F32)]
-    joined_one, even_one, odd_one = run(kernel_e, outs, (tile_own, basis, *lay_one))
+    joined_one, even_one, odd_one = run(
+        kernel_e, outs, (tile_own, rim_even, rim_odd, *lay_one), aliases={1: 1, 2: 2}
+    )
     blk_one = swap_pairs(even_one, odd_one, "blk")
 
     links = frac_trans.shape[0]
@@ -533,9 +536,10 @@
 
     def kernel_q(
         faces_ref, accum_ref, basis_ref, source_ref, row_ref, depth_ref, link_ref, facc_ref,
-        trans_ref, count_ref, sface_ref, forward_ref, back_ref, ssource_ref, scale_ref, edge_ref,
-        sedge_ref, frac_ref, linked_ref,
+        trans_ref, node_ref, count_ref, sface_ref, forward_ref, back_ref, ssource_ref, scale_ref, edge_ref,
+        sedge_ref, frac_ref, turned_ref, linked_ref,
     ):
+        turned_ref[...] = node_ref[...].astype(F32).T.astype(BF16)
         live = (iota((1, slots), 1) < count_ref[0]).astype(F32)
         couple = live * as_line(link_ref[...])
         frac_diag = as_line(facc_ref[...]) + couple
@@ -615,8 +619,9 @@
         ((4, cell_cols, depth), F32),
         ((2, cell_rows, depth), F32),
         ((TILE, slots), F32),
+        ((2 * slots, LANES), BF16),
     ]
-    sfaces, forward, back, ssource, scale, edge_faces, sedges, frac_pack = run(
+    sfaces, forward, back, ssource, scale, edge_faces, sedges, frac_pack, node_hot = run(
         kernel_q,
         outs,
         (
@@ -629,9 +634,10 @@
             frac_link.reshape(small),
             frac_accum.reshape(small),
             frac_trans,
+            hot_node,
             frac_count,
         ),
-        smem=(9,),
+        smem=(10,),
         scratch=(pltpu.VMEM((cells, depth), F32),),
     )
 
@@ -658,8 +664,8 @@
     last = cell_rows - 1
 
     def kernel_b(
-        sface_ref, forward_ref, back_ref, ssource_ref, edge_ref, sedge_ref, node_ref, weight_ref,
-        frac_ref, fsrc_ref, own_ref, joined_ref, blk_even, blk_odd, *refs,
+        sface_ref, forward_ref, back_ref, ssource_ref, edge_ref, sedge_ref, node_ref, turned_ref,
+        weight_ref, frac_ref, fsrc_ref, own_ref, joined_ref, blk_even, blk_odd, *refs,
     ):
         lay_refs = refs[:lay_pairs]
         p2_ref, rows_ref, f_ref, tile_ref, parts_ref = refs[lay_pairs : lay_pairs + 5]
@@ -682,7 +688,7 @@
         pressure_at = nodes_at_slots(second, node_ref[...], weight_ref[...])
         fracture = frac_ref[1:2, :] * (as_line(fsrc_ref[...]) + couple * pressure_at)
         f_ref[...] = fracture
-        linked = slots_at_nodes(couple * fracture, node_ref[...], weight_ref[...])
+        linked = slots_at_nodes(couple * fracture, turned_ref[...], weight_ref[...])
 
         def columns():
             for x in range(cell_rows):
@@ -723,8 +729,8 @@
         kernel_b,
         outs,
         (
-            sfaces, forward, back, ssource, edge_faces, sedges, hot_node, node_weight,
-            frac_pack, slot_source, tile_own, joined_one, *blk_one, *lay_one,
+            sfaces, forward, back, ssource, edge_faces, sedges, hot_node, node_hot,
+            node_weight, frac_pack, slot_source, tile_own, joined_one, *blk_one, *lay_one,
         ),
     )
     lay_two = swap_pairs(loads[0], loads[-1], "lay")

time: 24.6 us -> 24.5 us (level)
  transfers between devices with their start and end apart: 6 -> 6, of which waited for: 4 -> 4; matrix products, arithmetic and copies ran while one was open for 0% -> 0% of each run, Pallas kernels for 13% -> 14%
where the time goes in v5:
time: 24.5 us; the launch traced here: 24.4 us
  starting transfers between devices  8.9 us (36%)
  Pallas kernels  7.11 us (29%)
  waiting for transfers between devices  6.85 us (28%)
  between operations  1.47 us (6%)
    pallas_call x8, Pallas kernels, run(): pl.pallas_call(kernel, out_shape=[jax.ShapeDtypeStruct(shape, dtype) for...  7.11 us
    ppermute x2, starting transfers between devices, swap_pairs(): got.append(lax.ppermute(odd_load, axis, odd))  6.93 us
    ppermute x2, waiting for transfers between devices, swap_pairs(): got.append(lax.ppermute(odd_load, axis, odd))  4.43 us
    ppermute x4, waiting for transfers between devices, swap_pairs(): got = [lax.ppermute(even_load, axis, even)]  2.43 us
    ppermute x4, starting transfers between devices, swap_pairs(): got = [lax.ppermute(even_load, axis, even)]  1.97 us
  transfers between devices with their start and end apart: 6, of which 4 were waited for; matrix products, arithmetic and copies ran while one was open for 0% of the time, Pallas kernels for 14%

profile of v5, /device:TPU:8, one launch (start us, length us, event | category | flops | bytes accessed | tf_op | source)
XLA Modules:
  0.0 24.4 jit_solution(27744901636950998)
XLA Ops:
  0.6 0.0 copy-start.5
  0.6 0.0 copy-start.6
  0.7 0.0 copy-start.1
  0.7 0.0 copy-start
  0.7 0.0 copy-start.2
  0.7 1.7 %shard_map.140 = (f32[4,16,16,256]{3,2,1,0:T(8,128)S(1)}, f32[16,16,256]{2,1,0:T(8,128)S(1)}, f32[8,128]{1,0:T(8,128)S(1)}, s32[4,128]{1,0:T(4,128)S(1)}, f32[13...) custom-call(f32[4,16,16,256]{3,2,1,0:T(8,128)} %basis_hbm.1, f32[16,16,256]{2,1,0:T(8,128)} %source_hbm.1, ...), custom_call_target="tpu_custom_call" | custom-call | tf_op jit(solution)/shard_map/pallas_call | solution.py:38
  2.4 0.1 collective-permute-start
  2.5 1.2 %collective-permute-done.refs_0_ = f32[136,128]{1,0:T(8,128)S(1)} collective-permute-done((f32[136,128]{1,0:T(8,128)S(1)}, f32[136,128]{1,0:T(8,128)S(1)}, u32[]{:S(2)}, u32[]{:S(2)}) %collective-permute-start) | collective-permute-done | bytes 69664 | tf_op jit(solution)/shard_map/ppermute | solution.py:24
  3.7 1.6 %collective-permute-start.1 = (f32[136,128]{1,0:T(8,128)S(1)}, f32[136,128]{1,0:T(8,128)S(1)}, u32[]{:S(2)}, u32[]{:S(2)}) collective-permute-start(f32[136,128]{1,0:T(8,128)S(1)} %get-tuple-element.61), channel_id=1, source_target_pairs={{0,2},{2,0},{4,6},{6,4},{8,10},{10,8},{12,14},{14,12},{16,18},{18,... | collective-permute-start | bytes 208904 | tf_op jit(solution)/shard_map/ppermute | solution.py:24
  5.3 3.3 %collective-permute-start.2 = (f32[136,128]{1,0:T(8,128)S(1)}, f32[136,128]{1,0:T(8,128)S(1)}, u32[]{:S(2)}, u32[]{:S(2)}) collective-permute-start(f32[136,128]{1,0:T(8,128)S(1)} %get-tuple-element.62), channel_id=1, source_target_pairs={{2,4},{4,2},{6,8},{8,6},{10,12},{12,10},{14,16},{16,14},{18,20},{2... | collective-permute-start | bytes 208904 | tf_op jit(solution)/shard_map/ppermute | solution.py:26
  9.2 0.9 %shard_map.141 = (bf16[256,512]{1,0:T(8,128)(2,1)S(1)}, bf16[256,512]{1,0:T(8,128)(2,1)S(1)}, bf16[128,1024]{1,0:T(8,128)(2,1)S(1)}, f32[8,1024]{1,0:T(8,128)S(1)}) custom-call(f32[4,16,16,256]{3,2,1,0:T(8,128)S(1)} %get-tuple-element.40.basis_ref, s32[4,128]{1,0:T(4,128)S(1)} %get-tuple-element.42.cell_ref), custom_call_target="tpu_custom_call" | custom-call | tf_op jit(solution)/shard_map/pallas_call | solution.py:38
  10.1 0.0 copy-start.3
  10.1 0.0 copy-done.5
  10.1 0.0 copy-done.6
  10.1 0.0 copy-done.1
  10.2 0.0 copy-done
  10.2 0.0 copy-done.2
  10.2 1.6 %shard_map.142 = (f32[6,16,16,256]{3,2,1,0:T(8,128)S(1)}, f32[8,16,16,256]{3,2,1,0:T(8,128)S(1)}, f32[8,16,16,256]{3,2,1,0:T(8,128)S(1)}, f32[16,16,256]{2,1,0:T...) custom-call(f32[6,16,16,256]{3,2,1,0:T(8,128)S(1)} %copy-done, ...), custom_call_target="tpu_custom_call" | custom-call | tf_op jit(solution)/shard_map/pallas_call | solution.py:38
  11.8 0.0 collective-permute-done.1.blk_even.one_even
  11.8 1.4 %collective-permute-done.2.blk_odd.one_odd = f32[136,128]{1,0:T(8,128)S(1)} collective-permute-done((f32[136,128]{1,0:T(8,128)S(1)}, f32[136,128]{1,0:T(8,128)S(1)}, u32[]{:S(2)}, u32[]{:S(2)}) %collective-permute-start.2) | collective-permute-done | bytes 69664 | tf_op jit(solution)/shard_map/ppermute | solution.py:26
  13.3 0.0 copy-done.3
  13.3 0.0 copy-start.4
  13.3 0.9 %shard_map.144 = (f32[16,16,256]{2,1,0:T(8,128)S(1)}, f32[2,16,256]{2,1,0:T(8,128)S(1)}, f32[1,512]{1,0:T(1,128)S(1)}, f32[8,128]{1,0:T(8,128)S(1)}, f32[5,8,128]{2,1,0:T(8,128)S(1)}, /*index=5*/f32[40,128]{1,0:T(8,128)S(1)}) custom-call(f32[6,16,16,256]{3,2,1,0:T(8,128)S(1)} %get-tuple-element.46.sface_ref, ...), custom_call_target="tpu_custom_call" | custom-call | tf_op jit(solution)/shard_map/pallas_call | solution.py:38
  14.2 0.1 collective-permute-start.3
  14.3 1.2 %collective-permute-done.3.refs_0_.refs_1_ = f32[40,128]{1,0:T(8,128)S(1)} collective-permute-done((f32[40,128]{1,0:T(8,128)S(1)}, f32[40,128]{1,0:T(8,128)S(1)}, u32[]{:S(2)}, u32[]{:S(2)}) %collective-permute-start.3) | collective-permute-done | bytes 20512 | tf_op jit(solution)/shard_map/ppermute | solution.py:24
  15.4 0.3 %collective-permute-start.4 = (f32[40,128]{1,0:T(8,128)S(1)}, f32[40,128]{1,0:T(8,128)S(1)}, u32[]{:S(2)}, u32[]{:S(2)}) collective-permute-start(f32[40,128]{1,0:T(8,128)S(1)} %get-tuple-element.74), channel_id=1, source_target_pairs={{0,2},{2,0},{4,6},{6,4},{8,10},{10,8},{12,14},{14,12},{16,18},{18,... | collective-permute-start | bytes 61448 | tf_op jit(solution)/shard_map/ppermute | solution.py:24
  15.7 3.7 %collective-permute-start.5 = (f32[40,128]{1,0:T(8,128)S(1)}, f32[40,128]{1,0:T(8,128)S(1)}, u32[]{:S(2)}, u32[]{:S(2)}) collective-permute-start(f32[40,128]{1,0:T(8,128)S(1)} %get-tuple-element.75), channel_id=1, source_target_pairs={{2,4},{4,2},{6,8},{8,6},{10,12},{12,10},{14,16},{16,14},{18,20},{2... | collective-permute-start | bytes 61448 | tf_op jit(solution)/shard_map/ppermute | solution.py:26
  19.4 0.0 copy-done.4
  19.4 0.8 %shard_map.145 = (f32[16,16,256]{2,1,0:T(8,128)S(1)}, f32[1,512]{1,0:T(1,128)S(1)}, s32[1,1024]{1,0:T(1,128)S(1)}, bf16[128,1024]{1,0:T(8,128)(2,1)S(1)}) custom-call(f32[6,16,16,256]{3,2,1,0:T(8,128)S(1)} %get-tuple-element.46.sface_ref, f32[16,16,256]{2,1,0:T(8,128)S(1)} %get-tuple-element.48.ssource_ref, f32[16,16,256]{2,1,0:T(8,128)S(1)} %get-tuple-element.49.scale_ref, ...), custom_call_target="tpu_custom_call" | custom-call | tf_op jit(solution)/shard_map/pallas_call | solution.py:38
  20.2 0.0 collective-permute-done.4.two_even
  20.2 3.0 %collective-permute-done.5.two_odd = f32[40,128]{1,0:T(8,128)S(1)} collective-permute-done((f32[40,128]{1,0:T(8,128)S(1)}, f32[40,128]{1,0:T(8,128)S(1)}, u32[]{:S(2)}, u32[]{:S(2)}) %collective-permute-start.5) | collective-permute-done | bytes 20512 | tf_op jit(solution)/shard_map/ppermute | solution.py:26
  23.2 1.2 %shard_map.147 = (f32[16,16,256]{2,1,0:T(8,128)}, f32[4,128]{1,0:T(4,128)}) custom-call(f32[6,16,16,256]{3,2,1,0:T(8,128)S(1)} %get-tuple-element.46.sface_ref, f32[8,16,16,256]{3,2,1,0:T(8,128)S(1)} %get-tuple-element.47.forward_ref, f32[16,16,256]{2,1,0:T(8,128)S(1)} %get-tuple-element.65.base_ref, f32[2,16,256]{2,1,0:T(8,128)S(1)} %get-tuple-element.52.sedge_ref, ...), custom_call_target="tpu_custom_call" | custom-call | tf_op jit(solution)/shard_map/pallas_call | solution.py:38
  (2 shorter events, 0.0 us)
Async XLA Ops:
  0.6 9.5 %copy-start.5 = (f32[512]{0:T(512)S(1)}, f32[512]{0:T(512)}, u32[]{:S(2)}) copy-start(f32[512]{0:T(512)} %param.21) | copy-start | bytes 6148
  0.6 9.5 %copy-start.6 = (f32[512]{0:T(512)S(1)}, f32[512]{0:T(512)}, u32[]{:S(2)}) copy-start(f32[512]{0:T(512)} %param.20) | copy-start | bytes 6148
  0.7 9.5 %copy-start.1 = (f32[16,16,256]{2,1,0:T(8,128)S(1)}, f32[16,16,256]{2,1,0:T(8,128)}, u32[]{:S(2)}) copy-start(f32[16,16,256]{2,1,0:T(8,128)} %accum_ref.1) | copy-start | bytes 786436
  0.7 9.5 %copy-start = (f32[6,16,16,256]{3,2,1,0:T(8,128)S(1)}, f32[6,16,16,256]{3,2,1,0:T(8,128)}, u32[]{:S(2)}) copy-start(f32[6,16,16,256]{3,2,1,0:T(8,128)} %faces_ref.1) | copy-start | bytes 4718596
  0.7 9.5 %copy-start.2 = (f32[2,512]{1,0:T(2,128)S(1)}, f32[2,512]{1,0:T(2,128)}, u32[]{:S(2)}) copy-start(f32[2,512]{1,0:T(2,128)} %trans_ref.3) | copy-start | bytes 12292
  2.4 1.3 %collective-permute-start = (f32[136,128]{1,0:T(8,128)S(1)}, f32[136,128]{1,0:T(8,128)S(1)}, u32[]{:S(2)}, u32[]{:S(2)}) collective-permute-start(f32[136,128]{1,0:T(8,128)S(1)} %get-tuple-element.59), channel_id=1, source_target_pairs={{0,1},{1,0},{2,3},{3,2},{4,5},{5,4},{6,7},{7,6},{8,9},{9,8},{10,11... | collective-permute-start | bytes 208904 | tf_op jit(solution)/shard_map/ppermute | solution.py:24
  3.7 8.1 %collective-permute-start.1 = (f32[136,128]{1,0:T(8,128)S(1)}, f32[136,128]{1,0:T(8,128)S(1)}, u32[]{:S(2)}, u32[]{:S(2)}) collective-permute-start(f32[136,128]{1,0:T(8,128)S(1)} %get-tuple-element.61), channel_id=1, source_target_pairs={{0,2},{2,0},{4,6},{6,4},{8,10},{10,8},{12,14},{14,12},{16,18},{18,... | collective-permute-start | bytes 208904 | tf_op jit(solution)/shard_map/ppermute | solution.py:24
  5.3 8.0 %collective-permute-start.2 = (f32[136,128]{1,0:T(8,128)S(1)}, f32[136,128]{1,0:T(8,128)S(1)}, u32[]{:S(2)}, u32[]{:S(2)}) collective-permute-start(f32[136,128]{1,0:T(8,128)S(1)} %get-tuple-element.62), channel_id=1, source_target_pairs={{2,4},{4,2},{6,8},{8,6},{10,12},{12,10},{14,16},{16,14},{18,20},{2... | collective-permute-start | bytes 208904 | tf_op jit(solution)/shard_map/ppermute | solution.py:26
  10.1 3.2 %copy-start.3 = (f32[512]{0:T(512)S(1)}, f32[512]{0:T(512)}, u32[]{:S(2)}) copy-start(f32[512]{0:T(512)} %param.19) | copy-start | bytes 6148
  13.3 6.1 %copy-start.4 = (s32[2,512]{1,0:T(2,128)S(1)}, s32[2,512]{1,0:T(2,128)}, u32[]{:S(2)}) copy-start(s32[2,512]{1,0:T(2,128)} %peer_ref.1) | copy-start | bytes 12292
  14.2 1.3 %collective-permute-start.3 = (f32[40,128]{1,0:T(8,128)S(1)}, f32[40,128]{1,0:T(8,128)S(1)}, u32[]{:S(2)}, u32[]{:S(2)}) collective-permute-start(f32[40,128]{1,0:T(8,128)S(1)} %get-tuple-element.71), channel_id=1, source_target_pairs={{0,1},{1,0},{2,3},{3,2},{4,5},{5,4},{6,7},{7,6},{8,9},{9,8},{10,11... | collective-permute-start | bytes 61448 | tf_op jit(solution)/shard_map/ppermute | solution.py:24
  15.4 4.7 %collective-permute-start.4 = (f32[40,128]{1,0:T(8,128)S(1)}, f32[40,128]{1,0:T(8,128)S(1)}, u32[]{:S(2)}, u32[]{:S(2)}) collective-permute-start(f32[40,128]{1,0:T(8,128)S(1)} %get-tuple-element.74), channel_id=1, source_target_pairs={{0,2},{2,0},{4,6},{6,4},{8,10},{10,8},{12,14},{14,12},{16,18},{18,... | collective-permute-start | bytes 61448 | tf_op jit(solution)/shard_map/ppermute | solution.py:24
  15.7 7.5 %collective-permute-start.5 = (f32[40,128]{1,0:T(8,128)S(1)}, f32[40,128]{1,0:T(8,128)S(1)}, u32[]{:S(2)}, u32[]{:S(2)}) collective-permute-start(f32[40,128]{1,0:T(8,128)S(1)} %get-tuple-element.75), channel_id=1, source_target_pairs={{2,4},{4,2},{6,8},{8,6},{10,12},{12,10},{14,16},{16,14},{18,20},{2... | collective-permute-start | bytes 61448 | tf_op jit(solution)/shard_map/ppermute | solution.py:26

commit v6 on v5

--- a/solution.py
+++ b/solution.py
@@ -384,7 +384,6 @@
         slot_hbm, refs = refs[:slot_kinds], refs[slot_kinds:]
         (basis_ref, source_ref, tile_ref), refs = refs[:3], refs[3:]
         slot_refs, refs = refs[:slot_kinds], refs[slot_kinds:]
-        rim_refs, refs = refs[:2], refs[2:]
         loads, (cdiag_ref, ratio_ref, sems, small_sems) = refs[:-4], refs[-4:]
         copies = []
         for i in range(pieces):
@@ -419,19 +418,10 @@
             edge = jnp.zeros((2, TILE), F32)
             return jnp.concatenate([edge, lines, edge], axis=0)
 
-        blk_even = is_even("blk")
-        rim_edges = (blk_even * (cell_cols - 1), (1 - blk_even) * (cell_cols - 1))
-
         def column(x):
             if x % piece == 0:
                 for copy in copies[x // piece]:
                     copy.wait()
-            for ref, edge in zip(rim_refs, rim_edges):
-                for k in range(4):
-                    row = basis_ref[k, x, pl.ds(edge, 1), :]
-                    for i, span in enumerate(spans):
-                        line = (k * len(spans) + i) * cell_rows + x
-                        ref[line : line + 1, :] = row[:, span]
             return basis_terms(x, source_ref[x], lambda k: basis_ref[k, x])
 
         for copy in small_copies:
@@ -455,7 +445,7 @@
 
     outs = [(basis.shape, F32), (block, F32), ((TILE, LANES), F32)]
     outs = outs + [(value.shape, value.dtype) for value in slot_arrays]
-    outs = outs + [(load_one, F32)] * (2 + lay_pairs)
+    outs = outs + [(load_one, F32)] * lay_pairs
     basis, matrix_source, tile_own, *rest = run(
         kernel_a,
         outs,
@@ -471,7 +461,7 @@
         ),
         in_place=range(4 + slot_kinds),
     )
-    slot_cell, rim_even, rim_odd, *loads = rest
+    slot_cell, *loads = rest
     slot_source = frac_source.reshape(small)
     lay_one = swap_pairs(loads[0], loads[-1], "lay")
 
@@ -484,25 +474,21 @@
     def blk_sides(even_ref, odd_ref, window):
         return low_high(is_even("blk"), even_ref[window], odd_ref[window])
 
-    def kernel_e(tile_ref, rim_even_ref, rim_odd_ref, *refs):
-        got, (join_ref, even_ref, odd_ref) = refs[:-3], refs[-3:]
-        low, high = lay_sides(got, (slice(layer_rows, layer_rows + TILE), slice(0, LANES)))
-        joined = join_rows(tile_ref[...], low, high)
-        join_ref[...] = joined
-        even_ref[layer_rows:, :] = joined
-        odd_ref[layer_rows:, :] = joined
-
-    outs = [((TILE, LANES), F32), (load_one, F32), (load_one, F32)]
-    joined_one, even_one, odd_one = run(
-        kernel_e, outs, (tile_own, rim_even, rim_odd, *lay_one), aliases={1: 1, 2: 2}
-    )
-    blk_one = swap_pairs(even_one, odd_one, "blk")
 
     links = frac_trans.shape[0]
 
     def kernel_p(
-        basis_ref, cell_ref, row_ref, depth_ref, node_ref, weight_ref
+        basis_ref, cell_ref, row_ref, depth_ref, node_ref, weight_ref, *rim_refs
     ):
+        blk_even = is_even("blk")
+        rim_edges = (blk_even * (cell_cols - 1), (1 - blk_even) * (cell_cols - 1))
+        for x in range(cell_rows):
+            for ref, edge in zip(rim_refs, rim_edges):
+                for k in range(4):
+                    row = basis_ref[k, x, pl.ds(edge, 1), :]
+                    for i, span in enumerate(spans):
+                        line = (k * len(spans) + i) * cell_rows + x
+                        ref[line : line + 1, :] = row[:, span]
         cell = as_line(cell_ref[...])
         at_row = lax.shift_right_logical(cell, depth_bits)
         at_depth = jnp.bitwise_and(cell, depth - 1)
@@ -529,8 +515,26 @@
         ((depth, slots), BF16),
         ((LANES, 2 * slots), BF16),
         ((TILE, 2 * slots), F32),
+        (load_one, F32),
+        (load_one, F32),
     ]
-    hot_row, hot_depth, hot_node, node_weight = run(kernel_p, outs, (basis, slot_cell))
+    hot_row, hot_depth, hot_node, node_weight, rim_even, rim_odd = run(
+        kernel_p, outs, (basis, slot_cell)
+    )
+
+    def kernel_e(tile_ref, rim_even_ref, rim_odd_ref, *refs):
+        got, (join_ref, even_ref, odd_ref) = refs[:-3], refs[-3:]
+        low, high = lay_sides(got, (slice(layer_rows, layer_rows + TILE), slice(0, LANES)))
+        joined = join_rows(tile_ref[...], low, high)
+        join_ref[...] = joined
+        even_ref[layer_rows:, :] = joined
+        odd_ref[layer_rows:, :] = joined
+
+    outs = [((TILE, LANES), F32), (load_one, F32), (load_one, F32)]
+    joined_one, even_one, odd_one = run(
+        kernel_e, outs, (tile_own, rim_even, rim_odd, *lay_one), aliases={1: 1, 2: 2}
+    )
+    blk_one = swap_pairs(even_one, odd_one, "blk")
 
     tables = 8
 

time: 24.5 us -> 24.3 us (level)
    ppermute x4, waiting for transfers between devices: 2.43 us -> 1.49 us  [swap_pairs(): got = [lax.ppermute(even_load, axis, even)]]
    ppermute x2, waiting for transfers between devices: 4.43 us -> 5.19 us  [swap_pairs(): got.append(lax.ppermute(odd_load, axis, odd))]
where the time goes in v6:
time: 24.3 us; the launch traced here: 24.1 us
  starting transfers between devices  8.89 us (37%)
  Pallas kernels  7.05 us (29%)
  waiting for transfers between devices  6.67 us (27%)
  between operations  1.47 us (6%)
    ppermute x2, starting transfers between devices, swap_pairs(): got.append(lax.ppermute(odd_load, axis, odd))  7.12 us
    pallas_call x8, Pallas kernels, run(): pl.pallas_call(kernel, out_shape=[jax.ShapeDtypeStruct(shape, dtype) for...  7.05 us
    ppermute x2, waiting for transfers between devices, swap_pairs(): got.append(lax.ppermute(odd_load, axis, odd))  5.19 us
    ppermute x4, starting transfers between devices, swap_pairs(): got = [lax.ppermute(even_load, axis, even)]  1.77 us
    ppermute x4, waiting for transfers between devices, swap_pairs(): got = [lax.ppermute(even_load, axis, even)]  1.49 us
  transfers between devices with their start and end apart: 6, of which 4 were waited for; matrix products, arithmetic and copies ran while one was open for 0% of the time, Pallas kernels for 14%

profile of v6, /device:TPU:8, one launch (start us, length us, event | category | flops | bytes accessed | tf_op | source)
XLA Modules:
  0.0 24.1 jit_solution(3662778690384704371)
XLA Ops:
  0.6 0.0 copy-start.5
  0.6 0.0 copy-start.6
  0.7 0.0 copy-start.1
  0.7 0.0 copy-start
  0.7 0.0 copy-start.2
  0.7 1.6 %shard_map.140 = (f32[4,16,16,256]{3,2,1,0:T(8,128)S(1)}, f32[16,16,256]{2,1,0:T(8,128)S(1)}, f32[8,128]{1,0:T(8,128)S(1)}, s32[4,128]{1,0:T(4,128)S(1)}, f32[136,128]{1,0:T(8,128)S(1)}) custom-call(f32[4,16,16,256]{3,2,1,0:T(8,128)} %basis_hbm.1, f32[16,16,256]{2,1,0:T(8,128)} %source_hbm.1, f32[4,4]{1,0:T(4,128)} %cdiag_hbm.1, f32[4,4,4]{2,1,0:T(4,128)} %ratio_hbm.1, ...), custom_call_target="tpu_custom_call" | custom-call | tf_op jit(solution)/shard_map/pallas_call | solution.py:38
  2.3 0.1 collective-permute-start
  2.4 0.9 %shard_map.141 = (bf16[256,512]{1,0:T(8,128)(2,1)S(1)}, bf16[256,512]{1,0:T(8,128)(2,1)S(1)}, bf16[128,1024]{1,0:T(8,128)(2,1)S(1)}, f32[8,1024]{1,0:T(8,128)S(1...) custom-call(f32[4,16,16,256]{3,2,1,0:T(8,128)S(1)} %get-tuple-element.40.basis_ref, ...), custom_call_target="tpu_custom_call" | custom-call | tf_op jit(solution)/shard_map/pallas_call | solution.py:38
  3.4 0.3 %collective-permute-done.refs_0_ = f32[136,128]{1,0:T(8,128)S(1)} collective-permute-done((f32[136,128]{1,0:T(8,128)S(1)}, f32[136,128]{1,0:T(8,128)S(1)}, u32[]{:S(2)}, u32[]{:S(2)}) %collective-permute-start) | collective-permute-done | bytes 69664 | tf_op jit(solution)/shard_map/ppermute | solution.py:24
  3.7 0.0 copy-start.3
  3.7 1.6 %collective-permute-start.1 = (f32[136,128]{1,0:T(8,128)S(1)}, f32[136,128]{1,0:T(8,128)S(1)}, u32[]{:S(2)}, u32[]{:S(2)}) collective-permute-start(f32[136,128]{1,0:T(8,128)S(1)} %get-tuple-element.61), channel_id=1, source_target_pairs={{0,2},{2,0},{4,6},{6,4},{8,10},{10,8},{12,14},{14,12},{16,18},{18,... | collective-permute-start | bytes 208904 | tf_op jit(solution)/shard_map/ppermute | solution.py:24
  5.2 3.3 %collective-permute-start.2 = (f32[136,128]{1,0:T(8,128)S(1)}, f32[136,128]{1,0:T(8,128)S(1)}, u32[]{:S(2)}, u32[]{:S(2)}) collective-permute-start(f32[136,128]{1,0:T(8,128)S(1)} %get-tuple-element.62), channel_id=1, source_target_pairs={{2,4},{4,2},{6,8},{8,6},{10,12},{12,10},{14,16},{16,14},{18,20},{2... | collective-permute-start | bytes 208904 | tf_op jit(solution)/shard_map/ppermute | solution.py:26
  9.2 0.0 copy-done.5
  9.2 0.0 copy-done.6
  9.2 0.0 copy-done.1
  9.2 0.0 copy-done
  9.2 0.0 copy-done.2
  9.2 1.6 %shard_map.142 = (f32[6,16,16,256]{3,2,1,0:T(8,128)S(1)}, f32[8,16,16,256]{3,2,1,0:T(8,128)S(1)}, f32[8,16,16,256]{3,2,1,0:T(8,128)S(1)}, f32[16,16,256]{2,1,0:T...) custom-call(f32[6,16,16,256]{3,2,1,0:T(8,128)S(1)} %copy-done, ...), custom_call_target="tpu_custom_call" | custom-call | tf_op jit(solution)/shard_map/pallas_call | solution.py:38
  10.8 0.0 collective-permute-done.1.blk_even.one_even
  10.8 2.4 %collective-permute-done.2.blk_odd.one_odd = f32[136,128]{1,0:T(8,128)S(1)} collective-permute-done((f32[136,128]{1,0:T(8,128)S(1)}, f32[136,128]{1,0:T(8,128)S(1)}, u32[]{:S(2)}, u32[]{:S(2)}) %collective-permute-start.2) | collective-permute-done | bytes 69664 | tf_op jit(solution)/shard_map/ppermute | solution.py:26
  13.2 0.0 copy-done.3
  13.2 0.0 copy-start.4
  13.2 0.9 %shard_map.144 = (f32[16,16,256]{2,1,0:T(8,128)S(1)}, f32[2,16,256]{2,1,0:T(8,128)S(1)}, f32[1,512]{1,0:T(1,128)S(1)}, f32[8,128]{1,0:T(8,128)S(1)}, f32[5,8,128]{2,1,0:T(8,128)S(1)}, /*index=5*/f32[40,128]{1,0:T(8,128)S(1)}) custom-call(f32[6,16,16,256]{3,2,1,0:T(8,128)S(1)} %get-tuple-element.46.sface_ref, ...), custom_call_target="tpu_custom_call" | custom-call | tf_op jit(solution)/shard_map/pallas_call | solution.py:38
  14.1 0.1 collective-permute-start.3
  14.2 1.2 %collective-permute-done.3.refs_0_.refs_1_ = f32[40,128]{1,0:T(8,128)S(1)} collective-permute-done((f32[40,128]{1,0:T(8,128)S(1)}, f32[40,128]{1,0:T(8,128)S(1)}, u32[]{:S(2)}, u32[]{:S(2)}) %collective-permute-start.3) | collective-permute-done | bytes 20512 | tf_op jit(solution)/shard_map/ppermute | solution.py:24
  15.4 0.1 collective-permute-start.4
  15.5 3.9 %collective-permute-start.5 = (f32[40,128]{1,0:T(8,128)S(1)}, f32[40,128]{1,0:T(8,128)S(1)}, u32[]{:S(2)}, u32[]{:S(2)}) collective-permute-start(f32[40,128]{1,0:T(8,128)S(1)} %get-tuple-element.75), channel_id=1, source_target_pairs={{2,4},{4,2},{6,8},{8,6},{10,12},{12,10},{14,16},{16,14},{18,20},{2... | collective-permute-start | bytes 61448 | tf_op jit(solution)/shard_map/ppermute | solution.py:26
  19.3 0.0 copy-done.4
  19.3 0.8 %shard_map.145 = (f32[16,16,256]{2,1,0:T(8,128)S(1)}, f32[1,512]{1,0:T(1,128)S(1)}, s32[1,1024]{1,0:T(1,128)S(1)}, bf16[128,1024]{1,0:T(8,128)(2,1)S(1)}) custom-call(f32[6,16,16,256]{3,2,1,0:T(8,128)S(1)} %get-tuple-element.46.sface_ref, f32[16,16,256]{2,1,0:T(8,128)S(1)} %get-tuple-element.48.ssource_ref, f32[16,16,256]{2,1,0:T(8,128)S(1)} %get-tuple-element.49.scale_ref, ...), custom_call_target="tpu_custom_call" | custom-call | tf_op jit(solution)/shard_map/pallas_call | solution.py:38
  20.1 0.0 collective-permute-done.4.two_even
  20.1 2.8 %collective-permute-done.5.two_odd = f32[40,128]{1,0:T(8,128)S(1)} collective-permute-done((f32[40,128]{1,0:T(8,128)S(1)}, f32[40,128]{1,0:T(8,128)S(1)}, u32[]{:S(2)}, u32[]{:S(2)}) %collective-permute-start.5) | collective-permute-done | bytes 20512 | tf_op jit(solution)/shard_map/ppermute | solution.py:26
  22.9 1.2 %shard_map.147 = (f32[16,16,256]{2,1,0:T(8,128)}, f32[4,128]{1,0:T(4,128)}) custom-call(f32[6,16,16,256]{3,2,1,0:T(8,128)S(1)} %get-tuple-element.46.sface_ref, f32[8,16,16,256]{3,2,1,0:T(8,128)S(1)} %get-tuple-element.47.forward_ref, f32[16,16,256]{2,1,0:T(8,128)S(1)} %get-tuple-element.65.base_ref, f32[2,16,256]{2,1,0:T(8,128)S(1)} %get-tuple-element.52.sedge_ref, ...), custom_call_target="tpu_custom_call" | custom-call | tf_op jit(solution)/shard_map/pallas_call | solution.py:38
  (2 shorter events, 0.0 us)
Async XLA Ops:
  0.6 8.5 %copy-start.5 = (f32[512]{0:T(512)S(1)}, f32[512]{0:T(512)}, u32[]{:S(2)}) copy-start(f32[512]{0:T(512)} %param.21) | copy-start | bytes 6148
  0.6 8.5 %copy-start.6 = (f32[512]{0:T(512)S(1)}, f32[512]{0:T(512)}, u32[]{:S(2)}) copy-start(f32[512]{0:T(512)} %param.20) | copy-start | bytes 6148
  0.7 8.5 %copy-start.1 = (f32[16,16,256]{2,1,0:T(8,128)S(1)}, f32[16,16,256]{2,1,0:T(8,128)}, u32[]{:S(2)}) copy-start(f32[16,16,256]{2,1,0:T(8,128)} %accum_ref.1) | copy-start | bytes 786436
  0.7 8.5 %copy-start = (f32[6,16,16,256]{3,2,1,0:T(8,128)S(1)}, f32[6,16,16,256]{3,2,1,0:T(8,128)}, u32[]{:S(2)}) copy-start(f32[6,16,16,256]{3,2,1,0:T(8,128)} %faces_ref.1) | copy-start | bytes 4718596
  0.7 8.5 %copy-start.2 = (f32[2,512]{1,0:T(2,128)S(1)}, f32[2,512]{1,0:T(2,128)}, u32[]{:S(2)}) copy-start(f32[2,512]{1,0:T(2,128)} %trans_ref.3) | copy-start | bytes 12292
  2.3 1.3 %collective-permute-start = (f32[136,128]{1,0:T(8,128)S(1)}, f32[136,128]{1,0:T(8,128)S(1)}, u32[]{:S(2)}, u32[]{:S(2)}) collective-permute-start(f32[136,128]{1,0:T(8,128)S(1)} %get-tuple-element.59), channel_id=1, source_target_pairs={{0,1},{1,0},{2,3},{3,2},{4,5},{5,4},{6,7},{7,6},{8,9},{9,8},{10,11... | collective-permute-start | bytes 208904 | tf_op jit(solution)/shard_map/ppermute | solution.py:24
  3.7 9.6 %copy-start.3 = (f32[512]{0:T(512)S(1)}, f32[512]{0:T(512)}, u32[]{:S(2)}) copy-start(f32[512]{0:T(512)} %param.19) | copy-start | bytes 6148
  3.7 7.2 %collective-permute-start.1 = (f32[136,128]{1,0:T(8,128)S(1)}, f32[136,128]{1,0:T(8,128)S(1)}, u32[]{:S(2)}, u32[]{:S(2)}) collective-permute-start(f32[136,128]{1,0:T(8,128)S(1)} %get-tuple-element.61), channel_id=1, source_target_pairs={{0,2},{2,0},{4,6},{6,4},{8,10},{10,8},{12,14},{14,12},{16,18},{18,... | collective-permute-start | bytes 208904 | tf_op jit(solution)/shard_map/ppermute | solution.py:24
  5.2 8.0 %collective-permute-start.2 = (f32[136,128]{1,0:T(8,128)S(1)}, f32[136,128]{1,0:T(8,128)S(1)}, u32[]{:S(2)}, u32[]{:S(2)}) collective-permute-start(f32[136,128]{1,0:T(8,128)S(1)} %get-tuple-element.62), channel_id=1, source_target_pairs={{2,4},{4,2},{6,8},{8,6},{10,12},{12,10},{14,16},{16,14},{18,20},{2... | collective-permute-start | bytes 208904 | tf_op jit(solution)/shard_map/ppermute | solution.py:26
  13.2 6.1 %copy-start.4 = (s32[2,512]{1,0:T(2,128)S(1)}, s32[2,512]{1,0:T(2,128)}, u32[]{:S(2)}) copy-start(s32[2,512]{1,0:T(2,128)} %peer_ref.1) | copy-start | bytes 12292
  14.1 1.3 %collective-permute-start.3 = (f32[40,128]{1,0:T(8,128)S(1)}, f32[40,128]{1,0:T(8,128)S(1)}, u32[]{:S(2)}, u32[]{:S(2)}) collective-permute-start(f32[40,128]{1,0:T(8,128)S(1)} %get-tuple-element.71), channel_id=1, source_target_pairs={{0,1},{1,0},{2,3},{3,2},{4,5},{5,4},{6,7},{7,6},{8,9},{9,8},{10,11... | collective-permute-start | bytes 61448 | tf_op jit(solution)/shard_map/ppermute | solution.py:24
  15.4 4.7 %collective-permute-start.4 = (f32[40,128]{1,0:T(8,128)S(1)}, f32[40,128]{1,0:T(8,128)S(1)}, u32[]{:S(2)}, u32[]{:S(2)}) collective-permute-start(f32[40,128]{1,0:T(8,128)S(1)} %get-tuple-element.74), channel_id=1, source_target_pairs={{0,2},{2,0},{4,6},{6,4},{8,10},{10,8},{12,14},{14,12},{16,18},{18,... | collective-permute-start | bytes 61448 | tf_op jit(solution)/shard_map/ppermute | solution.py:24
  15.5 7.5 %collective-permute-start.5 = (f32[40,128]{1,0:T(8,128)S(1)}, f32[40,128]{1,0:T(8,128)S(1)}, u32[]{:S(2)}, u32[]{:S(2)}) collective-permute-start(f32[40,128]{1,0:T(8,128)S(1)} %get-tuple-element.75), channel_id=1, source_target_pairs={{2,4},{4,2},{6,8},{8,6},{10,12},{12,10},{14,16},{16,14},{18,20},{2... | collective-permute-start | bytes 61448 | tf_op jit(solution)/shard_map/ppermute | solution.py:26
